TPU v7x, 32 devices: a whole 2x2x4 slice. The times are simulated.
32 devices in a mesh: dp: 8 (over z, y), seq: 4 (over x, core).
Axes of the slice: x: 2, y: 2, z: 4, core: 2. Of those that a mesh axis runs over, the one named last changes fastest.
Arguments:
- tokens: bfloat16 [8, 4096, 768], P('dp', 'seq'), may hold values from -6 to 6
- time_steps: int32 [8, 2], P('dp'), may hold values from 0 to 999
- data_group: int32 [8], P('dp'), may hold values from 0 to 1, as said below
- cotangent: bfloat16 [8, 4096, 768], P('dp', 'seq'), may hold values from -6 to 6
- attn_norm_gain: bfloat16 [768], replicated, may hold values from 0.25 to 1.75
- attn_norm_bias: bfloat16 [768], replicated, may hold values from -1.75 to 1.75
- qkv_weight: bfloat16 [768, 2304], replicated, may hold values from -0.21875 to 0.21875
- query_bias: bfloat16 [768], replicated, may hold values from -3 to 3
- value_bias: bfloat16 [768], replicated, may hold values from -3 to 3
- out_weight: bfloat16 [768, 768], replicated, may hold values from -0.625 to 0.625
- out_bias: bfloat16 [768], replicated, may hold values from -1.75 to 1.75
- mlp_norm_gain: bfloat16 [768], replicated, may hold values from 0.25 to 1.75
- mlp_norm_bias: bfloat16 [768], replicated, may hold values from -1.75 to 1.75
- up_weight: bfloat16 [768, 3072], replicated, may hold values from -0.21875 to 0.21875
- up_bias: bfloat16 [3072], replicated, may hold values from -3 to 3
- down_weight: bfloat16 [3072, 768], replicated, may hold values from -0.15625 to 0.15625
- down_bias: bfloat16 [768], replicated, may hold values from -1.75 to 1.75
- time_table: bfloat16 [1000, 768], replicated, may hold values from -3 to 3
Outputs:
- output: bfloat16 [8, 4096, 768], P('dp', 'seq')
- grad_tokens: bfloat16 [8, 4096, 768], P('dp', 'seq')
- grad_attn_norm_gain: float32 [768], replicated
- grad_attn_norm_bias: float32 [768], replicated
- grad_qkv_weight: float32 [768, 2304], P(None, 'dp')
- grad_query_bias: float32 [768], replicated
- grad_value_bias: float32 [768], replicated
- grad_out_weight: float32 [768, 768], P(None, 'dp')
- grad_out_bias: float32 [768], replicated
- grad_mlp_norm_gain: float32 [768], replicated
- grad_mlp_norm_bias: float32 [768], replicated
- grad_up_weight: float32 [768, 3072], P(None, 'dp')
- grad_up_bias: float32 [3072], replicated
- grad_down_weight: float32 [3072, 768], P(None, 'dp')
- grad_down_bias: float32 [768], replicated
- grad_time_table: float32 [1000, 768], P(None, 'dp')
Inputs may be any that keep to these rules, and one draw needn't show every extreme that they name: `data_group`: exactly half of the 8 blocks have the value 1.
All inputs are finite; a program needn't handle non-finite values.
Results may differ from a plain program's by a relative error of at most 0.012.
Values may be sent and summed in bfloat16 or wider, within the bound.
No kernel may reach another device: no remote copies, remote signals or barrier semaphores. Data moves between devices by JAX's collectives and lax.ppermute only.
A program may use at most 256 MiB of HBM per device.

v0:
```python
from functools import partial

import jax
import jax.numpy as jnp
from jax import lax
from jax.sharding import PartitionSpec as P

HEADS = 12
HEAD_DIM = 64


EPSILON = 1e-05
HIGHEST = lax.Precision.HIGHEST


def layer_norm(hidden, gain, shift):
    center = hidden - jnp.mean(hidden, -1, keepdims=True)
    spread = jnp.mean(center * center, -1, keepdims=True)
    return center * lax.rsqrt(spread + EPSILON) * gain + shift


def to_rows(values, part_count, segment):
    per_part = values.shape[0] // part_count
    row_count = per_part // segment
    shaped = values.reshape((part_count, row_count, segment) + values.shape[1:])
    return jnp.swapaxes(shaped, 0, 1).reshape((row_count, part_count * segment) + values.shape[1:])


def from_rows(values, part_count):
    row_count = values.shape[0]
    segment = values.shape[1] // part_count
    shaped = values.reshape((row_count, part_count, segment) + values.shape[2:])
    return jnp.swapaxes(shaped, 0, 1).reshape(
        (part_count * row_count * segment,) + values.shape[2:]
    )


def to_blocks(values, block):
    row_count, length = (values.shape[0], values.shape[1])
    shaped = values.reshape((row_count, length // block, block) + values.shape[2:])
    return jnp.swapaxes(shaped, 0, 1)


def from_blocks(values):
    merged = jnp.swapaxes(values, 0, 1)
    return merged.reshape((merged.shape[0], merged.shape[1] * merged.shape[2]) + merged.shape[3:])


def attend(heads_all, part_count, segment):
    row_data = to_rows(heads_all, part_count, segment)
    queries = row_data[:, :, 0]
    keys_all = row_data[:, :, 1]
    values = row_data[:, :, 2]
    scale = queries.shape[-1] ** (-0.5)
    block = min(512, queries.shape[1])

    def one_block(query_block):
        scores = (
            jnp.einsum("rqhe,rkhe->rhqk", query_block, keys_all, preferred_element_type=jnp.float32)
            * scale
        )
        peak = jnp.max(scores, -1, keepdims=True)
        log_total = peak + jnp.log(jnp.sum(jnp.exp(scores - peak), -1, keepdims=True))
        weights = jnp.exp(scores - log_total).astype(jnp.bfloat16)
        mixed_block = jnp.einsum(
            "rhqk,rkhe->rqhe", weights, values, preferred_element_type=jnp.float32
        )
        return (mixed_block.astype(jnp.bfloat16), jnp.swapaxes(log_total[..., 0], 1, 2))

    mixed_parts, log_parts = lax.map(one_block, to_blocks(queries, block))
    mixed_rows = from_blocks(mixed_parts)
    row_count, length = (mixed_rows.shape[0], mixed_rows.shape[1])
    mixed_rows = mixed_rows.reshape(row_count, length, -1)
    log_rows = from_blocks(log_parts)
    return (from_rows(mixed_rows, part_count), from_rows(log_rows, part_count))


def attend_back(heads_all, grad_heads, log_sums, part_count, segment):
    row_data = to_rows(heads_all, part_count, segment)
    queries = row_data[:, :, 0]
    keys_all = row_data[:, :, 1]
    values = row_data[:, :, 2]
    grad_rows = to_rows(grad_heads, part_count, segment)
    log_rows = to_rows(log_sums, part_count, segment)
    scale = queries.shape[-1] ** (-0.5)
    block = min(512, queries.shape[1])

    def one_block(carry, inputs):
        key_total, value_total = carry
        query_block, grad_block, log_block = inputs
        log_here = jnp.swapaxes(log_block, 1, 2)[..., None]
        scores = (
            jnp.einsum("rqhe,rkhe->rhqk", query_block, keys_all, preferred_element_type=jnp.float32)
            * scale
        )
        weights_full = jnp.exp(scores - log_here)
        weights_low = weights_full.astype(jnp.bfloat16)
        value_total = value_total + jnp.einsum(
            "rhqk,rqhe->rkhe", weights_low, grad_block, preferred_element_type=jnp.float32
        )
        grad_weights = jnp.einsum(
            "rqhe,rkhe->rhqk", grad_block, values, preferred_element_type=jnp.float32
        )
        inner = jnp.sum(weights_full * grad_weights, -1, keepdims=True)
        grad_scores = (weights_full * (grad_weights - inner)).astype(jnp.bfloat16)
        grad_query = (
            jnp.einsum("rhqk,rkhe->rqhe", grad_scores, keys_all, preferred_element_type=jnp.float32)
            * scale
        )
        key_total = (
            key_total
            + jnp.einsum(
                "rhqk,rqhe->rkhe", grad_scores, query_block, preferred_element_type=jnp.float32
            )
            * scale
        )
        return ((key_total, value_total), grad_query)

    empty = jnp.zeros(queries.shape, jnp.float32)
    (grad_key, grad_values), query_parts = lax.scan(
        one_block,
        (empty, empty),
        (to_blocks(queries, block), to_blocks(grad_rows, block), to_blocks(log_rows, block)),
    )
    grad_query = from_blocks(query_parts)
    stacked = jnp.stack([grad_query, grad_key, grad_values], axis=2).astype(jnp.bfloat16)
    row_count, length = (stacked.shape[0], stacked.shape[1])
    stacked = stacked.reshape(row_count, length, 3, -1)
    return from_rows(stacked, part_count)


def on_device(
    tokens,
    time_steps,
    data_group,
    cotangent,
    attn_norm_gain,
    attn_norm_bias,
    qkv_weight,
    query_bias,
    value_bias,
    out_weight,
    out_bias,
    mlp_norm_gain,
    mlp_norm_bias,
    up_weight,
    up_bias,
    down_weight,
    down_bias,
    time_table,
):
    part_count = lax.axis_size("seq")
    inputs = tokens[0].astype(jnp.float32)
    tok_here = inputs.shape[0]
    width = inputs.shape[1]
    heads_dev = HEADS // part_count
    head_cols = heads_dev * HEAD_DIM
    short_seg = tok_here // 2
    is_short = data_group[0] == 0
    segment = jnp.where(is_short, short_seg, tok_here).astype(jnp.int32)
    row_index = jnp.arange(tok_here, dtype=jnp.int32) // segment
    row_limit = time_steps.shape[1]
    row_onehot = (row_index[:, None] == jnp.arange(row_limit, dtype=jnp.int32)[None, :]).astype(
        jnp.float32
    )
    step_onehot = (
        time_steps[0][:, None] == jnp.arange(time_table.shape[0], dtype=jnp.int32)[None, :]
    )
    row_table = jnp.dot(
        step_onehot.astype(jnp.bfloat16), time_table, preferred_element_type=jnp.float32
    )
    hidden = inputs + jnp.dot(row_onehot, row_table, precision=HIGHEST)
    gain_one = attn_norm_gain.astype(jnp.float32)
    shift_one = attn_norm_bias.astype(jnp.float32)
    normed, norm_one_back = jax.vjp(layer_norm, hidden, gain_one, shift_one)
    normed_low = normed.astype(jnp.bfloat16)
    bias_all = jnp.concatenate([query_bias, jnp.zeros_like(query_bias), value_bias]).astype(
        jnp.float32
    )
    projected = (
        jnp.dot(normed_low, qkv_weight, preferred_element_type=jnp.float32) + bias_all
    ).astype(jnp.bfloat16)
    sending = jnp.moveaxis(projected.reshape(tok_here, 3, part_count, head_cols), 2, 0)
    heads_all = lax.all_to_all(sending, "seq", split_axis=0, concat_axis=0, tiled=True)
    heads_all = heads_all.reshape(-1, 3, heads_dev, HEAD_DIM)
    mixed, log_sums = lax.cond(
        is_short,
        lambda: attend(heads_all, part_count, short_seg),
        lambda: attend(heads_all, part_count, tok_here),
    )
    mixed_send = mixed.reshape(part_count, -1, head_cols)
    returned = lax.all_to_all(mixed_send, "seq", split_axis=0, concat_axis=0, tiled=True)
    attended = jnp.moveaxis(returned, 0, 1).reshape(tok_here, width)
    branch = jnp.dot(attended, out_weight, preferred_element_type=jnp.float32) + out_bias.astype(
        jnp.float32
    )
    resid = hidden + branch
    gain_two = mlp_norm_gain.astype(jnp.float32)
    shift_two = mlp_norm_bias.astype(jnp.float32)
    normed_two, norm_two_back = jax.vjp(layer_norm, resid, gain_two, shift_two)
    normed_two_low = normed_two.astype(jnp.bfloat16)
    up_act = jnp.dot(
        normed_two_low, up_weight, preferred_element_type=jnp.float32
    ) + up_bias.astype(jnp.float32)
    gelu_act, gelu_back = jax.vjp(partial(jax.nn.gelu, approximate=False), up_act)
    gelu_low = gelu_act.astype(jnp.bfloat16)
    down_out = jnp.dot(
        gelu_low, down_weight, preferred_element_type=jnp.float32
    ) + down_bias.astype(jnp.float32)
    result = (resid + down_out).astype(jnp.bfloat16)
    grad_out = cotangent[0].astype(jnp.float32)
    grad_down_low = cotangent[0]
    grad_down_w = jnp.dot(gelu_low.T, grad_down_low, preferred_element_type=jnp.float32)
    grad_down_b = jnp.sum(grad_down_low, 0, dtype=jnp.float32)
    grad_gelu = jnp.dot(grad_down_low, down_weight.T, preferred_element_type=jnp.float32)
    (grad_up_act,) = gelu_back(grad_gelu)
    grad_up_low = grad_up_act.astype(jnp.bfloat16)
    grad_up_w = jnp.dot(normed_two_low.T, grad_up_low, preferred_element_type=jnp.float32)
    grad_up_b = jnp.sum(grad_up_low, 0, dtype=jnp.float32)
    grad_normed_two = jnp.dot(grad_up_low, up_weight.T, preferred_element_type=jnp.float32)
    grad_resid_norm, grad_gain_two, grad_shift_two = norm_two_back(grad_normed_two)
    grad_resid = grad_out + grad_resid_norm
    grad_branch = grad_resid.astype(jnp.bfloat16)
    grad_out_w = jnp.dot(attended.T, grad_branch, preferred_element_type=jnp.float32)
    grad_out_b = jnp.sum(grad_branch, 0, dtype=jnp.float32)
    grad_attended = jnp.dot(grad_branch, out_weight.T, preferred_element_type=jnp.float32).astype(
        jnp.bfloat16
    )
    grad_sending = jnp.moveaxis(grad_attended.reshape(tok_here, part_count, head_cols), 1, 0)
    grad_heads = lax.all_to_all(grad_sending, "seq", split_axis=0, concat_axis=0, tiled=True)
    grad_heads = grad_heads.reshape(-1, heads_dev, HEAD_DIM)
    grad_qkv_heads = lax.cond(
        is_short,
        lambda: attend_back(heads_all, grad_heads, log_sums, part_count, short_seg),
        lambda: attend_back(heads_all, grad_heads, log_sums, part_count, tok_here),
    )
    grad_qkv_heads = grad_qkv_heads.reshape(part_count, -1, 3, head_cols)
    grad_back = lax.all_to_all(grad_qkv_heads, "seq", split_axis=0, concat_axis=0, tiled=True)
    grad_qkv = jnp.moveaxis(grad_back, 0, 2).reshape(tok_here, 3 * width)
    grad_qkv_w = jnp.dot(normed_low.T, grad_qkv, preferred_element_type=jnp.float32)
    grad_qkv_b = jnp.sum(grad_qkv, 0, dtype=jnp.float32)
    grad_query_b = grad_qkv_b[:width]
    grad_value_b = grad_qkv_b[2 * width :]
    grad_normed = jnp.dot(grad_qkv, qkv_weight.T, preferred_element_type=jnp.float32)
    grad_hidden_norm, grad_gain_one, grad_shift_one = norm_one_back(grad_normed)
    grad_hidden = grad_resid + grad_hidden_norm
    grad_input = grad_hidden.astype(jnp.bfloat16)
    row_sums = jnp.dot(row_onehot.T, grad_hidden, precision=HIGHEST)
    grad_table = jnp.dot(step_onehot.astype(jnp.float32).T, row_sums, precision=HIGHEST)
    summed = lax.psum(
        (
            grad_gain_one,
            grad_shift_one,
            grad_query_b,
            grad_value_b,
            grad_out_b,
            grad_gain_two,
            grad_shift_two,
            grad_up_b,
            grad_down_b,
        ),
        ("dp", "seq"),
    )
    (
        sum_gain_one,
        sum_shift_one,
        sum_query,
        sum_value,
        sum_out_b,
        sum_gain_two,
        sum_shift_two,
        sum_up_b,
        sum_down_b,
    ) = summed
    matrices = (grad_qkv_w, grad_out_w, grad_up_w, grad_down_w, grad_table)
    shares = (
        lax.psum_scatter(matrices[0], "dp", scatter_dimension=1, tiled=True),
        lax.psum_scatter(matrices[1], "dp", scatter_dimension=1, tiled=True),
        lax.psum_scatter(matrices[2], "dp", scatter_dimension=1, tiled=True),
        lax.psum_scatter(matrices[3], "dp", scatter_dimension=1, tiled=True),
        lax.psum_scatter(matrices[4], "dp", scatter_dimension=1, tiled=True),
    )
    final = (
        lax.psum(shares[0].astype(jnp.bfloat16), "seq").astype(jnp.float32),
        lax.psum(shares[1].astype(jnp.bfloat16), "seq").astype(jnp.float32),
        lax.psum(shares[2].astype(jnp.bfloat16), "seq").astype(jnp.float32),
        lax.psum(shares[3].astype(jnp.bfloat16), "seq").astype(jnp.float32),
        lax.psum(shares[4].astype(jnp.bfloat16), "seq").astype(jnp.float32),
    )
    sum_qkv_w, sum_out_w, sum_up_w, sum_down_w, sum_table = final
    return (
        result[None],
        grad_input[None],
        sum_gain_one,
        sum_shift_one,
        sum_qkv_w,
        sum_query,
        sum_value,
        sum_out_w,
        sum_out_b,
        sum_gain_two,
        sum_shift_two,
        sum_up_w,
        sum_up_b,
        sum_down_w,
        sum_down_b,
        sum_table,
    )


def solution(mesh):
    placed = (
        P("dp", "seq", None),
        P("dp", None),
        P("dp"),
        P("dp", "seq", None),
        P(),
        P(),
        P(),
        P(),
        P(),
        P(),
        P(),
        P(),
        P(),
        P(),
        P(),
        P(),
        P(),
        P(),
    )
    return jax.shard_map(
        on_device,
        mesh=mesh,
        in_specs=placed,
        out_specs=(
            P("dp", "seq", None),
            P("dp", "seq", None),
            P(),
            P(),
            P(None, "dp"),
            P(),
            P(),
            P(None, "dp"),
            P(),
            P(),
            P(),
            P(None, "dp"),
            P(),
            P(None, "dp"),
            P(),
            P(None, "dp"),
        ),
        check_vma=False,
    )
```

profile of v0, /device:TPU:0, one launch (start us, length us, event | category | flops | bytes accessed | tf_op | source)
XLA Modules:
  0.0 2046.5 jit_solution(15102713713867713025)
XLA Ops:
  41.7 54.5 %all-to-all-done = bf16[4,1024,3,192]{1,3,2,0:T(8,128)(2,1)} async-done(((bf16[4,1024,3,192]{1,3,2,0:T(8,128)(2,1)}), bf16[4,1024,3,192]{1,3,2,0:T(8,128)(2,1)}, u32[]{:S(2)}, u32[]{:S(2)}) %all-to-all-start) | async-done | bytes 4718624 | tf_op jit(solution)/shard_map/all_to_all | solution.py:184
  96.2 193.6 %conditional.2 = (bf16[4096,192]{1,0:T(8,128)(2,1)}, f32[4096,3]{1,0:T(8,128)}) conditional(s32[]{:T(128)} %bitcast.44, (bf16[4,1024,3,192]{1,3,2,0:T(8,128)(2,1)}) %tuple.79, bf16[4,1024,3,192]{1,3,2,0:T(8,128)(2,1)} %all-to-all-done), branch_computations={%region_2.7_spmd, %region_7.12_spmd} | conditional | flops 1661137920 | bytes 133107920 | solution.py:186
  138.3 144.3 %while.51 = (s32[]{:T(128)}, bf16[4,2,512,3,64]{2,4,3,1,0:T(8,128)(2,1)}, f32[4,2,512,3]{2,3,1,0:T(4,128)}, bf16[4,2,512,3,64]{2,4,3,1,0:T(8,128)(2,1)}, bf16[2,...) while((s32[]{:T(128)}, bf16[4,2,512,3,64]{2,4,3,1,0:T(8,128)(2,1)}, ...), condition=%wide.region_11.11_spmd, body=%wide.region_8.10_spmd.sunk | while | flops 1661137920 | bytes 85823616 | solution.py:70
  323.4 35.9 %multiply_convert_fusion.2 = (bf16[1024,3072]{1,0:T(8,128)(2,1)}, f32[1024,3072]{1,0:T(8,128)}, f32[1024,3072]{1,0:T(8,128)}) fusion(f32[3072]{0:T(1024)S(1)} %copy-done.41, bf16[768,3072]{1,0:T(8,128)(2,1)S(1)} %bitcast.404, f32[1024,768]{0,1:T(8,128)S(1)} %get-tuple-element.599, f32[768]{0:T(1024)S(1)} %copy-done.44, f32[768]{0:T(1024)S(1)} %convert_element_type.170, ...), kind=kOutput, calls=%fused_computation.105 | convolution fusion | flops 5043388416 | bytes 39348224 | tf_op jit(solution)/shard_map/dot_general | solution.py:202
  359.3 17.9 convert_reduce_fusion
  400.3 23.3 %all_to_all.26 = bf16[4,1024,192]{1,2,0:T(8,128)(2,1)} all-to-all(bf16[4,1024,192]{1,2,0:T(8,128)(2,1)S(1)} %bitcast.397), channel_id=1, replica_groups=mesh['dp'=8,'seq'=4] {'seq'}, dimensions={0} | all-to-all | bytes 3145728 | tf_op jit(solution)/shard_map/all_to_all | solution.py:230
  423.6 460.4 %conditional.3 = (bf16[4096,3,192]{2,1,0:T(4,128)(2,1)}) conditional(s32[]{:T(128)} %bitcast.44, (bf16[4,1024,3,192]{1,3,2,0:T(8,128)(2,1)}, bf16[4,1024,192]{1,2,0:T(8,128)(2,1)}, f32[4096,3]{1,0:T(8,128)}) %tuple.38, (bf16[4,1024,3,192]{1,3,2,0:T(8,128)(2,1)}, bf16[4,1024,192]{1,2,0:T(8,128)(2,1)}, f32[4096,3]{1,0:T(8,128)}) %tuple.38), branch_computations={%region_16.20_spmd, %region_20.24_spmd} | conditional | flops 4121883648 | bytes 292737280 | solution.py:232
  472.8 344.5 %while.53 = (s32[]{:T(128)}, f32[2,2048,3,64]{1,3,2,0:T(8,128)}, f32[2,2048,3,64]{1,3,2,0:T(8,128)}, bf16[4,2,512,3,64]{2,4,3,1,0:T(8,128)(2,1)}, bf16[4,2,512,3...) while((s32[]{:T(128)}, f32[2,2048,3,64]{1,3,2,0:T(8,128)}, ...), condition=%wide.region_23.23_spmd.clone, body=%wide.region_21.22_spmd.clone.sunk | while | flops 4106155008 | bytes 210849968 | solution.py:120
  500.9 17.3 multiply_reduce_fusion.14
  518.1 21.1 %multiply_convert_fusion.5 = bf16[2,3,512,2048]{3,2,1,0:T(8,128)(2,1)} fusion(f32[2,3,512,2048]{3,2,1,0:T(8,128)} %get-tuple-element.782, f32[2,3,512,2048]{3,2,1,0:T(8,128)} %fusion.186, f32[2,3,512]{2,1,0:T(4,128)} %get-tuple-element.783, f32[2,3,512]{2,1,0:T(4,128)S(1)} %dynamic-slice_bitcast_fusion.4), kind=kLoop, calls=%fused_computation.73.clone.1 | loop fusion | flops 31457280 | bytes 62939136 | tf_op jit(solution)/shard_map/cond/branch_1_fun/while/body/eval_jaxpr/convert_element_type | solution.py:105
  586.4 17.3 multiply_reduce_fusion.14
  603.7 21.1 %multiply_convert_fusion.5 = bf16[2,3,512,2048]{3,2,1,0:T(8,128)(2,1)} fusion(f32[2,3,512,2048]{3,2,1,0:T(8,128)} %get-tuple-element.782, f32[2,3,512,2048]{3,2,1,0:T(8,128)} %fusion.186, f32[2,3,512]{2,1,0:T(4,128)} %get-tuple-element.783, f32[2,3,512]{2,1,0:T(4,128)S(1)} %dynamic-slice_bitcast_fusion.4), kind=kLoop, calls=%fused_computation.73.clone.1 | loop fusion | flops 31457280 | bytes 62939136 | tf_op jit(solution)/shard_map/cond/branch_1_fun/while/body/eval_jaxpr/convert_element_type | solution.py:105
  672.9 17.3 multiply_reduce_fusion.14
  690.2 21.1 %multiply_convert_fusion.5 = bf16[2,3,512,2048]{3,2,1,0:T(8,128)(2,1)} fusion(f32[2,3,512,2048]{3,2,1,0:T(8,128)} %get-tuple-element.782, f32[2,3,512,2048]{3,2,1,0:T(8,128)} %fusion.186, f32[2,3,512]{2,1,0:T(4,128)} %get-tuple-element.783, f32[2,3,512]{2,1,0:T(4,128)S(1)} %dynamic-slice_bitcast_fusion.4), kind=kLoop, calls=%fused_computation.73.clone.1 | loop fusion | flops 31457280 | bytes 62939136 | tf_op jit(solution)/shard_map/cond/branch_1_fun/while/body/eval_jaxpr/convert_element_type | solution.py:105
  759.4 17.3 multiply_reduce_fusion.14
  776.7 21.1 %multiply_convert_fusion.5 = bf16[2,3,512,2048]{3,2,1,0:T(8,128)(2,1)} fusion(f32[2,3,512,2048]{3,2,1,0:T(8,128)} %get-tuple-element.782, f32[2,3,512,2048]{3,2,1,0:T(8,128)} %fusion.186, f32[2,3,512]{2,1,0:T(4,128)} %get-tuple-element.783, f32[2,3,512]{2,1,0:T(4,128)S(1)} %dynamic-slice_bitcast_fusion.4), kind=kLoop, calls=%fused_computation.73.clone.1 | loop fusion | flops 31457280 | bytes 62939136 | tf_op jit(solution)/shard_map/cond/branch_1_fun/while/body/eval_jaxpr/convert_element_type | solution.py:105
  865.1 18.5 pad_maximum_fusion.1
  906.5 49.0 %all-to-all-done.3 = bf16[4,1024,3,192]{1,3,2,0:T(8,128)(2,1)} async-done(((bf16[4,1024,3,192]{1,3,2,0:T(8,128)(2,1)}), bf16[4,1024,3,192]{1,3,2,0:T(8,128)(2,1)}, u32[]{:S(2)}, u32[]{:S(2)}) %all-to-all-start.3) | async-done | bytes 4718624 | tf_op jit(solution)/shard_map/all_to_all | solution.py:238
  1027.8 404.0 %reduce-scatter.8.cloned.1.call-done = f32[768,96]{0,1:T(8,128)} async-done(((f32[768,768]{0,1:T(8,128)}), f32[768,96]{0,1:T(8,128)}) %reduce-scatter.8.cloned.1.call-update) | async-done | bytes 294928 | tf_op jit(solution)/shard_map/reduce_scatter | solution.py:278
  1433.5 78.1 %reduce-scatter.14.cloned.1.call-done = f32[1000,96]{0,1:T(8,128)} async-done(((f32[1000,768]{0,1:T(8,128)}), f32[1000,96]{0,1:T(8,128)}) %reduce-scatter.14.cloned.1.call-update) | async-done | bytes 384016 | tf_op jit(solution)/shard_map/reduce_scatter | solution.py:281
  1513.2 164.4 %reduce-scatter.12.cloned.1.call-done = f32[3072,96]{0,1:T(8,128)} async-done(((f32[3072,768]{0,1:T(8,128)}), f32[3072,96]{0,1:T(8,128)}) %reduce-scatter.12.cloned.1.call-update) | async-done | bytes 1179664 | tf_op jit(solution)/shard_map/reduce_scatter | solution.py:280
  1679.7 163.9 %reduce-scatter.10.cloned.1.call-done = f32[768,384]{1,0:T(8,128)} async-done(((f32[768,3072]{1,0:T(8,128)}), f32[768,384]{1,0:T(8,128)}) %reduce-scatter.10.cloned.1.call-update) | async-done | bytes 1179664 | tf_op jit(solution)/shard_map/reduce_scatter | solution.py:279
  1845.8 129.6 %reduce-scatter.6.cloned.1.call-done = f32[768,288]{0,1:T(8,128)} async-done(((f32[768,2304]{0,1:T(8,128)}), f32[768,288]{0,1:T(8,128)}) %reduce-scatter.6.cloned.1.call-update) | async-done | bytes 884752 | tf_op jit(solution)/shard_map/reduce_scatter | solution.py:277
  1989.9 40.9 %all-reduce = (f32[768]{0:T(1024)}, f32[768]{0:T(1024)}, f32[768]{0:T(1024)}, f32[768]{0:T(1024)}, f32[768]{0:T(1024)}, /*index=5*/f32[768]{0:T(1024)}, f32[768]{0:T(1024)}, f32[3072]{0:T(1024)}, f32[768]{0:T(1024)}) all-reduce(f32[768]{0:T(1024)} %get-tuple-element.484, ...), channel_id=1, replica_groups=mesh['dp'=8,'seq'=4] {'dp','seq'}, use_global_device_ids=true, to_apply=%region_27.28 | all-reduce | flops 9216 | bytes 73728 | tf_op jit(solution)/shard_map/psum | solution.py:250
  (267 shorter events, 686.1 us)
Async XLA Ops:
  7.2 11.9 copy-start
  36.7 59.5 %all-to-all-start = ((bf16[4,1024,3,192]{1,3,2,0:T(8,128)(2,1)}), bf16[4,1024,3,192]{1,3,2,0:T(8,128)(2,1)}, u32[]{:S(2)}, u32[]{:S(2)}) async-start(bf16[4,1024,3,192]{1,3,2,0:T(8,128)(2,1)} %copy.195), calls=%async_computation | async-start | bytes 9437184 | tf_op jit(solution)/shard_map/all_to_all | solution.py:184
  151.8 11.5 copy-start.3
  187.8 11.5 copy-start.3
  223.8 11.5 copy-start.3
  259.9 11.5 copy-start.3
  289.7 10.2 copy-start.42
  293.6 24.5 %all-to-all-start.1 = ((bf16[4,1024,192]{1,2,0:T(8,128)(2,1)}), bf16[4,1024,192]{1,2,0:T(8,128)(2,1)}, u32[]{:S(2)}, u32[]{:S(2)}) async-start(bf16[4,1024,192]{1,2,0:T(8,128)(2,1)} %copy.198), calls=%async_computation.1 | async-start | bytes 3145728 | tf_op jit(solution)/shard_map/all_to_all | solution.py:192
  298.0 97.5 %copy-start.36 = (f32[768]{0:T(1024)}, f32[768]{0:T(1024)S(1)}, u32[]{:S(2)}) copy-start(f32[768]{0:T(1024)S(1)} %convert_element_type.170) | copy-start | bytes 9220
  322.6 36.7 %copy-start.9 = (f32[1024,768]{0,1:T(8,128)}, f32[1024,768]{0,1:T(8,128)S(1)}, u32[]{:S(2)}) copy-start(f32[1024,768]{0,1:T(8,128)S(1)} %get-tuple-element.599) | copy-start | bytes 9437188
  322.6 72.9 %copy-start.24 = (f32[1024]{0:T(1024)}, f32[1024]{0:T(1024)S(1)}, u32[]{:S(2)}) copy-start(f32[1024]{0:T(1024)S(1)} %broadcast_multiply_fusion) | copy-start | bytes 12292
  323.4 72.2 %copy-start.37 = (f32[1024]{0:T(1024)}, f32[1024]{0:T(1024)S(1)}, u32[]{:S(2)}) copy-start(f32[1024]{0:T(1024)S(1)} %fusion.107) | copy-start | bytes 12292
  323.4 35.9 %copy-start.17 = (bf16[1,1024,768]{2,1,0:T(8,128)(2,1)S(1)}, bf16[1,1024,768]{2,1,0:T(8,128)(2,1)}, u32[]{:S(2)}) copy-start(bf16[1,1024,768]{2,1,0:T(8,128)(2,1)} %param.33) | copy-start | bytes 4718596
  474.9 13.4 copy-start.2
  559.6 13.4 copy-start.2
  646.1 13.4 copy-start.2
  732.6 13.4 copy-start.2
  896.7 58.8 %all-to-all-start.3 = ((bf16[4,1024,3,192]{1,3,2,0:T(8,128)(2,1)}), bf16[4,1024,3,192]{1,3,2,0:T(8,128)(2,1)}, u32[]{:S(2)}, u32[]{:S(2)}) async-start(bf16[4,1024,3,192]{1,3,2,0:T(8,128)(2,1)} %copy.207), calls=%async_computation.3 | async-start | bytes 9437184 | tf_op jit(solution)/shard_map/all_to_all | solution.py:238
  901.7 530.1 %reduce-scatter.8.cloned.1.call-start = ((), (), s32[]{:S(2)}) async-start(), calls=%async_computation.10 | async-start | bytes 2654208 | tf_op jit(solution)/shard_map/reduce_scatter | solution.py:278
  906.5 605.1 %reduce-scatter.14.cloned.1.call-start = ((), (), s32[]{:S(2)}) async-start(), calls=%async_computation.13 | async-start | bytes 3538944 | tf_op jit(solution)/shard_map/reduce_scatter | solution.py:281
  981.9 695.7 %reduce-scatter.12.cloned.1.call-start = ((), (), s32[]{:S(2)}) async-start(), calls=%async_computation.12 | async-start | bytes 10616832 | tf_op jit(solution)/shard_map/reduce_scatter | solution.py:280
  992.1 851.5 %reduce-scatter.10.cloned.1.call-start = ((), (), s32[]{:S(2)}) async-start(), calls=%async_computation.11 | async-start | bytes 10616832 | tf_op jit(solution)/shard_map/reduce_scatter | solution.py:279
  1003.7 971.6 %reduce-scatter.6.cloned.1.call-start = ((), (), s32[]{:S(2)}) async-start(), calls=%async_computation.9 | async-start | bytes 7962624 | tf_op jit(solution)/shard_map/reduce_scatter | solution.py:277
  1014.6 1016.1 %all-reduce.4.cloned.1.call-start = ((), (), s32[]{:S(2)}) async-start(), calls=%async_computation.14 | async-start | bytes 3932160 | tf_op jit(solution)/shard_map/psum | solution.py:284
  (43 other events, 156.5 us)
Sparse Core Ops, SparseCore 0:
  906.6 525.2 reduce-scatter.7
  1435.4 76.0 reduce-scatter.13
  1515.1 162.4 reduce-scatter.11
  1681.0 162.5 reduce-scatter.9
  1847.1 128.1 reduce-scatter.5
  1979.3 50.1 all-reduce.3
where the time goes:
time: 2060 us; the launch traced here: 2050 us
  waiting for transfers between devices  1060 us (51%)
  matrix products  488 us (24%)
  other arithmetic  199 us (10%)
  local copies, waits for them, and re-layouts  195 us (9%)
  blocking collectives  64.2 us (3%)
    reduce_scatter x1, waiting for transfers between devices, on_device(): lax.psum_scatter(matrices[1], 'dp', scatter_dimension=1, tiled=True)  404 us
    reduce_scatter x1, waiting for transfers between devices, on_device(): lax.psum_scatter(matrices[3], 'dp', scatter_dimension=1, tiled=True)  164 us
    reduce_scatter x1, waiting for transfers between devices, on_device(): lax.psum_scatter(matrices[2], 'dp', scatter_dimension=1, tiled=True)  164 us
    reduce_scatter x1, waiting for transfers between devices, on_device(): lax.psum_scatter(matrices[0], 'dp', scatter_dimension=1, tiled=True)  130 us
    dot_general x8, matrix products, one_block(): jnp.einsum('rqhe,rkhe->rhqk', query_block, keys_all, preferred_element_ty...  107 us
    convert_element_type x4, other arithmetic, one_block(): grad_scores = (weights_full * (grad_weights - inner)).astype(jnp.bfloat16)  84.4 us
    reduce_scatter x1, waiting for transfers between devices, on_device(): lax.psum_scatter(matrices[4], 'dp', scatter_dimension=1, tiled=True)  78.1 us
    dot_general x4, matrix products, one_block(): jnp.einsum('rqhe,rkhe->rhqk', grad_block, values, preferred_element_type=...  69.2 us
  transfers between devices with their start and end apart: 9, of which 8 were waited for; matrix products, arithmetic and copies ran while one was open for 5% of the time, Pallas kernels for 0%

commit v1 on v0

v1 whole, which is shorter than its diff:
```python
from functools import partial

import jax
import jax.numpy as jnp
from jax import lax
from jax.experimental import pallas as pl
from jax.experimental.pallas import tpu as pltpu
from jax.sharding import PartitionSpec as P

HEADS = 12
HEAD_DIM = 64
EPSILON = 1e-05
LOG2E = 1.4426950408889634
SCALE = HEAD_DIM**-0.5
BF16 = jnp.bfloat16
F32 = jnp.float32
NN = (((1,), (0,)), ((), ()))
NT = (((1,), (1,)), ((), ()))
TN = (((0,), (0,)), ((), ()))


def dot(left, right, dims=NN):
    return lax.dot_general(left, right, dims, preferred_element_type=F32)


def split_low(values, count):
    parts = []
    for _ in range(count):
        term = values.astype(BF16)
        parts.append(term)
        values = values - term.astype(F32)
    return parts


def attend_kernel(short_ref, heads_ref, sent_ref, mixed_ref, log_ref, keys, values, *, segment):
    step = pl.program_id(1)
    chunks = keys.shape[0]

    @pl.when(step == 0)
    def _():
        for chunk in range(chunks):
            source, part = divmod(chunk, 2)
            cols = slice(part * segment, (part + 1) * segment)
            key = heads_ref[source, 1, 0, :, cols]
            keys[chunk, 0:64, :] = key
            keys[chunk, 64:128, :] = key
            values[chunk, 0:64, :] = heads_ref[source, 2, 0, :, cols]
            values[chunk, 64:80, :] = jnp.ones((16, segment), BF16)

    source, part = step // 2, step % 2
    cols = pl.ds(pl.multiple_of(part * segment, segment), segment)
    scaled = heads_ref[source, 0, 0, :, cols].astype(F32) * (SCALE * LOG2E)
    queries = jnp.concatenate(split_low(scaled, 2), 0)

    def run(order):
        peak = total = None
        after = dot(keys[order[0]], queries, TN)
        for index, chunk in enumerate(order):
            scores = after
            if index + 1 < len(order):
                after = dot(keys[order[index + 1]], queries, TN)
            here = jnp.max(scores, 0, keepdims=True)
            top = here if peak is None else jnp.maximum(peak, here)
            weights = jnp.exp2(scores - top).astype(BF16)
            mixed = dot(values[chunk], weights)
            total = mixed if peak is None else total * jnp.exp2(peak - top) + mixed
            peak = top
        norm = total[64:65, :]
        mixed = total[:64] / norm
        mixed_ref[0, 0] = mixed
        sent_ref[0, 0] = mixed.astype(BF16)
        log_ref[0, 0] = peak + jnp.log2(norm)

    is_short = short_ref[0] != 0

    @pl.when(is_short)
    def _():
        run([2 * index + part for index in range(chunks // 2)])

    @pl.when(jnp.logical_not(is_short))
    def _():
        run(list(range(chunks)))


def attend(is_short, heads):
    sources, _, count, depth, tokens = heads.shape
    segment = tokens // 2
    work = count * (sources * tokens) ** 2
    return pl.pallas_call(
        partial(attend_kernel, segment=segment),
        grid_spec=pltpu.PrefetchScalarGridSpec(
            num_scalar_prefetch=1,
            grid=(count, 2 * sources),
            in_specs=[pl.BlockSpec((sources, 3, 1, depth, tokens), lambda h, i, s: (0, 0, h, 0, 0))],
            out_specs=[
                pl.BlockSpec((1, 1, depth, segment), lambda h, i, s: (h, i // 2, 0, i % 2)),
                pl.BlockSpec((1, 1, depth, segment), lambda h, i, s: (h, i // 2, 0, i % 2)),
                pl.BlockSpec((1, 1, 1, segment), lambda h, i, s: (h, i, 0, 0)),
            ],
            scratch_shapes=[
                pltpu.VMEM((2 * sources, 128, segment), BF16),
                pltpu.VMEM((2 * sources, 80, segment), BF16),
            ],
        ),
        out_shape=[
            jax.ShapeDtypeStruct((count, sources, depth, tokens), BF16),
            jax.ShapeDtypeStruct((count, sources, depth, tokens), F32),
            jax.ShapeDtypeStruct((count, 2 * sources, 1, segment), F32),
        ],
        compiler_params=pltpu.CompilerParams(vmem_limit_bytes=40 << 20),
        cost_estimate=pl.CostEstimate(
            flops=16 * work * depth, transcendentals=work, bytes_accessed=8 * heads.size // 3
        ),
        name="attend",
    )(is_short, heads)


def attend_back_kernel(
    short_ref, heads_ref, mixed_ref, grad_ref, log_ref, out_ref, q_aug, g_aug, k_aug, v_aug, grad_q, *, segment
):
    step = pl.program_id(1)
    chunks = q_aug.shape[0]

    @pl.when(step == 0)
    def _():
        minus = jnp.full((16, segment), -1.0, BF16)
        zeros = jnp.zeros((13, segment), BF16)
        for chunk in range(chunks):
            source, part = divmod(chunk, 2)
            cols = slice(part * segment, (part + 1) * segment)
            scaled = heads_ref[source, 0, 0, :, cols].astype(F32) * (SCALE * LOG2E)
            high, low = split_low(scaled, 2)
            q_aug[chunk, 0:64, :] = high
            q_aug[chunk, 64:128, :] = low
            q_aug[chunk, 128:144, :] = jnp.concatenate(split_low(log_ref[0, chunk], 3) + [zeros], 0)
            grad = grad_ref[0, source, :, cols]
            inner = jnp.sum(
                grad.astype(F32) * mixed_ref[0, source, :, cols], 0, keepdims=True
            )
            g_aug[chunk, 0:64, :] = grad
            g_aug[chunk, 64:80, :] = jnp.concatenate(split_low(inner, 3) + [zeros], 0)
            key = heads_ref[source, 1, 0, :, cols]
            k_aug[chunk, 0:64, :] = key
            k_aug[chunk, 64:128, :] = key
            k_aug[chunk, 128:144, :] = minus
            v_aug[chunk, 0:64, :] = heads_ref[source, 2, 0, :, cols]
            v_aug[chunk, 64:80, :] = minus
        grad_q[...] = jnp.zeros_like(grad_q)

    source, part = step // 2, step % 2
    cols = pl.ds(pl.multiple_of(part * segment, segment), segment)

    def run(order):
        key, value = k_aug[step], v_aug[step]
        turned = key[0:64].T

        def products(chunk):
            return dot(q_aug[chunk], key, TN), dot(g_aug[chunk], value, TN)

        key_total = value_total = None
        after = products(order[0])
        for index, chunk in enumerate(order):
            scores, grads = after
            if index + 1 < len(order):
                after = products(order[index + 1])
            weights = jnp.exp2(scores)
            g_scores = (weights * grads).astype(BF16)
            value_part = dot(g_aug[chunk, 0:64, :], weights.astype(BF16))
            key_part = dot(q_aug[chunk, 0:128, :], g_scores)
            value_total = value_part if value_total is None else value_total + value_part
            key_total = key_part if key_total is None else key_total + key_part
            grad_q[chunk] += dot(g_scores, turned)
        out_ref[source, 1, 0, :, cols] = (
            (key_total[0:64] + key_total[64:128]) * (1.0 / LOG2E)
        ).astype(BF16)
        out_ref[source, 2, 0, :, cols] = value_total.astype(BF16)

    is_short = short_ref[0] != 0

    @pl.when(is_short)
    def _():
        run([2 * index + part for index in range(chunks // 2)])

    @pl.when(jnp.logical_not(is_short))
    def _():
        run(list(range(chunks)))

    @pl.when(step == chunks - 1)
    def _():
        for chunk in range(chunks):
            source, part = divmod(chunk, 2)
            cols = slice(part * segment, (part + 1) * segment)
            out_ref[source, 0, 0, :, cols] = (grad_q[chunk] * SCALE).T.astype(BF16)


def attend_back(is_short, heads, mixed, grad, log_sums):
    sources, _, count, depth, tokens = heads.shape
    segment = tokens // 2
    work = count * (sources * tokens) ** 2
    return pl.pallas_call(
        partial(attend_back_kernel, segment=segment),
        grid_spec=pltpu.PrefetchScalarGridSpec(
            num_scalar_prefetch=1,
            grid=(count, 2 * sources),
            in_specs=[
                pl.BlockSpec((sources, 3, 1, depth, tokens), lambda h, i, s: (0, 0, h, 0, 0)),
                pl.BlockSpec((1, sources, depth, tokens), lambda h, i, s: (h, 0, 0, 0)),
                pl.BlockSpec((1, sources, depth, tokens), lambda h, i, s: (h, 0, 0, 0)),
                pl.BlockSpec((1, 2 * sources, 1, segment), lambda h, i, s: (h, 0, 0, 0)),
            ],
            out_specs=pl.BlockSpec((sources, 3, 1, depth, tokens), lambda h, i, s: (0, 0, h, 0, 0)),
            scratch_shapes=[
                pltpu.VMEM((2 * sources, 144, segment), BF16),
                pltpu.VMEM((2 * sources, 80, segment), BF16),
                pltpu.VMEM((2 * sources, 144, segment), BF16),
                pltpu.VMEM((2 * sources, 80, segment), BF16),
                pltpu.VMEM((2 * sources, segment, depth), F32),
            ],
        ),
        out_shape=jax.ShapeDtypeStruct(heads.shape, BF16),
        compiler_params=pltpu.CompilerParams(vmem_limit_bytes=40 << 20),
        cost_estimate=pl.CostEstimate(
            flops=40 * work * depth, transcendentals=work, bytes_accessed=6 * heads.size
        ),
        name="attend_back",
    )(is_short, heads, mixed, grad, log_sums)


def swap(values, axis, bit):
    size = lax.axis_size(axis)
    return lax.ppermute(values, axis, [(j, j ^ bit) for j in range(size)])


def sum_all(values):
    for axis in ("seq", "dp"):
        bit = 1
        while bit < lax.axis_size(axis):
            values = values + swap(values, axis, bit)
            bit *= 2
    return values


def halve(parts, axis, flag, bit):
    kept = lax.dynamic_index_in_dim(parts, flag, axis, keepdims=False)
    sent = lax.dynamic_index_in_dim(parts, 1 - flag, axis, keepdims=False)
    got = swap(sent, "seq", bit)
    return (kept.astype(F32) + got.astype(F32)).astype(BF16)


def reduce_columns(grad):
    dp = lax.axis_size("dp")
    place = lax.axis_index("seq")
    columns, rows = grad.shape
    parts = grad.reshape(dp, 2, 2, columns // dp // 4, rows)
    parts = halve(parts, 2, place % 2, 1)
    parts = halve(parts, 1, place // 2, 2)
    parts = lax.all_to_all(parts, "dp", split_axis=0, concat_axis=0, tiled=True)
    share = jnp.sum(parts.astype(F32), 0).astype(BF16)
    return lax.all_gather(share, "seq", axis=0, tiled=True).astype(F32)


def layer_norm(hidden, gain, shift):
    center = hidden - jnp.mean(hidden, -1, keepdims=True)
    spread = jnp.mean(center * center, -1, keepdims=True)
    return center * lax.rsqrt(spread + EPSILON) * gain + shift


def on_device(
    tokens,
    time_steps,
    data_group,
    cotangent,
    attn_norm_gain,
    attn_norm_bias,
    qkv_weight,
    query_bias,
    value_bias,
    out_weight,
    out_bias,
    mlp_norm_gain,
    mlp_norm_bias,
    up_weight,
    up_bias,
    down_weight,
    down_bias,
    time_table,
):
    sources = lax.axis_size("seq")
    dp = lax.axis_size("dp")
    inputs = tokens[0].astype(F32)
    tok_here, width = inputs.shape
    rounds = HEADS // sources
    half = tok_here // 2
    is_short = data_group[0] == 0
    short_flag = is_short.astype(jnp.int32)[None]
    row_table = time_table[time_steps[0]].astype(F32)
    second = jnp.where(is_short, row_table[1], row_table[0])
    hidden = (inputs.reshape(2, half, width) + jnp.stack([row_table[0], second])[:, None, :]).reshape(
        tok_here, width
    )
    gain_one = attn_norm_gain.astype(F32)
    shift_one = attn_norm_bias.astype(F32)
    normed, norm_one_back = jax.vjp(layer_norm, hidden, gain_one, shift_one)
    normed_low = normed.astype(BF16)
    bias_all = jnp.concatenate([query_bias, jnp.zeros_like(query_bias), value_bias]).astype(F32)
    projected = (dot(qkv_weight, normed_low, (((0,), (1,)), ((), ()))) + bias_all[:, None]).astype(BF16)
    by_round = projected.reshape(3, sources, rounds, HEAD_DIM, tok_here)

    def exchange(values):
        return lax.all_to_all(values, "seq", split_axis=0, concat_axis=0, tiled=True)

    heads, mixed, logs, returned = [], [], [], []
    for r in range(rounds):
        heads.append(exchange(jnp.swapaxes(by_round[:, :, r], 0, 1))[:, :, None])
    for r in range(rounds):
        sent, whole, log = attend(short_flag, heads[r])
        mixed.append(whole)
        logs.append(log)
        returned.append(exchange(sent[0]))
    attended = jnp.stack(returned, 1).reshape(width, tok_here)
    branch = dot(attended, out_weight, TN) + out_bias.astype(F32)
    resid = hidden + branch
    gain_two = mlp_norm_gain.astype(F32)
    shift_two = mlp_norm_bias.astype(F32)
    normed_two, norm_two_back = jax.vjp(layer_norm, resid, gain_two, shift_two)
    normed_two_low = normed_two.astype(BF16)
    up_act = dot(normed_two_low, up_weight) + up_bias.astype(F32)
    gelu_act, gelu_back = jax.vjp(partial(jax.nn.gelu, approximate=False), up_act)
    gelu_low = gelu_act.astype(BF16)
    down_out = dot(gelu_low, down_weight) + down_bias.astype(F32)
    result = (resid + down_out).astype(BF16)
    grad_out = cotangent[0].astype(F32)
    grad_down_low = cotangent[0]
    grad_down_b = jnp.sum(grad_down_low, 0, dtype=F32)
    grad_gelu = dot(grad_down_low, down_weight, NT)
    (grad_up_act,) = gelu_back(grad_gelu)
    grad_up_low = grad_up_act.astype(BF16)
    grad_up_b = jnp.sum(grad_up_low, 0, dtype=F32)
    grad_normed_two = dot(grad_up_low, up_weight, NT)
    grad_resid_norm, grad_gain_two, grad_shift_two = norm_two_back(grad_normed_two)
    grad_resid = grad_out + grad_resid_norm
    grad_branch = grad_resid.astype(BF16)
    grad_out_b = jnp.sum(grad_branch, 0, dtype=F32)
    grad_attended = dot(out_weight, grad_branch, NT).astype(BF16)
    grad_by_round = grad_attended.reshape(sources, rounds, HEAD_DIM, tok_here)
    grad_heads = [exchange(grad_by_round[:, r])[None] for r in range(rounds)]

    g_down_t = dot(grad_down_low, gelu_low, TN).astype(BF16)
    g_up_t = dot(grad_up_low, normed_two_low, TN).astype(BF16)
    g_out_t = dot(grad_branch, attended, (((0,), (1,)), ((), ()))).astype(BF16)
    sum_down = reduce_columns(g_down_t)
    sum_up = reduce_columns(g_up_t)
    sum_out = reduce_columns(g_out_t)
    mine = (jnp.arange(dp) == lax.axis_index("dp"))[:, None]
    first = lax.axis_index("seq") == 0
    steps_slot = jnp.where(mine & first, time_steps.astype(F32), 0.0)
    early = sum_all(
        jnp.concatenate(
            [grad_gain_two, grad_shift_two, grad_up_b, grad_down_b, grad_out_b, steps_slot.reshape(-1)]
        )
    )

    grad_back = []
    for r in range(rounds):
        g = attend_back(short_flag, heads[r], mixed[r], grad_heads[r], logs[r])
        grad_back.append(exchange(g[:, :, 0]))
    grad_qkv = jnp.swapaxes(jnp.stack(grad_back, 2), 0, 1).reshape(3 * width, tok_here)
    g_qkv_t = dot(grad_qkv, normed_low).astype(BF16)
    sum_qkv = reduce_columns(g_qkv_t)
    grad_qkv_b = jnp.sum(grad_qkv, 1, dtype=F32)
    grad_normed = dot(grad_qkv, qkv_weight, (((0,), (1,)), ((), ())))
    grad_hidden_norm, grad_gain_one, grad_shift_one = norm_one_back(grad_normed)
    grad_hidden = grad_resid + grad_hidden_norm
    grad_input = grad_hidden.astype(BF16)
    halves = jnp.sum(grad_hidden.reshape(2, half, width), 1)
    row_sums = jnp.where(
        is_short, halves, jnp.stack([halves[0] + halves[1], jnp.zeros_like(halves[0])])
    )
    row_slot = jnp.where(mine[:, :, None], row_sums[None], 0.0)
    late = sum_all(
        jnp.concatenate(
            [
                grad_gain_one,
                grad_shift_one,
                grad_qkv_b[:width],
                grad_qkv_b[2 * width :],
                row_slot.reshape(-1),
            ]
        )
    )
    ends = [width, width, up_bias.shape[0], width, width]
    points = [sum(ends[: i + 1]) for i in range(len(ends))]
    sum_gain_two, sum_shift_two, sum_up_b, sum_down_b, sum_out_b, all_steps = jnp.split(early, points)
    sum_gain_one, sum_shift_one, sum_query, sum_value, all_rows = jnp.split(
        late, [width, 2 * width, 3 * width, 4 * width]
    )
    table_rows = time_table.shape[0]
    share = width // dp
    rows_mine = lax.dynamic_slice_in_dim(
        all_rows.reshape(-1, width), lax.axis_index("dp") * share, share, 1
    )
    hits = (
        jnp.arange(table_rows, dtype=jnp.int32)[:, None] == all_steps.astype(jnp.int32)[None, :]
    ).astype(F32)
    sum_table = jnp.dot(hits, rows_mine, precision=lax.Precision.HIGHEST)
    return (
        result[None],
        grad_input[None],
        sum_gain_one,
        sum_shift_one,
        sum_qkv.T,
        sum_query,
        sum_value,
        sum_out.T,
        sum_out_b,
        sum_gain_two,
        sum_shift_two,
        sum_up.T,
        sum_up_b,
        sum_down.T,
        sum_down_b,
        sum_table,
    )


def solution(mesh):
    placed = (P("dp", "seq", None), P("dp", None), P("dp"), P("dp", "seq", None)) + (P(),) * 14
    column = P(None, "dp")
    return jax.shard_map(
        on_device,
        mesh=mesh,
        in_specs=placed,
        out_specs=(
            P("dp", "seq", None),
            P("dp", "seq", None),
            P(),
            P(),
            column,
            P(),
            P(),
            column,
            P(),
            P(),
            P(),
            column,
            P(),
            column,
            P(),
            column,
        ),
        check_vma=False,
    )
```

time: 2060 us -> 687 us (0.33)
  waiting for transfers between devices: 1060 us -> 79 us
  matrix products: 488 us -> 112 us
  Pallas kernels: 0 us -> 203 us
  other arithmetic: 199 us -> 61.4 us
  local copies, waits for them, and re-layouts: 195 us -> 87.5 us
  starting transfers between devices: 14.9 us -> 93.4 us
  blocking collectives: 64.2 us -> 37.2 us
    reduce_scatter x5 -> x0, waiting for transfers between devices: 940 us -> none  [the longest x1 404 us: on_device(): lax.psum_scatter(matrices[1], 'dp', scatter_dimension=1, tiled=True)]
    dot_general x44 -> x13, matrix products: 488 us -> 112 us  [the longest x12 110 us: dot(): return lax.dot_general(left, right, dims, preferred_element_type=F32)]
    pallas_call x0 -> x6, Pallas kernels: none -> 203 us  [the longest x3 126 us: attend_back(): pl.pallas_call(partial(attend_back_kernel, segment=segment), grid_spec=pl...]
    convert_element_type x21 -> x18, other arithmetic: 107 us -> 21.8 us  [the longest x8 16.7 us: halve(): return (kept.astype(F32) + got.astype(F32)).astype(BF16)]
    all_to_all x3 -> x16, waiting for transfers between devices: 119 us -> 37 us  [the longest x12 37 us: exchange(): lax.all_to_all(values, 'seq', split_axis=0, concat_axis=0, tiled=True)]
    another operation x9 -> x1, local copies, waits for them, and re-layouts: 65.5 us -> 0.12 us  [on_device(): attended = jnp.stack(returned, 1).reshape(width, tok_here)]
    all_to_all x3 -> x16, starting transfers between devices: 14.3 us -> 73.6 us  [the longest x12 52.8 us: exchange(): lax.all_to_all(values, 'seq', split_axis=0, concat_axis=0, tiled=True)]
    ppermute x0 -> x18, waiting for transfers between devices: none -> 42 us  [swap(): return lax.ppermute(values, axis, [(j, j ^ bit) for j in range(size)])]
  transfers between devices with their start and end apart: 9 -> 34, of which waited for: 8 -> 9; matrix products, arithmetic and copies ran while one was open for 5% -> 19% of each run, Pallas kernels for 0% -> 30%
where the time goes in v1:
time: 687 us; the launch traced here: 676 us
  Pallas kernels  203 us (30%)
  matrix products  112 us (16%)
  starting transfers between devices  93.4 us (14%)
  local copies, waits for them, and re-layouts  87.5 us (13%)
  waiting for transfers between devices  79 us (11%)
  other arithmetic  61.4 us (9%)
  blocking collectives  37.2 us (5%)
    pallas_call x3, Pallas kernels, attend_back(): pl.pallas_call(partial(attend_back_kernel, segment=segment), grid_spec=pl...  126 us
    dot_general x12, matrix products, dot(): return lax.dot_general(left, right, dims, preferred_element_type=F32)  110 us
    pallas_call x3, Pallas kernels, attend(): pl.pallas_call(partial(attend_kernel, segment=segment), grid_spec=pltpu.P...  77.4 us
    all_to_all x12, starting transfers between devices, exchange(): lax.all_to_all(values, 'seq', split_axis=0, concat_axis=0, tiled=True)  52.8 us
    unnamed x169, local copies, waits for them, and re-layouts  45.1 us
    ppermute x18, waiting for transfers between devices, swap(): return lax.ppermute(values, axis, [(j, j ^ bit) for j in range(size)])  42 us
    all_gather x4, blocking collectives, reduce_columns(): return lax.all_gather(share, 'seq', axis=0, tiled=True).astype(F32)  37.2 us
    all_to_all x12, waiting for transfers between devices, exchange(): lax.all_to_all(values, 'seq', split_axis=0, concat_axis=0, tiled=True)  37 us
  transfers between devices with their start and end apart: 34, of which 9 were waited for; matrix products, arithmetic and copies ran while one was open for 19% of the time, Pallas kernels for 30%

profile of v1, /device:TPU:0, one launch (start us, length us, event | category | flops | bytes accessed | tf_op | source)
XLA Modules:
  0.0 676.2 jit_solution(4867299237422023982)
XLA Ops:
  13.3 6.7 copy.47
  33.1 18.1 %all-to-all-done = bf16[4,3,64,1024]{3,2,1,0:T(8,128)(2,1)} async-done(((bf16[4,3,64,1024]{3,2,1,0:T(8,128)(2,1)}), bf16[4,3,64,1024]{3,2,1,0:T(8,128)(2,1)}, u32[]{:S(2)}, u32[]{:S(2)}) %all-to-all-start) | async-done | bytes 1572896 | tf_op jit(solution)/shard_map/all_to_all | solution.py:310
  65.2 10.6 %all-to-all-done.2 = bf16[4,3,64,1024]{3,2,1,0:T(8,128)(2,1)} async-done(((bf16[4,3,64,1024]{3,2,1,0:T(8,128)(2,1)}), bf16[4,3,64,1024]{3,2,1,0:T(8,128)(2,1)}, u32[]{:S(2)}, u32[]{:S(2)}) %all-to-all-start.2) | async-done | bytes 1572896 | tf_op jit(solution)/shard_map/all_to_all | solution.py:310
  80.2 25.8 %attend.3 = (bf16[1,4,64,1024]{3,2,1,0:T(8,128)(2,1)S(1)}, f32[1,4,64,1024]{3,2,1,0:T(8,128)S(1)}, f32[1,8,1,512]{3,2,1,0:T(1,128)S(1)}) custom-call(s32[1]{0:T(128)S(6)} %broadcast_in_dim.102.short_ref, bf16[4,3,1,64,1024]{4,3,2,1,0:T(8,128)(2,1)} %bitcast.10.heads_ref), custom_call_target="tpu_custom_call" | custom-call | flops 17179869184 | bytes 2097152 | tf_op jit(solution)/shard_map/attend/pallas_call | solution.py:89
  112.8 25.8 %attend.4 = (bf16[1,4,64,1024]{3,2,1,0:T(8,128)(2,1)S(1)}, f32[1,4,64,1024]{3,2,1,0:T(8,128)S(1)}, f32[1,8,1,512]{3,2,1,0:T(1,128)S(1)}) custom-call(s32[1]{0:T(128)S(6)} %broadcast_in_dim.102.short_ref, bf16[4,3,1,64,1024]{4,3,2,1,0:T(8,128)(2,1)} %bitcast.15.heads_ref), custom_call_target="tpu_custom_call" | custom-call | flops 17179869184 | bytes 2097152 | tf_op jit(solution)/shard_map/attend/pallas_call | solution.py:89
  145.2 25.8 %attend.5 = (bf16[1,4,64,1024]{3,2,1,0:T(8,128)(2,1)S(1)}, f32[1,4,64,1024]{3,2,1,0:T(8,128)S(1)}, f32[1,8,1,512]{3,2,1,0:T(1,128)S(1)}) custom-call(s32[1]{0:T(128)S(6)} %broadcast_in_dim.102.short_ref, bf16[4,3,1,64,1024]{4,3,2,1,0:T(8,128)(2,1)} %bitcast.20.heads_ref), custom_call_target="tpu_custom_call" | custom-call | flops 17179869184 | bytes 2097152 | tf_op jit(solution)/shard_map/attend/pallas_call | solution.py:89
  180.5 5.7 all-to-all-done.5
  191.3 35.3 %multiply_convert_fusion = (bf16[1024,3072]{1,0:T(8,128)(2,1)}, f32[1024,3072]{1,0:T(8,128)}, f32[1024,3072]{1,0:T(8,128)}) fusion(f32[3072]{0:T(1024)S(1)} %copy-done.62, bf16[768,3072]{1,0:T(8,128)(2,1)S(1)} %bitcast.242, f32[1024,768]{1,0:T(8,128)S(1)} %get-tuple-element.88, f32[768]{0:T(1024)S(1)} %copy-done.64, f32[768]{0:T(1024)S(1)} %copy-done.55, ...), kind=kOutput, calls=%fused_computation.5 | convolution fusion | flops 5043388416 | bytes 39348224 | tf_op jit(solution)/shard_map/dot_general | solution.py:23
  226.6 17.0 %convert_reduce_fusion = (f32[3072]{0:T(1024)}, bf16[1024,3072]{1,0:T(8,128)(2,1)}) fusion(f32[1024,3072]{1,0:T(8,128)} %get-tuple-element.66, bf16[3072,768]{1,0:T(8,128)(2,1)} %param.33, bf16[1,1024,768]{2,1,0:T(8,128)(2,1)} %param.21, f32[1024,3072]{1,0:T(8,128)} %get-tuple-element.89, f32[3072]{0:T(1024)} %convert_element_type.260), kind=kOutput, calls=%fused_computation.3 | convolution fusion | flops 4885312512 | bytes 37773312 | tf_op jit(solution)/shard_map/dot_general | solution.py:23
  243.6 10.1 %multiply_reduce_fusion = (f32[768]{0:T(1024)}, f32[1024]{0:T(1024)S(1)}, f32[768]{0:T(1024)}, f32[1024,768]{1,0:T(8,128)S(1)}) fusion(f32[1024,768]{1,0:T(8,128)S(1)} %get-tuple-element.88, f32[1024]{0:T(1024)S(1)} %fusion.27, f32[1024]{0:T(1024)S(1)} %broadcast_multiply_fusion, f32[768]{0:T(1024)S(1)} %copy-done.55, ...), kind=kOutput, calls=%fused_computation.40 | convolution fusion | flops 4838126592 | bytes 17323008 | tf_op jit(solution)/shard_map/dot_general | solution.py:23
  253.7 7.9 %convolution_convert_fusion.1 = bf16[3072,768]{1,0:T(8,128)(2,1)} fusion(bf16[1024,3072]{1,0:T(8,128)(2,1)S(1)} %copy-done.73, f32[1024,768]{1,0:T(8,128)S(1)} %get-tuple-element.88, f32[768]{0:T(1024)S(1)} %copy-done.64, f32[768]{0:T(1024)S(1)} %copy-done.55, f32[1024]{0:T(1024)S(1)} %fusion.27, f32[1024]{0:T(1024)S(1)} %broadcast_multiply_fusion), kind=kOutput, calls=%fused_computation.22 | convolution fusion | flops 4838129664 | bytes 14170112 | tf_op jit(solution)/shard_map/dot_general | solution.py:23
  272.3 7.7 %convolution_convert_fusion = bf16[3072,768]{0,1:T(8,128)(2,1)S(1)} fusion(bf16[1024,3072]{1,0:T(8,128)(2,1)} %get-tuple-element.65, bf16[1,1024,768]{2,1,0:T(8,128)(2,1)} %param.21), kind=kOutput, calls=%fused_computation.21 | convolution fusion | flops 4834197504 | bytes 12582912 | tf_op jit(solution)/shard_map/dot_general | solution.py:23
  306.2 41.9 %attend_back.3 = bf16[4,3,1,64,1024]{4,3,2,1,0:T(8,128)(2,1)S(1)} custom-call(s32[1]{0:T(128)S(6)} %broadcast_in_dim.102.short_ref, bf16[4,3,1,64,1024]{4,3,2,1,0:T(8,128)(2,1)} %bitcast.10.heads_ref, f32[1,4,64,1024]{3,2,1,0:T(8,128)S(1)} %copy-done.12, bf16[1,4,64,1024]{3,2,1,0:T(8,128)(2,1)} %bitcast.29.grad_ref, f32[1,8,1,512]{3,2,1,0:T(1,128)S(1)} %copy-done.16), custom_call_target="tpu_custom_call" | custom-call | flops 42949672960 | bytes 4718592 | tf_op jit(solution)/shard_map/attend_back/pallas_call | solution.py:200
  356.0 41.9 %attend_back.4 = bf16[4,3,1,64,1024]{4,3,2,1,0:T(8,128)(2,1)S(1)} custom-call(s32[1]{0:T(128)S(6)} %broadcast_in_dim.102.short_ref, bf16[4,3,1,64,1024]{4,3,2,1,0:T(8,128)(2,1)} %bitcast.15.heads_ref, f32[1,4,64,1024]{3,2,1,0:T(8,128)S(1)} %copy-done.10, bf16[1,4,64,1024]{3,2,1,0:T(8,128)(2,1)} %bitcast.34.grad_ref, f32[1,8,1,512]{3,2,1,0:T(1,128)S(1)} %copy-done.14), custom_call_target="tpu_custom_call" | custom-call | flops 42949672960 | bytes 4718592 | tf_op jit(solution)/shard_map/attend_back/pallas_call | solution.py:200
  404.9 41.9 %attend_back.5 = bf16[4,3,1,64,1024]{4,3,2,1,0:T(8,128)(2,1)S(1)} custom-call(s32[1]{0:T(128)S(6)} %broadcast_in_dim.102.short_ref, bf16[4,3,1,64,1024]{4,3,2,1,0:T(8,128)(2,1)} %bitcast.20.heads_ref, f32[1,4,64,1024]{3,2,1,0:T(8,128)S(1)} %copy-done.8, bf16[1,4,64,1024]{3,2,1,0:T(8,128)(2,1)} %bitcast.38.grad_ref, ...), custom_call_target="tpu_custom_call" | custom-call | flops 42949672960 | bytes 4718592 | tf_op jit(solution)/shard_map/attend_back/pallas_call | solution.py:200
  466.1 13.1 %collective-permute-done.8 = bf16[8,24,768]{2,1,0:T(8,128)(2,1)S(1)} collective-permute-done((bf16[8,24,768]{2,1,0:T(8,128)(2,1)S(1)}, bf16[8,24,768]{2,1,0:T(8,128)(2,1)S(1)}, u32[]{:S(2)}, u32[]{:S(2)}) %collective-permute-start.8) | collective-permute-done | bytes 294944 | tf_op jit(solution)/shard_map/ppermute | solution.py:231
  479.9 6.0 all-to-all-start.13
  510.1 21.4 %collective-permute-done.17 = bf16[8,24,3072]{2,1,0:T(8,128)(2,1)S(1)} collective-permute-done((bf16[8,24,3072]{2,1,0:T(8,128)(2,1)S(1)}, bf16[8,24,3072]{2,1,0:T(8,128)(2,1)S(1)}, u32[]{:S(2)}, u32[]{:S(2)}) %collective-permute-start.17) | collective-permute-done | bytes 1179680 | tf_op jit(solution)/shard_map/ppermute | solution.py:231
  532.9 6.0 all-to-all-start.15
  582.6 10.0 %fusion.19 = bf16[1,1024,768]{2,1,0:T(8,128)(2,1)} fusion(f32[1024,768]{1,0:T(8,128)} %copy-done.20, f32[768]{0:T(1024)S(1)} %convert_element_type.262, bf16[1024,3072]{1,0:T(8,128)(2,1)} %get-tuple-element.65, bf16[3072,768]{1,0:T(8,128)(2,1)} %param.33), kind=kOutput, calls=%fused_computation.75 | convolution fusion | flops 4834197504 | bytes 15731712 | tf_op jit(solution)/shard_map/dot_general | solution.py:23
  605.9 15.0 %all_gather.13 = bf16[96,768]{1,0:T(8,128)(2,1)S(1)} all-gather(bf16[24,768]{1,0:T(8,128)(2,1)} %reduce_sum.246), channel_id=1, replica_groups=mesh['dp'=8,'seq'=4] {'seq'}, dimensions={0}, use_global_device_ids=true | all-gather | bytes 184320 | tf_op jit(solution)/shard_map/all_gather | solution.py:259
  643.7 7.3 %all_gather.14 = bf16[384,768]{1,0:T(8,128)(2,1)S(1)} all-gather(bf16[96,768]{1,0:T(8,128)(2,1)} %reduce_sum.252), channel_id=1, replica_groups=mesh['dp'=8,'seq'=4] {'seq'}, dimensions={0}, use_global_device_ids=true | all-gather | bytes 737280 | tf_op jit(solution)/shard_map/all_gather | solution.py:259
  656.8 7.8 %all_gather.15 = bf16[96,3072]{1,0:T(8,128)(2,1)S(1)} all-gather(bf16[24,3072]{1,0:T(8,128)(2,1)} %reduce_sum.253), channel_id=1, replica_groups=mesh['dp'=8,'seq'=4] {'seq'}, dimensions={0}, use_global_device_ids=true | all-gather | bytes 737280 | tf_op jit(solution)/shard_map/all_gather | solution.py:259
  667.7 7.0 %all_gather.12 = bf16[288,768]{1,0:T(8,128)(2,1)S(1)} all-gather(bf16[72,768]{1,0:T(8,128)(2,1)} %reduce_sum.245), channel_id=1, replica_groups=mesh['dp'=8,'seq'=4] {'seq'}, dimensions={0}, use_global_device_ids=true | all-gather | bytes 552960 | tf_op jit(solution)/shard_map/all_gather | solution.py:259
  (339 shorter events, 257.3 us)
Async XLA Ops:
  26.1 25.1 %all-to-all-start = ((bf16[4,3,64,1024]{3,2,1,0:T(8,128)(2,1)}), bf16[4,3,64,1024]{3,2,1,0:T(8,128)(2,1)}, u32[]{:S(2)}, u32[]{:S(2)}) async-start(bf16[4,3,64,1024]{3,2,1,0:T(8,128)(2,1)} %bitcast.224), calls=%async_computation | async-start | bytes 3145728 | tf_op jit(solution)/shard_map/all_to_all | solution.py:310
  51.2 24.6 %all-to-all-start.2 = ((bf16[4,3,64,1024]{3,2,1,0:T(8,128)(2,1)}), bf16[4,3,64,1024]{3,2,1,0:T(8,128)(2,1)}, u32[]{:S(2)}, u32[]{:S(2)}) async-start(bf16[4,3,64,1024]{3,2,1,0:T(8,128)(2,1)} %bitcast.222), calls=%async_computation.2 | async-start | bytes 3145728 | tf_op jit(solution)/shard_map/all_to_all | solution.py:310
  75.8 32.6 %all-to-all-start.4 = ((bf16[4,3,64,1024]{3,2,1,0:T(8,128)(2,1)}), bf16[4,3,64,1024]{3,2,1,0:T(8,128)(2,1)}, u32[]{:S(2)}, u32[]{:S(2)}) async-start(bf16[4,3,64,1024]{3,2,1,0:T(8,128)(2,1)} %bitcast.223), calls=%async_computation.4 | async-start | bytes 3145728 | tf_op jit(solution)/shard_map/all_to_all | solution.py:310
  108.4 32.6 %all-to-all-start.1 = ((bf16[4,64,1024]{2,1,0:T(8,128)(2,1)}), bf16[4,64,1024]{2,1,0:T(8,128)(2,1)}, u32[]{:S(2)}, u32[]{:S(2)}) async-start(bf16[4,64,1024]{2,1,0:T(8,128)(2,1)} %bitcast.216), calls=%async_computation.1 | async-start | bytes 1048576 | tf_op jit(solution)/shard_map/all_to_all | solution.py:310
  141.0 31.7 %all-to-all-start.3 = ((bf16[4,64,1024]{2,1,0:T(8,128)(2,1)}), bf16[4,64,1024]{2,1,0:T(8,128)(2,1)}, u32[]{:S(2)}, u32[]{:S(2)}) async-start(bf16[4,64,1024]{2,1,0:T(8,128)(2,1)} %bitcast.217), calls=%async_computation.3 | async-start | bytes 1048576 | tf_op jit(solution)/shard_map/all_to_all | solution.py:310
  284.1 217.8 %collective-permute-start.16 = (bf16[8,2,24,3072]{3,2,1,0:T(8,128)(2,1)}, bf16[8,2,24,3072]{3,2,1,0:T(8,128)(2,1)}, u32[]{:S(2)}, u32[]{:S(2)}) collective-permute-start(bf16[8,2,24,3072]{3,2,1,0:T(8,128)(2,1)} %dynamic-slice_bitcast_fusion), channel_id=1, source_target_pairs={{0,1},{1,0},{2,3},{3,2},{4,5},{5,4},{6,7},{7,6},{8,9},{9,8},{10,11... | collective-permute-start | bytes 7077896 | tf_op jit(solution)/shard_map/ppermute | solution.py:231
  293.2 161.9 %collective-permute-start.7 = (bf16[8,2,24,768]{3,2,1,0:T(8,128)(2,1)}, bf16[8,2,24,768]{3,2,1,0:T(8,128)(2,1)}, u32[]{:S(2)}, u32[]{:S(2)}) collective-permute-start(bf16[8,2,24,768]{3,2,1,0:T(8,128)(2,1)} %dynamic-slice_bitcast_fusion.5), channel_id=1, source_target_pairs={{0,1},{1,0},{2,3},{3,2},{4,5},{5,4},{6,7},{7,6},{8,9},{9,8},{10,11... | collective-permute-start | bytes 1769480 | tf_op jit(solution)/shard_map/ppermute | solution.py:231
  300.2 49.2 %all-to-all-start.10 = ((bf16[4,64,1024]{2,1,0:T(8,128)(2,1)}), bf16[4,64,1024]{2,1,0:T(8,128)(2,1)}, u32[]{:S(2)}, u32[]{:S(2)}) async-start(bf16[4,64,1024]{2,1,0:T(8,128)(2,1)} %get-tuple-element.75), calls=%async_computation.10 | async-start | bytes 1048576 | tf_op jit(solution)/shard_map/all_to_all | solution.py:310
  349.3 49.8 %all-to-all-start.7 = ((bf16[4,3,64,1024]{3,2,1,0:T(8,128)(2,1)}), bf16[4,3,64,1024]{3,2,1,0:T(8,128)(2,1)}, u32[]{:S(2)}, u32[]{:S(2)}) async-start(bf16[4,3,64,1024]{3,2,1,0:T(8,128)(2,1)} %bitcast.214), calls=%async_computation.7 | async-start | bytes 3145728 | tf_op jit(solution)/shard_map/all_to_all | solution.py:310
  399.1 48.9 %all-to-all-start.9 = ((bf16[4,3,64,1024]{3,2,1,0:T(8,128)(2,1)}), bf16[4,3,64,1024]{3,2,1,0:T(8,128)(2,1)}, u32[]{:S(2)}, u32[]{:S(2)}) async-start(bf16[4,3,64,1024]{3,2,1,0:T(8,128)(2,1)} %bitcast.213), calls=%async_computation.9 | async-start | bytes 3145728 | tf_op jit(solution)/shard_map/all_to_all | solution.py:310
  448.0 32.0 %all-to-all-start.11 = ((bf16[4,3,64,1024]{3,2,1,0:T(8,128)(2,1)}), bf16[4,3,64,1024]{3,2,1,0:T(8,128)(2,1)}, u32[]{:S(2)}, u32[]{:S(2)}) async-start(bf16[4,3,64,1024]{3,2,1,0:T(8,128)(2,1)} %bitcast.212), calls=%async_computation.11 | async-start | bytes 3145728 | tf_op jit(solution)/shard_map/all_to_all | solution.py:310
  456.5 22.6 %collective-permute-start.8 = (bf16[8,24,768]{2,1,0:T(8,128)(2,1)S(1)}, bf16[8,24,768]{2,1,0:T(8,128)(2,1)S(1)}, u32[]{:S(2)}, u32[]{:S(2)}) collective-permute-start(bf16[8,24,768]{2,1,0:T(8,128)(2,1)S(1)} %dynamic-slice_bitcast_fusion.6), channel_id=1, source_target_pairs={{0,2},{1,3},{2,0},{3,1},{4,6},{5,7},{6,4},{7,5},{8,10},{9,11},{10,... | collective-permute-start | bytes 884744 | tf_op jit(solution)/shard_map/ppermute | solution.py:231
  464.9 74.1 %collective-permute-start.14 = (bf16[8,2,96,768]{3,2,0,1:T(8,128)(2,1)}, bf16[8,2,96,768]{3,2,0,1:T(8,128)(2,1)}, u32[]{:S(2)}, u32[]{:S(2)}) collective-permute-start(bf16[8,2,96,768]{3,2,0,1:T(8,128)(2,1)} %bitcast.206), channel_id=1, source_target_pairs={{0,1},{1,0},{2,3},{3,2},{4,5},{5,4},{6,7},{7,6},{8,9},{9,8},{10,11... | collective-permute-start | bytes 7077896 | tf_op jit(solution)/shard_map/ppermute | solution.py:231
  466.0 92.7 %collective-permute-start.10 = (f32[6160]{0:T(1024)}, f32[6160]{0:T(1024)}, u32[]{:S(2)}, u32[]{:S(2)}) collective-permute-start(f32[6160]{0:T(1024)} %add.279), channel_id=1, source_target_pairs={{0,2},{1,3},{2,0},{3,1},{4,6},{5,7},{6,4},{7,5},{8,10},{9,11},{10,... | collective-permute-start | bytes 73928 | tf_op jit(solution)/shard_map/ppermute | solution.py:231
  479.9 53.0 %all-to-all-start.13 = ((bf16[8,24,768]{2,1,0:T(8,128)(2,1)}), bf16[8,24,768]{2,1,0:T(8,128)(2,1)}, u32[]{:S(2)}, u32[]{:S(2)}) async-start(bf16[8,24,768]{2,1,0:T(8,128)(2,1)} %fusion.21), calls=%async_computation.13 | async-start | bytes 589824 | tf_op jit(solution)/shard_map/all_to_all | solution.py:257
  504.5 27.0 %collective-permute-start.17 = (bf16[8,24,3072]{2,1,0:T(8,128)(2,1)S(1)}, bf16[8,24,3072]{2,1,0:T(8,128)(2,1)S(1)}, u32[]{:S(2)}, u32[]{:S(2)}) collective-permute-start(bf16[8,24,3072]{2,1,0:T(8,128)(2,1)S(1)} %dynamic-slice_bitcast_fusion.2), channel_id=1, source_target_pairs={{0,2},{1,3},{2,0},{3,1},{4,6},{5,7},{6,4},{7,5},{8,10},{9,11},{10,... | collective-permute-start | bytes 3538952 | tf_op jit(solution)/shard_map/ppermute | solution.py:231
  532.9 45.4 %all-to-all-start.15 = ((bf16[8,24,3072]{2,1,0:T(8,128)(2,1)}), bf16[8,24,3072]{2,1,0:T(8,128)(2,1)}, u32[]{:S(2)}, u32[]{:S(2)}) async-start(bf16[8,24,3072]{2,1,0:T(8,128)(2,1)} %fusion.13), calls=%async_computation.15 | async-start | bytes 2359296 | tf_op jit(solution)/shard_map/all_to_all | solution.py:257
  544.5 30.9 %collective-permute-start.15 = (bf16[8,96,768]{2,1,0:T(8,128)(2,1)}, bf16[8,96,768]{2,1,0:T(8,128)(2,1)}, u32[]{:S(2)}, u32[]{:S(2)}) collective-permute-start(bf16[8,96,768]{2,1,0:T(8,128)(2,1)} %dynamic-slice_bitcast_fusion.3), channel_id=1, source_target_pairs={{0,2},{1,3},{2,0},{3,1},{4,6},{5,7},{6,4},{7,5},{8,10},{9,11},{10,... | collective-permute-start | bytes 3538952 | tf_op jit(solution)/shard_map/ppermute | solution.py:231
  552.4 43.8 %collective-permute-start.5 = (bf16[8,2,72,768]{3,2,1,0:T(8,128)(2,1)}, bf16[8,2,72,768]{3,2,1,0:T(8,128)(2,1)}, u32[]{:S(2)}, u32[]{:S(2)}) collective-permute-start(bf16[8,2,72,768]{3,2,1,0:T(8,128)(2,1)} %dynamic-slice_bitcast_fusion.1), channel_id=1, source_target_pairs={{0,1},{1,0},{2,3},{3,2},{4,5},{5,4},{6,7},{7,6},{8,9},{9,8},{10,11... | collective-permute-start | bytes 5308424 | tf_op jit(solution)/shard_map/ppermute | solution.py:231
  569.8 22.8 %collective-permute-start.13 = (f32[6160]{0:T(1024)}, f32[6160]{0:T(1024)}, u32[]{:S(2)}, u32[]{:S(2)}) collective-permute-start(f32[6160]{0:T(1024)} %add.282), channel_id=1, source_target_pairs={{0,16},{4,20},{8,24},{12,28},{16,0},{20,4},{24,8},{28,12},{1,17},{... | collective-permute-start | bytes 73928 | tf_op jit(solution)/shard_map/ppermute | solution.py:231
  574.0 19.4 %collective-permute-start.1 = (f32[15360]{0:T(1024)}, f32[15360]{0:T(1024)}, u32[]{:S(2)}, u32[]{:S(2)}) collective-permute-start(f32[15360]{0:T(1024)} %add.262), channel_id=1, source_target_pairs={{0,2},{1,3},{2,0},{3,1},{4,6},{5,7},{6,4},{7,5},{8,10},{9,11},{10,... | collective-permute-start | bytes 184328 | tf_op jit(solution)/shard_map/ppermute | solution.py:231
  578.3 57.3 %all-to-all-start.14 = ((bf16[8,96,768]{2,1,0:T(8,128)(2,1)}), bf16[8,96,768]{2,1,0:T(8,128)(2,1)}, u32[]{:S(2)}, u32[]{:S(2)}) async-start(bf16[8,96,768]{2,1,0:T(8,128)(2,1)} %fusion.14), calls=%async_computation.14 | async-start | bytes 2359296 | tf_op jit(solution)/shard_map/all_to_all | solution.py:257
  600.3 32.7 %collective-permute-start.6 = (bf16[8,72,768]{2,1,0:T(8,128)(2,1)}, bf16[8,72,768]{2,1,0:T(8,128)(2,1)}, u32[]{:S(2)}, u32[]{:S(2)}) collective-permute-start(bf16[8,72,768]{2,1,0:T(8,128)(2,1)} %dynamic-slice_bitcast_fusion.4), channel_id=1, source_target_pairs={{0,2},{1,3},{2,0},{3,1},{4,6},{5,7},{6,4},{7,5},{8,10},{9,11},{10,... | collective-permute-start | bytes 2654216 | tf_op jit(solution)/shard_map/ppermute | solution.py:231
  635.6 30.2 %all-to-all-start.12 = ((bf16[8,72,768]{2,1,0:T(8,128)(2,1)}), bf16[8,72,768]{2,1,0:T(8,128)(2,1)}, u32[]{:S(2)}, u32[]{:S(2)}) async-start(bf16[8,72,768]{2,1,0:T(8,128)(2,1)} %fusion.16), calls=%async_computation.12 | async-start | bytes 1769472 | tf_op jit(solution)/shard_map/all_to_all | solution.py:257
  (88 other events, 505.7 us)

commit v2 on v1

v2 whole, which is shorter than its diff:
```python
from functools import partial

import jax
import jax.numpy as jnp
from jax import lax
from jax.experimental import pallas as pl
from jax.experimental.pallas import tpu as pltpu
from jax.sharding import PartitionSpec as P

HEADS = 12
HEAD_DIM = 64
EPSILON = 1e-05
LOG2E = 1.4426950408889634
SCALE = HEAD_DIM**-0.5
BF16 = jnp.bfloat16
F32 = jnp.float32
NN = (((1,), (0,)), ((), ()))
NT = (((1,), (1,)), ((), ()))
TN = (((0,), (0,)), ((), ()))
VMEM = 62 << 20
SMALL_VMEM = 40 << 20


def dot(left, right, dims=NN):
    return lax.dot_general(left, right, dims, preferred_element_type=F32)


def split_low(values, count):
    parts = []
    for _ in range(count):
        term = values.astype(BF16)
        parts.append(term)
        values = values - term.astype(F32)
    return parts


def whole(*shape):
    return pl.BlockSpec(shape, lambda *_: (0,) * len(shape))


def halves(sources, segment):
    for chunk in range(2 * sources):
        source, part = divmod(chunk, 2)
        yield chunk, source, slice(part * segment, (part + 1) * segment)


def by_length(short_ref, run, chunks):
    part = pl.program_id(0) % 2
    is_short = short_ref[0] != 0

    @pl.when(is_short)
    def _():
        run([2 * index + part for index in range(chunks // 2)])

    @pl.when(jnp.logical_not(is_short))
    def _():
        run(list(range(chunks)))


def attend_kernel(short_ref, *refs, sources, segment, held):
    heads, refs = refs[:sources], refs[sources:]
    earlier, refs = refs[: sources * held], refs[sources * held :]
    sent, refs = refs[:sources], refs[sources:]
    mixed_ref, log_ref, queries, keys, values = refs
    step = pl.program_id(0)
    chunks = 2 * sources

    @pl.when(step == 0)
    def _():
        for old, new in zip(earlier, sent):
            new[0] = old[0]
        for chunk, source, cols in halves(sources, segment):
            scaled = heads[source][0, :, cols].astype(F32) * (SCALE * LOG2E)
            high, low = split_low(scaled, 2)
            queries[chunk, 0:64, :] = high
            queries[chunk, 64:128, :] = low
            key = heads[source][1, :, cols]
            keys[chunk, 0:64, :] = key
            keys[chunk, 64:128, :] = key
            values[chunk, 0:64, :] = heads[source][2, :, cols]
            values[chunk, 64:80, :] = jnp.ones((16, segment), BF16)

    def run(order):
        query = queries[step]
        peak = total = None
        later = dot(keys[order[0]], query, TN)
        for index, chunk in enumerate(order):
            scores = later
            if index + 1 < len(order):
                later = dot(keys[order[index + 1]], query, TN)
            here = jnp.max(scores, 0, keepdims=True)
            top = here if peak is None else jnp.maximum(peak, here)
            weights = jnp.exp2(scores - top).astype(BF16)
            mixed = dot(values[chunk], weights)
            total = mixed if peak is None else total * jnp.exp2(peak - top) + mixed
            peak = top
        norm = total[64:65, :]
        result = total[:64] / norm
        mixed_ref[step] = result
        log_ref[step] = peak + jnp.log2(norm)
        for chunk, source, cols in halves(sources, segment):

            @pl.when(step == chunk)
            def _():
                sent[source][held, :, cols] = result.astype(BF16)

    by_length(short_ref, run, chunks)


def attend(is_short, heads, earlier=()):
    sources = len(heads)
    _, depth, tokens = heads[0].shape
    segment, chunks = tokens // 2, 2 * sources
    work = (sources * tokens) ** 2
    held = len(earlier) // sources
    out = pl.pallas_call(
        partial(attend_kernel, sources=sources, segment=segment, held=held),
        grid_spec=pltpu.PrefetchScalarGridSpec(
            num_scalar_prefetch=1,
            grid=(chunks,),
            in_specs=[whole(3, depth, tokens)] * sources + [whole(1, depth, tokens)] * len(earlier),
            out_specs=[whole(1 + held, depth, tokens)] * sources
            + [whole(chunks, depth, segment), whole(chunks, 1, segment)],
            scratch_shapes=[
                pltpu.VMEM((chunks, 128, segment), BF16),
                pltpu.VMEM((chunks, 128, segment), BF16),
                pltpu.VMEM((chunks, 80, segment), BF16),
            ],
        ),
        out_shape=[jax.ShapeDtypeStruct((1 + held, depth, tokens), BF16)] * sources
        + [
            jax.ShapeDtypeStruct((chunks, depth, segment), F32),
            jax.ShapeDtypeStruct((chunks, 1, segment), F32),
        ],
        compiler_params=pltpu.CompilerParams(vmem_limit_bytes=SMALL_VMEM),
        cost_estimate=pl.CostEstimate(
            flops=16 * work * depth, transcendentals=work, bytes_accessed=16 * sources * tokens * depth
        ),
        name="attend",
    )(is_short, *heads, *earlier)
    return out[:sources], out[-2], out[-1]


def attend_back_kernel(short_ref, *refs, sources, segment):
    heads, grads, (mixed_ref, log_ref), refs = (
        refs[:sources],
        refs[sources : 2 * sources],
        refs[2 * sources : 2 * sources + 2],
        refs[2 * sources + 2 :],
    )
    outs, (q_aug, g_aug, k_aug, v_aug, grad_q) = refs[:sources], refs[sources:]
    step = pl.program_id(0)
    chunks = 2 * sources

    @pl.when(step == 0)
    def _():
        minus = jnp.full((16, segment), -1.0, BF16)
        zeros = jnp.zeros((13, segment), BF16)
        for chunk, source, cols in halves(sources, segment):
            scaled = heads[source][0, :, cols].astype(F32) * (SCALE * LOG2E)
            high, low = split_low(scaled, 2)
            q_aug[chunk, 0:64, :] = high
            q_aug[chunk, 64:128, :] = low
            q_aug[chunk, 128:144, :] = jnp.concatenate(split_low(log_ref[chunk], 3) + [zeros], 0)
            grad = grads[source][0, :, cols]
            inner = jnp.sum(grad.astype(F32) * mixed_ref[chunk], 0, keepdims=True)
            g_aug[chunk, 0:64, :] = grad
            g_aug[chunk, 64:80, :] = jnp.concatenate(split_low(inner, 3) + [zeros], 0)
            key = heads[source][1, :, cols]
            k_aug[chunk, 0:64, :] = key
            k_aug[chunk, 64:128, :] = key
            k_aug[chunk, 128:144, :] = minus
            v_aug[chunk, 0:64, :] = heads[source][2, :, cols]
            v_aug[chunk, 64:80, :] = minus
        grad_q[...] = jnp.zeros_like(grad_q)

    def run(order):
        key, value = k_aug[step], v_aug[step]
        turned = key[0:64].T

        def products(chunk):
            return dot(q_aug[chunk], key, TN), dot(g_aug[chunk], value, TN)

        key_total = value_total = None
        later = products(order[0])
        for index, chunk in enumerate(order):
            scores, slopes = later
            if index + 1 < len(order):
                later = products(order[index + 1])
            weights = jnp.exp2(scores)
            g_scores = (weights * slopes).astype(BF16)
            value_part = dot(g_aug[chunk, 0:64, :], weights.astype(BF16))
            key_part = dot(q_aug[chunk, 0:128, :], g_scores)
            value_total = value_part if value_total is None else value_total + value_part
            key_total = key_part if key_total is None else key_total + key_part
            grad_q[chunk] += dot(g_scores, turned)
        key_grad = ((key_total[0:64] + key_total[64:128]) * (1.0 / LOG2E)).astype(BF16)
        value_grad = value_total.astype(BF16)
        for chunk, source, cols in halves(sources, segment):

            @pl.when(step == chunk)
            def _():
                outs[source][1, :, cols] = key_grad
                outs[source][2, :, cols] = value_grad

    by_length(short_ref, run, chunks)

    @pl.when(step == chunks - 1)
    def _():
        for chunk, source, cols in halves(sources, segment):
            outs[source][0, :, cols] = (grad_q[chunk] * SCALE).T.astype(BF16)


def attend_back(is_short, heads, mixed, grads, log_sums, at):
    sources = len(heads)
    _, depth, tokens = heads[0].shape
    segment, chunks = tokens // 2, 2 * sources
    work = (sources * tokens) ** 2
    return pl.pallas_call(
        partial(attend_back_kernel, sources=sources, segment=segment),
        grid_spec=pltpu.PrefetchScalarGridSpec(
            num_scalar_prefetch=1,
            grid=(chunks,),
            in_specs=[whole(3, depth, tokens)] * sources
            + [pl.BlockSpec((1, depth, tokens), lambda i, s: (at, 0, 0))] * sources
            + [whole(chunks, depth, segment), whole(chunks, 1, segment)],
            out_specs=[whole(3, depth, tokens)] * sources,
            scratch_shapes=[
                pltpu.VMEM((chunks, 144, segment), BF16),
                pltpu.VMEM((chunks, 80, segment), BF16),
                pltpu.VMEM((chunks, 144, segment), BF16),
                pltpu.VMEM((chunks, 80, segment), BF16),
                pltpu.VMEM((chunks, segment, depth), F32),
            ],
        ),
        out_shape=[jax.ShapeDtypeStruct((3, depth, tokens), BF16)] * sources,
        compiler_params=pltpu.CompilerParams(vmem_limit_bytes=VMEM),
        cost_estimate=pl.CostEstimate(
            flops=40 * work * depth, transcendentals=work, bytes_accessed=40 * sources * tokens * depth
        ),
        name="attend_back",
    )(is_short, *heads, *grads, mixed, log_sums)


def normalize(hidden):
    center = hidden - jnp.mean(hidden, -1, keepdims=True)
    spread = jnp.mean(center * center, -1, keepdims=True)
    inverse = lax.rsqrt(spread + EPSILON)
    return center * inverse, inverse


def token_block(index, size):
    return pl.ds(pl.multiple_of(index * size, size), size)


def column_sum(values):
    return jnp.sum(values.astype(F32), 0, keepdims=True)


def project_kernel(place_ref, tokens, rows, gain, shift, weight, bias, normed, *refs, sources, rounds, block):
    outs, turned = refs[:-1], refs[-1]
    step = pl.program_id(0)
    count = tokens.shape[0] // block

    @pl.when(step == 0)
    def _():
        def body(index, _):
            here = token_block(index, block)
            row = rows[pl.ds(index // (count // 2), 1), :]
            scaled, _ = normalize(tokens[here, :].astype(F32) + row)
            low = (scaled * gain[...] + shift[...]).astype(BF16)
            normed[here, :] = low
            turned[:, here] = low.T
            return 0

        lax.fori_loop(0, count, body, 0)

    result = (dot(weight[...], turned[...], TN) + bias[...]).astype(BF16)
    pair, low_bit = step % (sources // 2), place_ref[0] % 2
    for high in range(sources // 2):
        for bit in range(2):

            @pl.when((pair == high) & (low_bit == bit))
            def _():
                for low in range(2):
                    for r in range(rounds):
                        at = (low * rounds + r) * HEAD_DIM
                        outs[r * sources + 2 * high + (low ^ bit)][0] = result[at : at + HEAD_DIM]


def project(place, tokens, rows, gain, shift, weight, bias, sources, rounds):
    tok_here, width = tokens.shape
    pair = 2 * rounds * HEAD_DIM
    pairs = sources // 2
    block_of = lambda i, p: i // pairs * pairs + (i % pairs ^ p[0] // 2)
    out = pl.pallas_call(
        partial(project_kernel, sources=sources, rounds=rounds, block=tok_here // 4),
        grid_spec=pltpu.PrefetchScalarGridSpec(
            num_scalar_prefetch=1,
            grid=(3 * pairs,),
            in_specs=[
                whole(tok_here, width),
                whole(2, width),
                whole(1, width),
                whole(1, width),
                pl.BlockSpec((width, pair), lambda i, p: (0, block_of(i, p))),
                pl.BlockSpec((pair, 1), lambda i, p: (block_of(i, p), 0)),
            ],
            out_specs=[whole(tok_here, width)]
            + [pl.BlockSpec((1, HEAD_DIM, tok_here), lambda i, p: (i // pairs, 0, 0))] * (rounds * sources),
            scratch_shapes=[pltpu.VMEM((width, tok_here), BF16)],
        ),
        out_shape=[jax.ShapeDtypeStruct((tok_here, width), BF16)]
        + [jax.ShapeDtypeStruct((3, HEAD_DIM, tok_here), BF16)] * (rounds * sources),
        compiler_params=pltpu.CompilerParams(vmem_limit_bytes=SMALL_VMEM),
        cost_estimate=pl.CostEstimate(
            flops=2 * tok_here * weight.size, transcendentals=0, bytes_accessed=4 * weight.size
        ),
        name="project",
    )(place, tokens, rows, gain, shift, weight, bias)
    return out[0], [out[1 + r * sources : 1 + (r + 1) * sources] for r in range(rounds)]


def mlp_kernel(place_ref, *refs, groups, sources, block):
    (in_groups, out_groups), rounds = groups, sum(map(len, groups[0]))
    gathered, refs = refs[: len(in_groups) * sources], refs[len(in_groups) * sources :]
    pieces = len(out_groups) * sources
    tokens, rows, cotangent, out_w, out_b, gain, shift, up_w, up_b, down_w, down_b = refs[:11]
    result, g_resid = refs[11:13]
    sent_grads = refs[13 : 13 + pieces]
    send, keep, vectors, g_up_b = refs[13 + pieces : 17 + pieces]
    attended, normed, resid, gelu_act, g_up, down_sum, g_normed, g_branch, g_attended = refs[17 + pieces :]
    step, last = pl.program_id(0), pl.num_programs(0) - 1
    tok_here, width = tokens.shape
    count = tok_here // block
    place = place_ref[0]
    low_bit = place % 2 == 0

    def head_rows(groups):
        for index in range(len(groups) * sources):
            group, j = divmod(index, sources)
            for at, r in enumerate(groups[group]):
                start = ((place ^ j) * rounds + r) * HEAD_DIM
                yield index, at, pl.ds(pl.multiple_of(start, HEAD_DIM), HEAD_DIM)

    def put(slot, grad):
        grad = grad.astype(BF16)
        middle = grad.shape[1] // 2
        left, right = grad[:, :middle], grad[:, middle:]

        @pl.when(low_bit)
        def _():
            keep[slot], send[slot] = left, right

        @pl.when(jnp.logical_not(low_bit))
        def _():
            keep[slot], send[slot] = right, left

    @pl.when(step == 0)
    def _():
        for index, at, here in head_rows(in_groups):
            attended[here, :] = gathered[index][at]

        def body(index, _):
            here = token_block(index, block)
            row = rows[pl.ds(index // (count // 2), 1), :]
            hidden = tokens[here, :].astype(F32) + row
            total = hidden + (dot(attended[:, here], out_w[...], TN) + out_b[...])
            resid[here, :] = total
            scaled, _ = normalize(total)
            normed[here, :] = (scaled * gain[...] + shift[...]).astype(BF16)
            return 0

        lax.fori_loop(0, count, body, 0)
        down_sum[...] = jnp.zeros_like(down_sum)
        g_normed[...] = jnp.zeros_like(g_normed)

    @pl.when(step < last)
    def _():
        def body(index, total):
            here = token_block(index, block)
            act = dot(normed[here, :], up_w[...]) + up_b[...]
            g_gelu = dot(cotangent[here, :], down_w[...], NT)
            below = 0.5 * (1.0 + lax.erf(act * 0.7071067811865476))
            density = 0.3989422804014327 * jnp.exp(-0.5 * act * act)
            low = (act * below).astype(BF16)
            grad = (g_gelu * (below + act * density)).astype(BF16)
            gelu_act[here, :] = low
            g_up[here, :] = grad
            down_sum[here, :] += dot(low, down_w[...])
            g_normed[here, :] += dot(grad, up_w[...], NT)
            return total + column_sum(grad)

        g_up_b[...] = lax.fori_loop(0, count, body, jnp.zeros(up_b.shape, F32))
        put(0, dot(g_up[...], normed[...], TN))
        put(1, dot(cotangent[...], gelu_act[...], TN))

    @pl.when(step == last)
    def _():
        def body(index, sums):
            here = token_block(index, block)
            total = resid[here, :]
            result[here, :] = (total + (down_sum[here, :] + down_b[...])).astype(BF16)
            scaled, inverse = normalize(total)
            grad = g_normed[here, :]
            inner = grad * gain[...]
            g_out = cotangent[here, :].astype(F32)
            g_total = g_out + inverse * (
                inner
                - jnp.mean(inner, -1, keepdims=True)
                - scaled * jnp.mean(inner * scaled, -1, keepdims=True)
            )
            g_resid[here, :] = g_total
            low = g_total.astype(BF16)
            g_branch[here, :] = low
            g_attended[:, here] = dot(out_w[...], low, NT).astype(BF16)
            parts = (grad * scaled, grad, low, g_out)
            return tuple(old + column_sum(new) for old, new in zip(sums, parts))

        empty = jnp.zeros((1, width), F32)
        sums = lax.fori_loop(0, count, body, (empty,) * 4)
        for index, at, here in head_rows(out_groups):
            sent_grads[index][at] = g_attended[here, :]
        for index, total in enumerate(sums):
            vectors[index : index + 1, :] = total
        put(0, dot(g_branch[...], attended[...], (((0,), (1,)), ((), ()))))
        put(1, jnp.zeros((width, width), F32))


def mlp(place, groups, gathered, tokens, rows, cotangent, out_w, out_b, gain, shift, up_w, up_b, down_w, down_b):
    tok_here, width = tokens.shape
    hidden_units = up_w.shape[1]
    sources = len(gathered[0])
    pieces = [part for group in gathered for part in group]
    depth = pieces[0].shape[1]
    shapes = [(len(group), depth, tok_here) for group in groups[1] for _ in range(sources)]
    steps = hidden_units // width
    slots = pl.BlockSpec((2, width, width // 2), lambda j, b: (j, 0, 0))
    at = lambda j: jnp.minimum(j, steps - 1)
    slot_shape = jax.ShapeDtypeStruct((2 * steps + 2, width, width // 2), BF16)
    out = pl.pallas_call(
        partial(mlp_kernel, groups=groups, sources=sources, block=tok_here // 2),
        grid_spec=pltpu.PrefetchScalarGridSpec(
            num_scalar_prefetch=1,
            grid=(steps + 1,),
            in_specs=[whole(*part.shape) for part in pieces]
            + [
                whole(tok_here, width),
                whole(2, width),
                whole(tok_here, width),
                whole(width, width),
                whole(1, width),
                whole(1, width),
                whole(1, width),
                pl.BlockSpec((width, width), lambda j, b: (0, at(j))),
                pl.BlockSpec((1, width), lambda j, b: (0, at(j))),
                pl.BlockSpec((width, width), lambda j, b: (at(j), 0)),
                whole(1, width),
            ],
            out_specs=[whole(tok_here, width)] * 2
            + [whole(*shape) for shape in shapes]
            + [slots, slots, whole(4, width), pl.BlockSpec((1, width), lambda j, b: (0, at(j)))],
            scratch_shapes=[
                pltpu.VMEM((width, tok_here), BF16),
                pltpu.VMEM((tok_here, width), BF16),
                pltpu.VMEM((tok_here, width), F32),
                pltpu.VMEM((tok_here, width), BF16),
                pltpu.VMEM((tok_here, width), BF16),
                pltpu.VMEM((tok_here, width), F32),
                pltpu.VMEM((tok_here, width), F32),
                pltpu.VMEM((tok_here, width), BF16),
                pltpu.VMEM((width, tok_here), BF16),
            ],
        ),
        out_shape=[
            jax.ShapeDtypeStruct((tok_here, width), BF16),
            jax.ShapeDtypeStruct((tok_here, width), F32),
        ]
        + [jax.ShapeDtypeStruct(shape, BF16) for shape in shapes]
        + [
            slot_shape,
            slot_shape,
            jax.ShapeDtypeStruct((4, width), F32),
            jax.ShapeDtypeStruct((1, hidden_units), F32),
        ],
        compiler_params=pltpu.CompilerParams(vmem_limit_bytes=VMEM),
        cost_estimate=pl.CostEstimate(
            flops=12 * tok_here * up_w.size, transcendentals=0, bytes_accessed=8 * up_w.size
        ),
        name="mlp",
    )(place, *pieces, tokens, rows, cotangent, out_w, out_b, gain, shift, up_w, up_b, down_w, down_b)
    grads = out[2 : 2 + len(shapes)]
    grads = [grads[g * sources : (g + 1) * sources] for g in range(len(groups[1]))]
    return out[0], out[1], grads, out[-4:]


def finish_kernel(place_ref, *refs, rounds, sources, block):
    pieces = rounds * sources
    back, refs = refs[:pieces], refs[pieces:]
    weight, tokens, rows, gain, g_resid, vectors, g_up_b, g_tokens, sums, g_normed, packed = refs
    step, last = pl.program_id(0), pl.num_programs(0) - 1
    pair, low_bit = step % (sources // 2), place_ref[0] % 2
    for high in range(sources // 2):

        @pl.when(pair == high)
        def _():
            for j in range(2 * high, 2 * high + 2):
                for r in range(rounds):
                    at = ((j % 2 ^ low_bit) * rounds + r) * HEAD_DIM
                    packed[pl.ds(pl.multiple_of(at, HEAD_DIM), HEAD_DIM), :] = back[r * sources + j][0]

    pairs, size = sources // 2, packed.shape[0]
    ones = jnp.ones((8, packed.shape[1]), BF16)
    bias = dot(ones, packed[...], NT)[0:1]
    for part in range(3):
        for at in range(pairs):

            @pl.when((step // pairs == part) & ((pair ^ place_ref[0] // 2) == at))
            def _():
                sums[10 + part : 11 + part, at * size : (at + 1) * size] = bias

    added = dot(packed[...], weight[...], (((0,), (1,)), ((), ())))

    @pl.when(step == 0)
    def _():
        g_normed[...] = added

    @pl.when(step > 0)
    def _():
        g_normed[...] += added

    @pl.when(step == last)
    def _():
        width = tokens.shape[1]
        count = tokens.shape[0] // block
        empty = jnp.zeros((1, width), F32)

        def half(first):
            def body(index, totals):
                here = token_block(index + first * (count // 2), block)
                scaled, inverse = normalize(tokens[here, :].astype(F32) + rows[first : first + 1, :])
                grad = g_normed[here, :]
                inner = grad * gain[...]
                g_hidden = g_resid[here, :] + inverse * (
                    inner
                    - jnp.mean(inner, -1, keepdims=True)
                    - scaled * jnp.mean(inner * scaled, -1, keepdims=True)
                )
                g_tokens[here, :] = g_hidden.astype(BF16)
                parts = (grad * scaled, grad, g_hidden)
                return tuple(old + column_sum(new) for old, new in zip(totals, parts))

            return lax.fori_loop(0, count // 2, body, (empty,) * 3)

        one, two = half(0), half(1)
        sums[0:1, :], sums[1:2, :] = one[0] + two[0], one[1] + two[1]
        sums[2:6, :] = vectors[...]
        for index in range(4):
            sums[6 + index : 7 + index, :] = g_up_b[:, index * width : (index + 1) * width]
        sums[13:14, :] = empty
        is_short = place_ref[1] != 0
        sums[14:15, :] = jnp.where(is_short, one[2], one[2] + two[2])
        sums[15:16, :] = jnp.where(is_short, two[2], 0.0)


def finish(place, back, weight, tokens, rows, gain, g_resid, vectors, g_up_b):
    tok_here, width = tokens.shape
    rounds, sources = len(back), len(back[0])
    pieces = [part for group in back for part in group]
    pair = 2 * rounds * HEAD_DIM
    pairs = sources // 2
    return pl.pallas_call(
        partial(finish_kernel, rounds=rounds, sources=sources, block=tok_here // 4),
        grid_spec=pltpu.PrefetchScalarGridSpec(
            num_scalar_prefetch=1,
            grid=(3 * pairs,),
            in_specs=[pl.BlockSpec((1, HEAD_DIM, tok_here), lambda i, p: (i // pairs, 0, 0))] * len(pieces)
            + [
                pl.BlockSpec(
                    (width, pair), lambda i, p: (0, i // pairs * pairs + (i % pairs ^ p[0] // 2))
                ),
                whole(tok_here, width),
                whole(2, width),
                whole(1, width),
                whole(tok_here, width),
                whole(*vectors.shape),
                whole(*g_up_b.shape),
            ],
            out_specs=[whole(tok_here, width), whole(16, width)],
            scratch_shapes=[pltpu.VMEM((tok_here, width), F32), pltpu.VMEM((pair, tok_here), BF16)],
        ),
        out_shape=[
            jax.ShapeDtypeStruct((tok_here, width), BF16),
            jax.ShapeDtypeStruct((16, width), F32),
        ],
        compiler_params=pltpu.CompilerParams(vmem_limit_bytes=SMALL_VMEM),
        cost_estimate=pl.CostEstimate(
            flops=2 * tok_here * weight.size, transcendentals=0, bytes_accessed=8 * weight.size
        ),
        name="finish",
    )(place, *pieces, weight, tokens, rows, gain, g_resid, vectors, g_up_b)


def qkv_grad_kernel(block_ref, *refs, rounds, sources, order):
    grads, refs = refs[: rounds * sources], refs[rounds * sources :]
    normed, (first, second, store) = refs[:sources], refs[sources:]
    size = 3 * HEAD_DIM
    for r in range(rounds):
        total = None
        for grad, part in zip(grads[r * sources : (r + 1) * sources], normed):
            here = jnp.concatenate([grad[p] for p in range(3)], 0)
            term = dot(here, part[...])
            total = term if total is None else total + term
        store[:, r * size : (r + 1) * size] = total.T.astype(BF16)
    half = len(order) // 2
    rows = first.shape[1]
    for at, index in enumerate(order):
        start = (block_ref[0] ^ index) * rows
        here = pl.ds(pl.multiple_of(start, rows), rows) if half > 1 else slice(at * rows, (at + 1) * rows)
        (second if at >= half else first)[at % half] = store[here, :]


def qkv_grad(block, grads, normed, order):
    rounds, sources = len(grads), len(normed)
    tok_here, width = normed[0].shape
    size = 3 * HEAD_DIM * rounds
    pieces = [part for group in grads for part in group]
    half = (len(order) // 2, width // len(order), size)
    return pl.pallas_call(
        partial(qkv_grad_kernel, rounds=rounds, sources=sources, order=order),
        grid_spec=pltpu.PrefetchScalarGridSpec(
            num_scalar_prefetch=1,
            grid=(1,),
            in_specs=[whole(*pieces[0].shape)] * len(pieces) + [whole(tok_here, width)] * sources,
            out_specs=[whole(*half)] * 2,
            scratch_shapes=[pltpu.VMEM((width, size), BF16)],
        ),
        out_shape=[jax.ShapeDtypeStruct(half, BF16)] * 2,
        compiler_params=pltpu.CompilerParams(vmem_limit_bytes=SMALL_VMEM),
        cost_estimate=pl.CostEstimate(
            flops=8 * tok_here * width * size, transcendentals=0, bytes_accessed=12 * tok_here * width
        ),
        name="qkv_grad",
    )(block, *pieces, *normed)


def swap(values, axis, bit):
    size = lax.axis_size(axis)
    return lax.ppermute(values, axis, [(j, j ^ bit) for j in range(size)])


def trade(parts, axis):
    return [parts[0]] + [swap(part, axis, i) for i, part in enumerate(parts) if i]


def spread(values, axis, count):
    return [values] + [swap(values, axis, i) for i in range(1, count)]


def total_of(parts):
    total = parts[0].astype(F32)
    for part in parts[1:]:
        total = total + part.astype(F32)
    return total


def after(values, *others):
    return lax.optimization_barrier((values, *others))[0]


def deal_kernel(bits_ref, *refs, steps):
    keep, got, (outgoing, staying) = refs[: steps + 2], refs[steps + 2 : 2 * steps + 4], refs[-2:]
    gate = bits_ref[0]
    for out, side in ((outgoing, 1 - gate), (staying, gate)):
        at = 0
        for left, right in zip(keep, got):
            rows = left.shape[2] // 2
            here = pl.ds(pl.multiple_of(side * rows, rows), rows)
            total = left[0, 0, here, :].astype(F32) + right[0, 0, here, :].astype(F32)
            out[0, at : at + rows, :] = total.astype(BF16)
            at += rows


def deal(gate, keep, got, dp):
    slots, width, lanes = keep.shape
    steps = slots // 2 - 1
    up_each, each = width * steps // dp, width // dp
    per_slot = width // up_each
    up = pl.BlockSpec(
        (1, 1, up_each, lanes),
        lambda i, b: (2 * (i // per_slot), i % per_slot, 0, 0),
    )
    rest = [
        pl.BlockSpec((1, 1, each, lanes), lambda i, b, slot=slot: (slot, i, 0, 0))
        for slot in [2 * k + 1 for k in range(steps)] + [2 * steps]
    ]
    views = lambda array: [array.reshape(slots, per_slot, up_each, lanes)] + [
        array.reshape(slots, dp, each, lanes)
    ] * (steps + 1)
    rows = up_each // 2 + (steps + 1) * each // 2
    shape = jax.ShapeDtypeStruct((dp, rows, lanes), BF16)
    return pl.pallas_call(
        partial(deal_kernel, steps=steps),
        grid_spec=pltpu.PrefetchScalarGridSpec(
            num_scalar_prefetch=1,
            grid=(dp,),
            in_specs=([up] + rest) * 2,
            out_specs=[pl.BlockSpec((1, rows, lanes), lambda i, b: (i, 0, 0))] * 2,
        ),
        out_shape=[shape, shape],
        cost_estimate=pl.CostEstimate(flops=keep.size, transcendentals=0, bytes_accessed=6 * keep.size),
        name="deal",
    )(gate, *views(keep), *views(got))


def undeal_kernel(place_ref, *refs, sources, steps, each):
    shares, (up, down, out, store) = refs[:sources], refs[sources:]
    lanes = store.shape[2]
    for j, share in enumerate(shares):
        store[place_ref[0] ^ j] = share[...].astype(F32)
    wide = steps * each
    for low in range(2):
        both = lambda at, size: jnp.concatenate([store[low, at : at + size], store[2 + low, at : at + size]], 0).T
        up[low * lanes : (low + 1) * lanes, :] = both(0, wide)
        for k in range(steps):
            at = (2 * k + low) * lanes
            down[at : at + lanes, :] = both(wide + k * each, each)
        out[low * lanes : (low + 1) * lanes, :] = both(2 * wide, each)


def undeal(place, shares, steps, width, dp):
    rows, lanes = shares[0].shape
    shapes = [(width, width * steps // dp), (width * steps, width // dp), (width, width // dp)]
    return pl.pallas_call(
        partial(undeal_kernel, sources=len(shares), steps=steps, each=width // dp // 2),
        grid_spec=pltpu.PrefetchScalarGridSpec(
            num_scalar_prefetch=1,
            grid=(1,),
            in_specs=[whole(rows, lanes)] * len(shares),
            out_specs=[whole(*shape) for shape in shapes],
            scratch_shapes=[pltpu.VMEM((len(shares), rows, lanes), F32)],
        ),
        out_shape=[jax.ShapeDtypeStruct(shape, F32) for shape in shapes],
        cost_estimate=pl.CostEstimate(flops=0, transcendentals=0, bytes_accessed=24 * rows * lanes),
        name="undeal",
    )(place, *shares)


def turn_kernel(*refs):
    *parts, out = refs
    half = len(parts) // 2
    at = 0
    for kept, got in zip(parts[:half], parts[half:]):
        total = (kept[0].astype(F32) + got[...].astype(F32)).T.astype(BF16)
        out[at : at + total.shape[0], :] = total
        at += total.shape[0]


def turn(kept, got):
    columns, rows = sum(part.shape[1] for part in got), got[0].shape[0]
    return pl.pallas_call(
        turn_kernel, out_shape=jax.ShapeDtypeStruct((columns, rows), BF16), name="turn"
    )(*kept, *got)


def regroup_kernel(place_ref, *refs, rounds):
    *shares, out = refs
    sources = len(shares)
    for j, share in enumerate(shares):
        for r in range(rounds):
            for p in range(3):
                at = ((p * sources + (place_ref[0] ^ j)) * rounds + r) * HEAD_DIM
                start = (r * 3 + p) * HEAD_DIM
                out[pl.ds(pl.multiple_of(at, HEAD_DIM), HEAD_DIM), :] = share[start : start + HEAD_DIM]


def regroup(place, shares, rounds):
    columns, rows = shares[0].shape
    total = columns * len(shares)
    return pl.pallas_call(
        partial(regroup_kernel, rounds=rounds),
        grid_spec=pltpu.PrefetchScalarGridSpec(
            num_scalar_prefetch=1,
            grid=(1,),
            in_specs=[whole(columns, rows)] * len(shares),
            out_specs=whole(total, rows),
        ),
        out_shape=jax.ShapeDtypeStruct((total, rows), BF16),
        name="regroup",
    )(place, *shares)


def stack_kernel(parts, out):
    rows = parts.shape[2]
    for index in range(parts.shape[0]):
        out[index * rows : (index + 1) * rows, :] = parts[index].astype(F32).T


def stack_rows(parts):
    count, columns, rows = parts.shape
    return pl.pallas_call(
        stack_kernel, out_shape=jax.ShapeDtypeStruct((rows * count, columns), F32), name="stack_rows"
    )(parts)


def exchange(values, axis):
    return lax.all_to_all(values, axis, split_axis=0, concat_axis=0, tiled=True)


def wide_sums(slots, place, dp):
    steps, width, lanes = slots.shape[0] // 2 - 1, slots.shape[1], slots.shape[2]
    pairs = slots.reshape(steps + 1, 2, width, lanes)
    up = pairs[:steps, 0].reshape(dp, 2, -1, lanes)
    down = pairs[:steps, 1].reshape(steps, dp, 2, -1, lanes)
    down = jnp.moveaxis(down, 0, 2).reshape(dp, 2, -1, lanes)
    out = pairs[steps, 0].reshape(dp, 2, -1, lanes)
    dealt = jnp.concatenate([up, down, out], 2)
    gate = place // 2
    pick = lambda index: lax.dynamic_index_in_dim(dealt, index, 1, keepdims=False)
    half_sum = total_of([pick(gate), swap(pick(1 - gate), "seq", 2)]).astype(BF16)
    share = jnp.sum(exchange(half_sum, "dp").astype(F32), 0).astype(BF16)
    shares = lax.all_gather(share, "seq", axis=0).reshape(2, 2, -1, lanes).astype(F32)
    each = width // dp // 2
    up, down, out = jnp.split(shares, [steps * each, 2 * steps * each], 2)
    turned = lambda part: jnp.transpose(part, (1, 3, 0, 2)).reshape(2 * lanes, -1)
    down = down.reshape(2, 2, steps, each, lanes)
    down = jnp.transpose(down, (2, 1, 4, 0, 3)).reshape(steps * 2 * lanes, 2 * each)
    return turned(up), down, turned(out)


def wide_columns(grads, dp, sources, rounds):
    grad = jnp.concatenate(grads, 2).reshape(-1, 3 * HEAD_DIM * rounds)
    width, columns = grad.shape
    rows = width // dp
    summed = jnp.sum(exchange(grad.reshape(dp, rows, columns), "dp").astype(F32), 0).astype(BF16)
    gathered = lax.all_gather(summed, "seq", axis=0).reshape(sources, rows, rounds, 3, HEAD_DIM)
    ordered = jnp.transpose(gathered, (1, 3, 0, 2, 4)).reshape(rows, dp, -1)
    return exchange(jnp.swapaxes(ordered, 0, 1), "dp").reshape(width, -1).astype(F32)


def on_device(
    tokens,
    time_steps,
    data_group,
    cotangent,
    attn_norm_gain,
    attn_norm_bias,
    qkv_weight,
    query_bias,
    value_bias,
    out_weight,
    out_bias,
    mlp_norm_gain,
    mlp_norm_bias,
    up_weight,
    up_bias,
    down_weight,
    down_bias,
    time_table,
):
    sources, dp = lax.axis_size("seq"), lax.axis_size("dp")
    place, block = lax.axis_index("seq"), lax.axis_index("dp")
    tokens, cotangent = tokens[0], cotangent[0]
    tok_here, width = tokens.shape
    hidden_units = up_weight.shape[1]
    rounds = HEADS // sources
    is_short = data_group[0] == 0
    short_flag = is_short.astype(jnp.int32)[None]
    rows = time_table[jnp.where(is_short, time_steps[0], time_steps[0, 0])].astype(F32)
    flat = lambda vector: vector.astype(F32)[None]
    qkv_bias = jnp.concatenate([query_bias, jnp.zeros_like(query_bias), value_bias]).astype(F32)

    place_arg = place.astype(jnp.int32)[None]
    block_arg = block.astype(jnp.int32)[None]
    few = dp <= 8

    normed, sending = project(
        place_arg,
        tokens,
        rows,
        flat(attn_norm_gain),
        flat(attn_norm_bias),
        qkv_weight,
        qkv_bias[:, None],
        sources,
        rounds,
    )
    heads, mixed, logs, sent = [trade(sending[0], "seq")], [], [], []
    returned = []
    for r in range(rounds):
        if r + 1 < rounds:
            ahead = sending[r + 1] if r < 1 else after(sending[r + 1], logs[r - 1])
            heads.append(trade(ahead, "seq"))
        out, full, log = attend(short_flag, heads[r], sent[0] if r == 1 else ())
        mixed.append(full)
        logs.append(log)
        sent.append(out)
        if r >= 1:
            returned.append(trade(out, "seq"))

    across = swap(after(normed, log), "seq", 2)
    groups = (((0, 1), (2,)), ((0,), (1, 2)))
    result, g_resid, sent_grads, (send, keep, vectors, g_up_b) = mlp(
        place_arg,
        groups,
        returned,
        tokens,
        rows,
        cotangent,
        out_weight,
        flat(out_bias),
        flat(mlp_norm_gain),
        flat(mlp_norm_bias),
        up_weight,
        flat(up_bias),
        down_weight,
        flat(down_bias),
    )
    got = swap(send, "seq", 1)
    first_grads = trade(sent_grads[0], "seq")
    if few:
        outgoing, staying = deal(place_arg // 2, keep, got, dp)
        got = swap(outgoing, "seq", 2)
        ready = outgoing
    else:
        ready = summed = total_of([keep, got]).astype(BF16)
    rest_grads = trade(sent_grads[1], "seq")
    beside = [normed, swap(normed, "seq", 1), across, swap(across, "seq", 1)]
    held = after(heads[0], ready)
    grads = [attend_back(short_flag, held, mixed[0], first_grads, logs[0], 0)]
    back = [trade(grads[0], "seq")]
    grads.append(attend_back(short_flag, heads[1], mixed[1], rest_grads, logs[1], 0))
    back.append(trade(grads[1], "seq"))
    order = (0, 4, 2, 6, 1, 5, 3, 7) if few else (0, 1)
    stay_a, away_a = qkv_grad(block_arg, grads, beside, order)
    if few:
        got_a = swap(away_a, "dp", 1)
        half_sum = total_of([staying, after(got, grads[1])]).astype(BF16)
        dealt = exchange(half_sum, "dp")
        ready = half_sum
    held = after(heads[2], stay_a, ready, *back[0])
    grads.append(attend_back(short_flag, held, mixed[2], rest_grads, logs[2], 1))
    back.append(trade(grads[2], "seq"))
    grads[2] = after(grads[2], *back[1])
    stay_b, away_b = qkv_grad(block_arg, grads[2:], beside, order)
    if few:
        parts = [stay_a, stay_b], [after(got_a, grads[2]), swap(away_b, "dp", 1)]
        for bit in (2, 4):
            kept = [total_of(pair).astype(BF16) for pair in zip(*parts)]
            size = kept[0].shape[0] // 2
            parts = [part[:size] for part in kept], [swap(part[size:], "dp", bit) for part in kept]
        summed = turn(parts[0], [part[0] for part in parts[1]])
        columns = regroup(place_arg, spread(summed, "seq", sources), rounds)

    flags = jnp.concatenate([place_arg, short_flag])
    g_tokens, small = finish(
        flags, back, qkv_weight, tokens, rows, flat(attn_norm_gain), g_resid, vectors, g_up_b
    )
    for bit in (1, 2):
        small = small + swap(small, "seq", bit)
    by_block = (jnp.arange(dp) == block)[:, None]
    row_slot = jnp.where(by_block[:, :, None], small[None, 14:], 0.0).reshape(-1, width)
    small = jnp.concatenate([small[:14], row_slot])
    steps = jnp.where(by_block, time_steps.astype(F32), 0.0)
    bit = 1
    while bit < dp:
        small = small + swap(small, "dp", bit)
        steps = steps + swap(steps, "dp", bit)
        bit *= 2
    if few:
        share = total_of([dealt[i] for i in range(dp)]).astype(BF16)
        shares = spread(share, "seq", sources)
        sum_up, sum_down, sum_out = undeal(place_arg, shares, hidden_units // width, width, dp)
        sum_qkv = stack_rows(exchange(columns.reshape(dp, 3 * width // dp, width // dp), "dp"))
    else:
        sum_up, sum_down, sum_out = wide_sums(summed, place, dp)
        sum_qkv = wide_columns(
            [jnp.stack(pair).reshape(2, width // 2, -1) for pair in ((stay_a, away_a), (stay_b, away_b))],
            dp,
            sources,
            rounds,
        )
    share_cols = width // dp
    rows_mine = lax.dynamic_slice_in_dim(small[14:], block * share_cols, share_cols, 1)
    table_rows = time_table.shape[0]
    hits = jnp.arange(table_rows, dtype=jnp.int32)[:, None] == steps.reshape(1, -1).astype(jnp.int32)
    sum_table = jnp.dot(hits.astype(F32), rows_mine, precision=lax.Precision.HIGHEST)
    return (
        result[None],
        g_tokens[None],
        small[0],
        small[1],
        sum_qkv,
        small[10],
        small[12],
        sum_out,
        small[4],
        small[2],
        small[3],
        sum_up,
        small[6:10].reshape(-1),
        sum_down,
        small[5],
        sum_table,
    )


def solution(mesh):
    placed = (P("dp", "seq", None), P("dp", None), P("dp"), P("dp", "seq", None)) + (P(),) * 14
    column = P(None, "dp")
    return jax.shard_map(
        on_device,
        mesh=mesh,
        in_specs=placed,
        out_specs=(
            P("dp", "seq", None),
            P("dp", "seq", None),
            P(),
            P(),
            column,
            P(),
            P(),
            column,
            P(),
            P(),
            P(),
            column,
            P(),
            column,
            P(),
            column,
        ),
        check_vma=False,
    )
```

time: 687 us -> 487 us (0.71)
  matrix products: 112 us -> 1.29 us
  Pallas kernels: 203 us -> 313 us
  other arithmetic: 61.4 us -> 9.1 us
  local copies, waits for them, and re-layouts: 87.5 us -> 35.4 us
  starting transfers between devices: 93.4 us -> 52.3 us
  blocking collectives: 37.2 us -> 0 us
  waiting for transfers between devices: 79 us -> 64.8 us
    dot_general x13 -> x1, matrix products: 112 us -> 1.29 us  [on_device(): jnp.dot(hits.astype(F32), rows_mine, precision=lax.Precision.HIGHEST)]
    pallas_call x6 -> x16, Pallas kernels: 203 us -> 313 us  [the longest x3 132 us: attend_back(): pl.pallas_call(partial(attend_back_kernel, sources=sources, segment=segme...]
    all_to_all x16 -> x2, starting transfers between devices: 73.6 us -> 11.6 us  [exchange(): return lax.all_to_all(values, axis, split_axis=0, concat_axis=0, tiled=True)]
    all_gather x4 -> x0, blocking collectives: 37.2 us -> none  [reduce_columns(): return lax.all_gather(share, 'seq', axis=0, tiled=True).astype(F32)]
    all_to_all x16 -> x2, waiting for transfers between devices: 37 us -> 6.59 us  [exchange(): return lax.all_to_all(values, axis, split_axis=0, concat_axis=0, tiled=True)]
    reduce_sum x12 -> x0, other arithmetic: 21.3 us -> none  [the longest x4 7.85 us: reduce_columns(): share = jnp.sum(parts.astype(F32), 0).astype(BF16)]
    ppermute x18 -> x55, starting transfers between devices: 19.8 us -> 40.7 us  [swap(): return lax.ppermute(values, axis, [(j, j ^ bit) for j in range(size)])]
    unnamed x169 -> x167, local copies, waits for them, and re-layouts: 45.1 us -> 25.9 us
  transfers between devices with their start and end apart: 34 -> 57, of which waited for: 9 -> 19; matrix products, arithmetic and copies ran while one was open for 19% -> 4% of each run, Pallas kernels for 30% -> 52%
where the time goes in v2:
time: 487 us; the launch traced here: 478 us
  Pallas kernels  313 us (64%)
  waiting for transfers between devices  64.8 us (13%)
  starting transfers between devices  52.3 us (11%)
  local copies, waits for them, and re-layouts  35.4 us (7%)
  other arithmetic  9.1 us (2%)
    pallas_call x3, Pallas kernels, attend_back(): pl.pallas_call(partial(attend_back_kernel, sources=sources, segment=segme...  132 us
    pallas_call x3, Pallas kernels, attend(): pl.pallas_call(partial(attend_kernel, sources=sources, segment=segment, h...  73.1 us
    ppermute x55, waiting for transfers between devices, swap(): return lax.ppermute(values, axis, [(j, j ^ bit) for j in range(size)])  58.2 us
    pallas_call x1, Pallas kernels, mlp(): pl.pallas_call(partial(mlp_kernel, groups=groups, sources=sources, block=...  53.8 us
    ppermute x55, starting transfers between devices, swap(): return lax.ppermute(values, axis, [(j, j ^ bit) for j in range(size)])  40.7 us
    unnamed x167, local copies, waits for them, and re-layouts  25.9 us
    pallas_call x1, Pallas kernels, finish(): pl.pallas_call(partial(finish_kernel, rounds=rounds, sources=sources, blo...  17 us
    all_to_all x2, starting transfers between devices, exchange(): return lax.all_to_all(values, axis, split_axis=0, concat_axis=0, tiled=True)  11.6 us
  transfers between devices with their start and end apart: 57, of which 19 were waited for; matrix products, arithmetic and copies ran while one was open for 4% of the time, Pallas kernels for 52%

profile of v2, /device:TPU:0, one launch (start us, length us, event | category | flops | bytes accessed | tf_op | source)
XLA Modules:
  0.0 478.4 jit_solution(17777462757609810500)
XLA Ops:
  9.3 7.7 %project.1 = (bf16[1024,768]{1,0:T(8,128)(2,1)S(1)}, bf16[3,64,1024]{2,1,0:T(8,128)(2,1)S(1)}, bf16[3,64,1024]{2,1,0:T(8,128)(2,1)S(1)}, bf16[3,64,1024]{2,1,0:T...) custom-call(s32[1]{0:T(128)} %bitcast.place_ref, ...), custom_call_target="tpu_custom_call" | custom-call | flops 3623878656 | bytes 7077888 | tf_op jit(solution)/shard_map/project/pallas_call | solution.py:296
  22.3 7.8 %collective-permute-done.4.refs_2_ = bf16[3,64,1024]{2,1,0:T(8,128)(2,1)S(1)} collective-permute-done((bf16[3,64,1024]{2,1,0:T(8,128)(2,1)S(1)}, bf16[3,64,1024]{2,1,0:T(8,128)(2,1)S(1)}, u32[]{:S(2)}, u32[]{:S(2)}) %collective-permute-start.4) | collective-permute-done | bytes 393248 | tf_op jit(solution)/shard_map/ppermute | solution.py:649
  30.1 7.9 %collective-permute-done.5.refs_3_ = bf16[3,64,1024]{2,1,0:T(8,128)(2,1)S(1)} collective-permute-done((bf16[3,64,1024]{2,1,0:T(8,128)(2,1)S(1)}, bf16[3,64,1024]{2,1,0:T(8,128)(2,1)S(1)}, u32[]{:S(2)}, u32[]{:S(2)}) %collective-permute-start.5) | collective-permute-done | bytes 393248 | tf_op jit(solution)/shard_map/ppermute | solution.py:649
  38.0 24.3 %attend.3 = (bf16[1,64,1024]{2,1,0:T(8,128)(2,1)S(1)}, bf16[1,64,1024]{2,1,0:T(8,128)(2,1)S(1)}, bf16[1,64,1024]{2,1,0:T(8,128)(2,1)S(1)}, bf16[1,64,1024]{2,1,0...) custom-call(s32[1]{0:T(128)S(6)} %broadcast_in_dim.110.short_ref, ...), custom_call_target="tpu_custom_call" | custom-call | flops 17179869184 | bytes 4194304 | tf_op jit(solution)/shard_map/attend/pallas_call | solution.py:116
  65.1 24.3 %attend.4 = (bf16[2,64,1024]{2,1,0:T(8,128)(2,1)S(1)}, bf16[2,64,1024]{2,1,0:T(8,128)(2,1)S(1)}, bf16[2,64,1024]{2,1,0:T(8,128)(2,1)S(1)}, bf16[2,64,1024]{2,1,0...) custom-call(s32[1]{0:T(128)S(6)} %broadcast_in_dim.110.short_ref, ...), custom_call_target="tpu_custom_call" | custom-call | flops 17179869184 | bytes 4194304 | tf_op jit(solution)/shard_map/attend/pallas_call | solution.py:116
  91.7 24.5 %attend.5 = (bf16[1,64,1024]{2,1,0:T(8,128)(2,1)S(1)}, bf16[1,64,1024]{2,1,0:T(8,128)(2,1)S(1)}, bf16[1,64,1024]{2,1,0:T(8,128)(2,1)S(1)}, bf16[1,64,1024]{2,1,0...) custom-call(s32[1]{0:T(128)S(6)} %broadcast_in_dim.110.short_ref, ...), custom_call_target="tpu_custom_call" | custom-call | flops 17179869184 | bytes 4194304 | tf_op jit(solution)/shard_map/attend/pallas_call | solution.py:116
  126.5 53.8 %mlp.1 = (bf16[1024,768]{1,0:T(8,128)(2,1)}, f32[1024,768]{1,0:T(8,128)}, bf16[1,64,1024]{2,1,0:T(8,128)(2,1)}, bf16[1,64,1024]{2,1,0:T(8,128)(2,1)}, bf16[1,64,...) custom-call(s32[1]{0:T(128)} %bitcast.place_ref, ...), custom_call_target="tpu_custom_call" | custom-call | flops 28991029248 | bytes 18874368 | tf_op jit(solution)/shard_map/mlp/pallas_call | solution.py:441
  185.4 3.6 collective-permute-done.22.refs_5_
  197.3 44.4 %attend_back.4 = (bf16[3,64,1024]{2,1,0:T(8,128)(2,1)}, bf16[3,64,1024]{2,1,0:T(8,128)(2,1)}, bf16[3,64,1024]{2,1,0:T(8,128)(2,1)}, bf16[3,64,1024]{2,1,0:T(8,128)(2,1)}) custom-call(s32[1]{0:T(128)S(6)} %broadcast_in_dim.110.short_ref, bf16[3,64,1024]{2,1,0:T(8,128)(2,1)} %copy-done.42, bf16[3,64,1024]{2,1,0:T(8,128)(2,1)} %copy-done.28, ...), custom_call_target="tpu_custom_call" | custom-call | flops 42949672960 | bytes 10485760 | tf_op jit(solution)/shard_map/attend_back/pallas_call | solution.py:219
  241.7 8.4 %deal.1 = (bf16[8,432,384]{2,1,0:T(8,128)(2,1)}, bf16[8,432,384]{2,1,0:T(8,128)(2,1)}) custom-call(s32[1]{0:T(128)S(6)} %select_n.49.bits_ref, bf16[10,2,384,384]{3,2,1,0:T(8,128)(2,1)} %bitcast.33, bf16[10,8,96,384]{3,2,1,0:T(8,128)(2,1)} %bitcast.34, bf16[10,8,96,384]{3,2,1,0:T(8,128)(2,1)} %bitcast.35, bf16[10,8,96,384]{3,2,1,0:T(8,128)(2,1)} %bitcast.36, ...), custom_call_target="tpu_custom_call" | custom-call | flops 2949120 | bytes 17694720 | tf_op jit(solution)/shard_map/deal/pallas_call | solution.py:702
  251.3 44.1 %attend_back.3 = (bf16[3,64,1024]{2,1,0:T(8,128)(2,1)}, bf16[3,64,1024]{2,1,0:T(8,128)(2,1)}, bf16[3,64,1024]{2,1,0:T(8,128)(2,1)}, bf16[3,64,1024]{2,1,0:T(8,128)(2,1)}) custom-call(s32[1]{0:T(128)S(6)} %broadcast_in_dim.110.short_ref, bf16[3,64,1024]{2,1,0:T(8,128)(2,1)} %copy-done.41, bf16[3,64,1024]{2,1,0:T(8,128)(2,1)} %copy-done.25, ...), custom_call_target="tpu_custom_call" | custom-call | flops 42949672960 | bytes 10485760 | tf_op jit(solution)/shard_map/attend_back/pallas_call | solution.py:219
  300.2 6.5 %qkv_grad.2 = (bf16[4,96,384]{2,1,0:T(8,128)(2,1)S(1)}, bf16[4,96,384]{2,1,0:T(8,128)(2,1)}) custom-call(s32[1]{0:T(128)} %bitcast.13.block_ref, bf16[3,64,1024]{2,1,0:T(8,128)(2,1)S(1)} %copy-done.3, bf16[3,64,1024]{2,1,0:T(8,128)(2,1)S(1)} %copy-done.11, bf16[3,64,1024]{2,1,0:T(8,128)(2,1)S(1)} %copy-done.10, ...), custom_call_target="tpu_custom_call" | custom-call | flops 2415919104 | bytes 9437184 | tf_op jit(solution)/shard_map/qkv_grad/pallas_call | solution.py:629
  307.4 4.2 collective-permute-done.31
  311.6 4.0 add_convert_fusion
  315.6 6.5 %all-to-all-start.1 = ((bf16[8,432,384]{2,1,0:T(8,128)(2,1)}), bf16[8,432,384]{2,1,0:T(8,128)(2,1)}, u32[]{:S(2)}, u32[]{:S(2)}) async-start(bf16[8,432,384]{2,1,0:T(8,128)(2,1)} %add_convert_fusion), calls=%async_computation.1 | async-start | bytes 5308416 | tf_op jit(solution)/shard_map/all_to_all | solution.py:807
  329.5 43.9 %attend_back.5 = (bf16[3,64,1024]{2,1,0:T(8,128)(2,1)}, bf16[3,64,1024]{2,1,0:T(8,128)(2,1)}, bf16[3,64,1024]{2,1,0:T(8,128)(2,1)}, bf16[3,64,1024]{2,1,0:T(8,128)(2,1)}) custom-call(s32[1]{0:T(128)S(6)} %broadcast_in_dim.110.short_ref, bf16[3,64,1024]{2,1,0:T(8,128)(2,1)} %copy-done.40, bf16[3,64,1024]{2,1,0:T(8,128)(2,1)} %copy-done.24, ...), custom_call_target="tpu_custom_call" | custom-call | flops 42949672960 | bytes 10485760 | tf_op jit(solution)/shard_map/attend_back/pallas_call | solution.py:219
  380.4 4.0 qkv_grad.3
  385.8 6.3 %collective-permute-done.42 = bf16[4,96,192]{2,1,0:T(8,128)(2,1)S(1)} collective-permute-done((bf16[4,96,192]{2,1,0:T(8,128)(2,1)S(1)}, bf16[4,96,192]{2,1,0:T(8,128)(2,1)S(1)}, u32[]{:S(2)}, u32[]{:S(2)}) %collective-permute-start.42) | collective-permute-done | bytes 147488 | tf_op jit(solution)/shard_map/ppermute | solution.py:649
  392.1 5.5 %collective-permute-done.41 = bf16[2,96,384]{2,1,0:T(8,128)(2,1)S(1)} collective-permute-done((bf16[2,96,384]{2,1,0:T(8,128)(2,1)S(1)}, bf16[2,96,384]{2,1,0:T(8,128)(2,1)S(1)}, u32[]{:S(2)}, u32[]{:S(2)}) %collective-permute-start.41) | collective-permute-done | bytes 147488 | tf_op jit(solution)/shard_map/ppermute | solution.py:649
  398.6 3.9 collective-permute-start.44
  402.6 17.0 %finish.1 = (bf16[1024,768]{1,0:T(8,128)(2,1)}, f32[16,768]{1,0:T(8,128)S(1)}) custom-call(s32[2]{0:T(128)S(1)} %pad_add_fusion.place_ref, bf16[3,64,1024]{2,1,0:T(8,128)(2,1)S(1)} %copy-done.4, bf16[3,64,1024]{2,1,0:T(8,128)(2,1)S(1)} %copy-done.32, bf16[3,64,1024]{2,1,0:T(8,128)(2,1)S(1)} %copy-done.34, bf16[3,64,1024]{2,1,0:T(8,128)(2,1)S(1)} %copy-done.36, ...), custom_call_target="tpu_custom_call" | custom-call | flops 3623878656 | bytes 14155776 | tf_op jit(solution)/shard_map/finish/pallas_call | solution.py:572
  441.9 5.1 %all-to-all-start = ((bf16[8,288,96]{2,1,0:T(8,128)(2,1)}), bf16[8,288,96]{2,1,0:T(8,128)(2,1)S(1)}, u32[]{:S(2)}, u32[]{:S(2)}) async-start(bf16[8,288,96]{2,1,0:T(8,128)(2,1)} %bitcast.39), calls=%async_computation | async-start | bytes 1179648 | tf_op jit(solution)/shard_map/all_to_all | solution.py:807
  456.4 6.6 %all-to-all-done.parts = bf16[8,288,96]{2,1,0:T(8,128)(2,1)S(1)} async-done(((bf16[8,288,96]{2,1,0:T(8,128)(2,1)}), bf16[8,288,96]{2,1,0:T(8,128)(2,1)S(1)}, u32[]{:S(2)}, u32[]{:S(2)}) %all-to-all-start) | async-done | bytes 442400 | tf_op jit(solution)/shard_map/all_to_all | solution.py:807
  470.4 3.8 undeal.1
  (325 shorter events, 107.6 us)
Async XLA Ops:
  20.2 44.6 %collective-permute-start = (bf16[3,64,1024]{2,1,0:T(8,128)(2,1)S(1)}, bf16[3,64,1024]{2,1,0:T(8,128)(2,1)S(1)}, u32[]{:S(2)}, u32[]{:S(2)}) collective-permute-start(bf16[3,64,1024]{2,1,0:T(8,128)(2,1)S(1)} %get-tuple-element.104), channel_id=1, source_target_pairs={{0,1},{1,0},{2,3},{3,2},{4,5},{5,4},{6,7},{7,6},{8,9},{9,8},{10,11... | collective-permute-start | bytes 1179656 | tf_op jit(solution)/shard_map/ppermute | solution.py:649
  20.3 44.7 %collective-permute-start.1 = (bf16[3,64,1024]{2,1,0:T(8,128)(2,1)S(1)}, bf16[3,64,1024]{2,1,0:T(8,128)(2,1)S(1)}, u32[]{:S(2)}, u32[]{:S(2)}) collective-permute-start(bf16[3,64,1024]{2,1,0:T(8,128)(2,1)S(1)} %get-tuple-element.105), channel_id=1, source_target_pairs={{0,2},{1,3},{2,0},{3,1},{4,6},{5,7},{6,4},{7,5},{8,10},{9,11},{10,... | collective-permute-start | bytes 1179656 | tf_op jit(solution)/shard_map/ppermute | solution.py:649
  22.3 42.8 %collective-permute-start.2 = (bf16[3,64,1024]{2,1,0:T(8,128)(2,1)S(1)}, bf16[3,64,1024]{2,1,0:T(8,128)(2,1)S(1)}, u32[]{:S(2)}, u32[]{:S(2)}) collective-permute-start(bf16[3,64,1024]{2,1,0:T(8,128)(2,1)S(1)} %get-tuple-element.106), channel_id=1, source_target_pairs={{0,3},{1,2},{2,1},{3,0},{4,7},{5,6},{6,5},{7,4},{8,11},{9,10},{10,... | collective-permute-start | bytes 1179656 | tf_op jit(solution)/shard_map/ppermute | solution.py:649
  62.9 28.7 %collective-permute-start.10 = (bf16[3,64,1024]{2,1,0:T(8,128)(2,1)S(1)}, bf16[3,64,1024]{2,1,0:T(8,128)(2,1)S(1)}, u32[]{:S(2)}, u32[]{:S(2)}) collective-permute-start(bf16[3,64,1024]{2,1,0:T(8,128)(2,1)S(1)} %get-tuple-element.126), channel_id=1, source_target_pairs={{0,2},{1,3},{2,0},{3,1},{4,6},{5,7},{6,4},{7,5},{8,10},{9,11},{10,... | collective-permute-start | bytes 1179656 | tf_op jit(solution)/shard_map/ppermute | solution.py:649
  89.5 30.6 %collective-permute-start.6 = (bf16[2,64,1024]{2,1,0:T(8,128)(2,1)S(1)}, bf16[2,64,1024]{2,1,0:T(8,128)(2,1)S(1)}, u32[]{:S(2)}, u32[]{:S(2)}) collective-permute-start(bf16[2,64,1024]{2,1,0:T(8,128)(2,1)S(1)} %get-tuple-element.116), channel_id=1, source_target_pairs={{0,1},{1,0},{2,3},{3,2},{4,5},{5,4},{6,7},{7,6},{8,9},{9,8},{10,11... | collective-permute-start | bytes 786440 | tf_op jit(solution)/shard_map/ppermute | solution.py:649
  89.8 33.2 %collective-permute-start.7 = (bf16[2,64,1024]{2,1,0:T(8,128)(2,1)S(1)}, bf16[2,64,1024]{2,1,0:T(8,128)(2,1)S(1)}, u32[]{:S(2)}, u32[]{:S(2)}) collective-permute-start(bf16[2,64,1024]{2,1,0:T(8,128)(2,1)S(1)} %get-tuple-element.117), channel_id=1, source_target_pairs={{0,2},{1,3},{2,0},{3,1},{4,6},{5,7},{6,4},{7,5},{8,10},{9,11},{10,... | collective-permute-start | bytes 786440 | tf_op jit(solution)/shard_map/ppermute | solution.py:649
  91.6 31.5 %collective-permute-start.8 = (bf16[2,64,1024]{2,1,0:T(8,128)(2,1)S(1)}, bf16[2,64,1024]{2,1,0:T(8,128)(2,1)S(1)}, u32[]{:S(2)}, u32[]{:S(2)}) collective-permute-start(bf16[2,64,1024]{2,1,0:T(8,128)(2,1)S(1)} %get-tuple-element.118), channel_id=1, source_target_pairs={{0,3},{1,2},{2,1},{3,0},{4,7},{5,6},{6,5},{7,4},{8,11},{9,10},{10,... | collective-permute-start | bytes 786440 | tf_op jit(solution)/shard_map/ppermute | solution.py:649
  180.3 61.4 %collective-permute-start.15 = (bf16[10,768,384]{2,1,0:T(8,128)(2,1)}, bf16[10,768,384]{2,1,0:T(8,128)(2,1)}, u32[]{:S(2)}, u32[]{:S(2)}) collective-permute-start(bf16[10,768,384]{2,1,0:T(8,128)(2,1)} %get-tuple-element.134), channel_id=1, source_target_pairs={{0,1},{1,0},{2,3},{3,2},{4,5},{5,4},{6,7},{7,6},{8,9},{9,8},{10,11... | collective-permute-start | bytes 17694728 | tf_op jit(solution)/shard_map/ppermute | solution.py:649
  183.8 67.0 %collective-permute-start.29 = (bf16[1024,768]{1,0:T(8,128)(2,1)S(1)}, bf16[1024,768]{1,0:T(8,128)(2,1)}, u32[]{:S(2)}, u32[]{:S(2)}) collective-permute-start(bf16[1024,768]{1,0:T(8,128)(2,1)S(1)} %get-tuple-element.161.refs_8_.refs_4_), channel_id=1, source_target_pairs={{0,2},{1,3},{2,0},{3,1},{4,6},{5,7},{6,4},{7,5},{8,10},{9,11},{10,... | collective-permute-start | bytes 4718600 | tf_op jit(solution)/shard_map/ppermute | solution.py:649
  189.0 61.2 %collective-permute-start.16 = (bf16[1,64,1024]{2,1,0:T(8,128)(2,1)}, bf16[1,64,1024]{2,1,0:T(8,128)(2,1)S(1)}, u32[]{:S(2)}, u32[]{:S(2)}) collective-permute-start(bf16[1,64,1024]{2,1,0:T(8,128)(2,1)} %get-tuple-element.141), channel_id=1, source_target_pairs={{0,1},{1,0},{2,3},{3,2},{4,5},{5,4},{6,7},{7,6},{8,9},{9,8},{10,11... | collective-permute-start | bytes 393224 | tf_op jit(solution)/shard_map/ppermute | solution.py:649
  190.6 59.6 %collective-permute-start.17 = (bf16[1,64,1024]{2,1,0:T(8,128)(2,1)}, bf16[1,64,1024]{2,1,0:T(8,128)(2,1)}, u32[]{:S(2)}, u32[]{:S(2)}) collective-permute-start(bf16[1,64,1024]{2,1,0:T(8,128)(2,1)} %get-tuple-element.142), channel_id=1, source_target_pairs={{0,2},{1,3},{2,0},{3,1},{4,6},{5,7},{6,4},{7,5},{8,10},{9,11},{10,... | collective-permute-start | bytes 393224 | tf_op jit(solution)/shard_map/ppermute | solution.py:649
  195.4 55.5 %collective-permute-start.18 = (bf16[1,64,1024]{2,1,0:T(8,128)(2,1)}, bf16[1,64,1024]{2,1,0:T(8,128)(2,1)}, u32[]{:S(2)}, u32[]{:S(2)}) collective-permute-start(bf16[1,64,1024]{2,1,0:T(8,128)(2,1)} %get-tuple-element.143), channel_id=1, source_target_pairs={{0,3},{1,2},{2,1},{3,0},{4,7},{5,6},{6,5},{7,4},{8,11},{9,10},{10,... | collective-permute-start | bytes 393224 | tf_op jit(solution)/shard_map/ppermute | solution.py:649
  241.7 53.7 %collective-permute-start.28 = (bf16[1024,768]{1,0:T(8,128)(2,1)S(1)}, bf16[1024,768]{1,0:T(8,128)(2,1)}, u32[]{:S(2)}, u32[]{:S(2)}) collective-permute-start(bf16[1024,768]{1,0:T(8,128)(2,1)S(1)} %get-tuple-element.161.refs_8_.refs_4_), channel_id=1, source_target_pairs={{0,1},{1,0},{2,3},{3,2},{4,5},{5,4},{6,7},{7,6},{8,9},{9,8},{10,11... | collective-permute-start | bytes 4718600 | tf_op jit(solution)/shard_map/ppermute | solution.py:649
  250.1 176.6 %collective-permute-start.52 = (f32[8,2]{1,0:T(8,128)S(1)}, f32[8,2]{1,0:T(8,128)S(1)}, u32[]{:S(2)}, u32[]{:S(2)}) collective-permute-start(f32[8,2]{1,0:T(8,128)S(1)} %broadcast_select_fusion.1), channel_id=1, source_target_pairs={{0,4},{4,0},{8,12},{12,8},{16,20},{20,16},{24,28},{28,24},{1,5},{5... | collective-permute-start | bytes 200 | tf_op jit(solution)/shard_map/ppermute | solution.py:649
  250.2 123.2 %collective-permute-start.25 = (bf16[3,64,1024]{2,1,0:T(8,128)(2,1)}, bf16[3,64,1024]{2,1,0:T(8,128)(2,1)}, u32[]{:S(2)}, u32[]{:S(2)}) collective-permute-start(bf16[3,64,1024]{2,1,0:T(8,128)(2,1)} %get-tuple-element.156.refs_5_), channel_id=1, source_target_pairs={{0,1},{1,0},{2,3},{3,2},{4,5},{5,4},{6,7},{7,6},{8,9},{9,8},{10,11... | collective-permute-start | bytes 1179656 | tf_op jit(solution)/shard_map/ppermute | solution.py:649
  250.8 44.8 %collective-permute-start.30 = (bf16[1024,768]{1,0:T(8,128)(2,1)}, bf16[1024,768]{1,0:T(8,128)(2,1)}, u32[]{:S(2)}, u32[]{:S(2)}) collective-permute-start(bf16[1024,768]{1,0:T(8,128)(2,1)} %collective-permute-done.29.refs_10_.refs_6_), channel_id=1, source_target_pairs={{0,1},{1,0},{2,3},{3,2},{4,5},{5,4},{6,7},{7,6},{8,9},{9,8},{10,11... | collective-permute-start | bytes 4718600 | tf_op jit(solution)/shard_map/ppermute | solution.py:649
  250.9 60.7 %collective-permute-start.31 = (bf16[8,432,384]{2,1,0:T(8,128)(2,1)}, bf16[8,432,384]{2,1,0:T(8,128)(2,1)}, u32[]{:S(2)}, u32[]{:S(2)}) collective-permute-start(bf16[8,432,384]{2,1,0:T(8,128)(2,1)} %get-tuple-element.135), channel_id=1, source_target_pairs={{0,2},{1,3},{2,0},{3,1},{4,6},{5,7},{6,4},{7,5},{8,10},{9,11},{10,... | collective-permute-start | bytes 7962632 | tf_op jit(solution)/shard_map/ppermute | solution.py:649
  295.6 27.8 %collective-permute-start.20 = (bf16[3,64,1024]{2,1,0:T(8,128)(2,1)}, bf16[3,64,1024]{2,1,0:T(8,128)(2,1)S(1)}, u32[]{:S(2)}, u32[]{:S(2)}) collective-permute-start(bf16[3,64,1024]{2,1,0:T(8,128)(2,1)} %get-tuple-element.147.refs_2_), channel_id=1, source_target_pairs={{0,2},{1,3},{2,0},{3,1},{4,6},{5,7},{6,4},{7,5},{8,10},{9,11},{10,... | collective-permute-start | bytes 1179656 | tf_op jit(solution)/shard_map/ppermute | solution.py:649
  315.6 126.3 %all-to-all-start.1 = ((bf16[8,432,384]{2,1,0:T(8,128)(2,1)}), bf16[8,432,384]{2,1,0:T(8,128)(2,1)}, u32[]{:S(2)}, u32[]{:S(2)}) async-start(bf16[8,432,384]{2,1,0:T(8,128)(2,1)} %add_convert_fusion), calls=%async_computation.1 | async-start | bytes 5308416 | tf_op jit(solution)/shard_map/all_to_all | solution.py:807
  322.9 52.0 %collective-permute-start.26 = (bf16[3,64,1024]{2,1,0:T(8,128)(2,1)}, bf16[3,64,1024]{2,1,0:T(8,128)(2,1)}, u32[]{:S(2)}, u32[]{:S(2)}) collective-permute-start(bf16[3,64,1024]{2,1,0:T(8,128)(2,1)} %get-tuple-element.157.refs_6_), channel_id=1, source_target_pairs={{0,2},{1,3},{2,0},{3,1},{4,6},{5,7},{6,4},{7,5},{8,10},{9,11},{10,... | collective-permute-start | bytes 1179656 | tf_op jit(solution)/shard_map/ppermute | solution.py:649
  324.2 51.0 %collective-permute-start.27 = (bf16[3,64,1024]{2,1,0:T(8,128)(2,1)}, bf16[3,64,1024]{2,1,0:T(8,128)(2,1)}, u32[]{:S(2)}, u32[]{:S(2)}) collective-permute-start(bf16[3,64,1024]{2,1,0:T(8,128)(2,1)} %get-tuple-element.158.refs_7_), channel_id=1, source_target_pairs={{0,3},{1,2},{2,1},{3,0},{4,7},{5,6},{6,5},{7,4},{8,11},{9,10},{10,... | collective-permute-start | bytes 1179656 | tf_op jit(solution)/shard_map/ppermute | solution.py:649
  328.1 56.3 %collective-permute-start.40 = (bf16[4,96,384]{2,1,0:T(8,128)(2,1)}, bf16[4,96,384]{2,1,0:T(8,128)(2,1)}, u32[]{:S(2)}, u32[]{:S(2)}) collective-permute-start(bf16[4,96,384]{2,1,0:T(8,128)(2,1)} %get-tuple-element.179), channel_id=1, source_target_pairs={{0,4},{4,0},{8,12},{12,8},{16,20},{20,16},{24,28},{28,24},{1,5},{5... | collective-permute-start | bytes 884744 | tf_op jit(solution)/shard_map/ppermute | solution.py:649
  374.9 27.6 %collective-permute-start.33 = (bf16[3,64,1024]{2,1,0:T(8,128)(2,1)}, bf16[3,64,1024]{2,1,0:T(8,128)(2,1)S(1)}, u32[]{:S(2)}, u32[]{:S(2)}) collective-permute-start(bf16[3,64,1024]{2,1,0:T(8,128)(2,1)} %get-tuple-element.182.refs_2_), channel_id=1, source_target_pairs={{0,2},{1,3},{2,0},{3,1},{4,6},{5,7},{6,4},{7,5},{8,10},{9,11},{10,... | collective-permute-start | bytes 1179656 | tf_op jit(solution)/shard_map/ppermute | solution.py:649
  398.6 28.7 %collective-permute-start.44 = (bf16[1,96,384]{2,1,0:T(8,128)(2,1)S(1)}, bf16[1,96,384]{2,1,0:T(8,128)(2,1)S(1)}, u32[]{:S(2)}, u32[]{:S(2)}) collective-permute-start(bf16[1,96,384]{2,1,0:T(8,128)(2,1)S(1)} %get-tuple-element.262), channel_id=1, source_target_pairs={{0,16},{4,20},{8,24},{12,28},{16,0},{20,4},{24,8},{28,12},{1,17},{... | collective-permute-start | bytes 221192 | tf_op jit(solution)/shard_map/ppermute | solution.py:649
  (115 other events, 1629.6 us)

commit v3 on v2

--- a/solution.py
+++ b/solution.py
@@ -44,67 +44,90 @@
         yield chunk, source, slice(part * segment, (part + 1) * segment)
 
 
-def by_length(short_ref, run, chunks):
-    part = pl.program_id(0) % 2
+def over_chunks(short_ref, chunks, body):
     is_short = short_ref[0] != 0
+    part = lax.rem(pl.program_id(0), 2)
 
     @pl.when(is_short)
     def _():
-        run([2 * index + part for index in range(chunks // 2)])
+        body([2 * k + part for k in range(chunks // 2)], True)
 
     @pl.when(jnp.logical_not(is_short))
     def _():
-        run(list(range(chunks)))
+        body(list(range(chunks)), True)
 
 
 def attend_kernel(short_ref, *refs, sources, segment, held):
     heads, refs = refs[:sources], refs[sources:]
     earlier, refs = refs[: sources * held], refs[sources * held :]
     sent, refs = refs[:sources], refs[sources:]
-    mixed_ref, log_ref, queries, keys, values = refs
+    mixed_ref, inverse_ref, weights_ref, queries, keys, values, sums, bounded = refs
     step = pl.program_id(0)
     chunks = 2 * sources
+    depth = HEAD_DIM
 
     @pl.when(step == 0)
     def _():
         for old, new in zip(earlier, sent):
             new[0] = old[0]
+        longest = [jnp.zeros((1, segment), F32)] * 2
         for chunk, source, cols in halves(sources, segment):
             scaled = heads[source][0, :, cols].astype(F32) * (SCALE * LOG2E)
             high, low = split_low(scaled, 2)
             queries[chunk, 0:64, :] = high
             queries[chunk, 64:128, :] = low
+            queries[chunk, 128:144, :] = jnp.zeros((16, segment), BF16)
             key = heads[source][1, :, cols]
             keys[chunk, 0:64, :] = key
             keys[chunk, 64:128, :] = key
+            keys[chunk, 128:144, :] = jnp.full((16, segment), -1.0, BF16)
             values[chunk, 0:64, :] = heads[source][2, :, cols]
             values[chunk, 64:80, :] = jnp.ones((16, segment), BF16)
-
-    def run(order):
+            sizes = [jnp.sum(x * x, 0, keepdims=True) for x in (scaled, key.astype(F32))]
+            longest = [jnp.maximum(old, new) for old, new in zip(longest, sizes)]
+        bound = jnp.max(longest[0]) * jnp.max(longest[1])
+        bounded[0] = (bound <= 3600.0).astype(jnp.int32)
+
+    @pl.when(bounded[0] == 0)
+    def _():
+        query = queries[step][0:128]
+        is_short = (short_ref[0] != 0).astype(jnp.int32)
+
+        def body(index, peak):
+            chunk = jnp.where(is_short != 0, 2 * index + lax.rem(step, 2), index)
+            scores = dot(keys[chunk][0:128], query, TN)
+            return jnp.maximum(peak, jnp.max(scores, 0, keepdims=True))
+
+        start = jnp.full((1, segment), -jnp.inf, F32)
+        peak = lax.fori_loop(0, jnp.where(is_short != 0, chunks // 2, chunks), body, start)
+        zeros = jnp.zeros((13, segment), BF16)
+        queries[step, 128:144, :] = jnp.concatenate(split_low(peak, 3) + [zeros], 0)
+
+    def body(order, first):
         query = queries[step]
-        peak = total = None
+        total = None
         later = dot(keys[order[0]], query, TN)
         for index, chunk in enumerate(order):
             scores = later
             if index + 1 < len(order):
                 later = dot(keys[order[index + 1]], query, TN)
-            here = jnp.max(scores, 0, keepdims=True)
-            top = here if peak is None else jnp.maximum(peak, here)
-            weights = jnp.exp2(scores - top).astype(BF16)
+            weights = jnp.exp2(scores).astype(BF16)
+            weights_ref[0, chunk] = weights.T
             mixed = dot(values[chunk], weights)
-            total = mixed if peak is None else total * jnp.exp2(peak - top) + mixed
-            peak = top
-        norm = total[64:65, :]
-        result = total[:64] / norm
-        mixed_ref[step] = result
-        log_ref[step] = peak + jnp.log2(norm)
-        for chunk, source, cols in halves(sources, segment):
-
-            @pl.when(step == chunk)
-            def _():
-                sent[source][held, :, cols] = result.astype(BF16)
-
-    by_length(short_ref, run, chunks)
+            total = mixed if total is None else total + mixed
+        sums[...] = total if first else sums[...] + total
+
+    over_chunks(short_ref, chunks, body)
+    total = sums[...]
+    inverse = 1.0 / total[depth : depth + 1, :]
+    result = total[:depth] * inverse
+    mixed_ref[step] = result
+    inverse_ref[step] = inverse
+    for chunk, source, cols in halves(sources, segment):
+
+        @pl.when(step == chunk)
+        def _():
+            sent[source][held, :, cols] = result.astype(BF16)
 
 
 def attend(is_short, heads, earlier=()):
@@ -120,90 +143,100 @@
             grid=(chunks,),
             in_specs=[whole(3, depth, tokens)] * sources + [whole(1, depth, tokens)] * len(earlier),
             out_specs=[whole(1 + held, depth, tokens)] * sources
-            + [whole(chunks, depth, segment), whole(chunks, 1, segment)],
+            + [
+                whole(chunks, depth, segment),
+                whole(chunks, 1, segment),
+                pl.BlockSpec((1, chunks, segment, segment), lambda i, s: (i, 0, 0, 0)),
+            ],
             scratch_shapes=[
-                pltpu.VMEM((chunks, 128, segment), BF16),
-                pltpu.VMEM((chunks, 128, segment), BF16),
+                pltpu.VMEM((chunks, 144, segment), BF16),
+                pltpu.VMEM((chunks, 144, segment), BF16),
                 pltpu.VMEM((chunks, 80, segment), BF16),
+                pltpu.VMEM((80, segment), F32),
+                pltpu.SMEM((1,), jnp.int32),
             ],
         ),
         out_shape=[jax.ShapeDtypeStruct((1 + held, depth, tokens), BF16)] * sources
         + [
             jax.ShapeDtypeStruct((chunks, depth, segment), F32),
             jax.ShapeDtypeStruct((chunks, 1, segment), F32),
+            jax.ShapeDtypeStruct((chunks, chunks, segment, segment), BF16),
         ],
         compiler_params=pltpu.CompilerParams(vmem_limit_bytes=SMALL_VMEM),
         cost_estimate=pl.CostEstimate(
-            flops=16 * work * depth, transcendentals=work, bytes_accessed=16 * sources * tokens * depth
+            flops=16 * work * depth, transcendentals=work, bytes_accessed=2 * work
         ),
         name="attend",
     )(is_short, *heads, *earlier)
-    return out[:sources], out[-2], out[-1]
+    return out[:sources], out[-3:]
 
 
 def attend_back_kernel(short_ref, *refs, sources, segment):
-    heads, grads, (mixed_ref, log_ref), refs = (
+    heads, grads, (mixed_ref, inverse_ref, weights_ref), refs = (
         refs[:sources],
         refs[sources : 2 * sources],
-        refs[2 * sources : 2 * sources + 2],
-        refs[2 * sources + 2 :],
+        refs[2 * sources : 2 * sources + 3],
+        refs[2 * sources + 3 :],
     )
-    outs, (q_aug, g_aug, k_aug, v_aug, grad_q) = refs[:sources], refs[sources:]
+    outs, (queries, g_aug, v_aug, grad_q, grad_kv) = refs[:sources], refs[sources:]
     step = pl.program_id(0)
     chunks = 2 * sources
 
     @pl.when(step == 0)
     def _():
-        minus = jnp.full((16, segment), -1.0, BF16)
         zeros = jnp.zeros((13, segment), BF16)
         for chunk, source, cols in halves(sources, segment):
-            scaled = heads[source][0, :, cols].astype(F32) * (SCALE * LOG2E)
-            high, low = split_low(scaled, 2)
-            q_aug[chunk, 0:64, :] = high
-            q_aug[chunk, 64:128, :] = low
-            q_aug[chunk, 128:144, :] = jnp.concatenate(split_low(log_ref[chunk], 3) + [zeros], 0)
-            grad = grads[source][0, :, cols]
-            inner = jnp.sum(grad.astype(F32) * mixed_ref[chunk], 0, keepdims=True)
-            g_aug[chunk, 0:64, :] = grad
-            g_aug[chunk, 64:80, :] = jnp.concatenate(split_low(inner, 3) + [zeros], 0)
-            key = heads[source][1, :, cols]
-            k_aug[chunk, 0:64, :] = key
-            k_aug[chunk, 64:128, :] = key
-            k_aug[chunk, 128:144, :] = minus
-            v_aug[chunk, 0:64, :] = heads[source][2, :, cols]
-            v_aug[chunk, 64:80, :] = minus
+            queries[chunk] = heads[source][0, :, cols]
+            grad = grads[source][0, :, cols].astype(F32) * inverse_ref[chunk]
+            high, low = split_low(grad, 2)
+            g_aug[chunk, 0:64, :] = high
+            g_aug[chunk, 64:128, :] = low
+            inner = jnp.sum(grad * mixed_ref[chunk], 0, keepdims=True)
+            g_aug[chunk, 128:144, :] = jnp.concatenate(split_low(inner, 3) + [zeros], 0)
         grad_q[...] = jnp.zeros_like(grad_q)
 
-    def run(order):
-        key, value = k_aug[step], v_aug[step]
-        turned = key[0:64].T
-
-        def products(chunk):
-            return dot(q_aug[chunk], key, TN), dot(g_aug[chunk], value, TN)
-
+    def column(index):
+        for chunk, source, cols in halves(sources, segment):
+
+            @pl.when(step == chunk)
+            def _():
+                index(source, cols)
+
+    def load(source, cols):
+        value = heads[source][2, :, cols]
+        v_aug[0:64, :] = value
+        v_aug[64:128, :] = value
+        v_aug[128:144, :] = jnp.full((16, segment), -1.0, BF16)
+        v_aug[144:208, :] = heads[source][1, :, cols]
+
+    column(load)
+    value = v_aug[0:144]
+    turned = v_aug[144:208].T
+
+    def body(order, first):
         key_total = value_total = None
-        later = products(order[0])
+        later = dot(g_aug[order[0]], value, TN)
         for index, chunk in enumerate(order):
-            scores, slopes = later
+            slopes = later
             if index + 1 < len(order):
-                later = products(order[index + 1])
-            weights = jnp.exp2(scores)
-            g_scores = (weights * slopes).astype(BF16)
-            value_part = dot(g_aug[chunk, 0:64, :], weights.astype(BF16))
-            key_part = dot(q_aug[chunk, 0:128, :], g_scores)
+                later = dot(g_aug[order[index + 1]], value, TN)
+            weights = weights_ref[chunk, 0]
+            g_scores = (weights.astype(F32) * slopes).astype(BF16)
+            value_part = dot(g_aug[chunk, 0:128, :], weights)
+            key_part = dot(queries[chunk], g_scores)
             value_total = value_part if value_total is None else value_total + value_part
             key_total = key_part if key_total is None else key_total + key_part
             grad_q[chunk] += dot(g_scores, turned)
-        key_grad = ((key_total[0:64] + key_total[64:128]) * (1.0 / LOG2E)).astype(BF16)
-        value_grad = value_total.astype(BF16)
-        for chunk, source, cols in halves(sources, segment):
-
-            @pl.when(step == chunk)
-            def _():
-                outs[source][1, :, cols] = key_grad
-                outs[source][2, :, cols] = value_grad
-
-    by_length(short_ref, run, chunks)
+        both = jnp.concatenate([key_total, value_total[0:64] + value_total[64:128]], 0)
+        grad_kv[...] = both if first else grad_kv[...] + both
+
+    over_chunks(short_ref, chunks, body)
+
+    def save(source, cols):
+        outs[source][1, :, cols] = (grad_kv[0:64] * SCALE).astype(BF16)
+        outs[source][2, :, cols] = grad_kv[64:128].astype(BF16)
+
+    column(save)
 
     @pl.when(step == chunks - 1)
     def _():
@@ -211,7 +244,7 @@
             outs[source][0, :, cols] = (grad_q[chunk] * SCALE).T.astype(BF16)
 
 
-def attend_back(is_short, heads, mixed, grads, log_sums, at):
+def attend_back(is_short, heads, saved, grads, at):
     sources = len(heads)
     _, depth, tokens = heads[0].shape
     segment, chunks = tokens // 2, 2 * sources
@@ -223,23 +256,27 @@
             grid=(chunks,),
             in_specs=[whole(3, depth, tokens)] * sources
             + [pl.BlockSpec((1, depth, tokens), lambda i, s: (at, 0, 0))] * sources
-            + [whole(chunks, depth, segment), whole(chunks, 1, segment)],
+            + [
+                whole(chunks, depth, segment),
+                whole(chunks, 1, segment),
+                pl.BlockSpec((chunks, 1, segment, segment), lambda i, s: (0, i, 0, 0)),
+            ],
             out_specs=[whole(3, depth, tokens)] * sources,
             scratch_shapes=[
+                pltpu.VMEM((chunks, 64, segment), BF16),
                 pltpu.VMEM((chunks, 144, segment), BF16),
-                pltpu.VMEM((chunks, 80, segment), BF16),
-                pltpu.VMEM((chunks, 144, segment), BF16),
-                pltpu.VMEM((chunks, 80, segment), BF16),
+                pltpu.VMEM((208, segment), BF16),
                 pltpu.VMEM((chunks, segment, depth), F32),
+                pltpu.VMEM((2 * depth, segment), F32),
             ],
         ),
         out_shape=[jax.ShapeDtypeStruct((3, depth, tokens), BF16)] * sources,
         compiler_params=pltpu.CompilerParams(vmem_limit_bytes=VMEM),
         cost_estimate=pl.CostEstimate(
-            flops=40 * work * depth, transcendentals=work, bytes_accessed=40 * sources * tokens * depth
+            flops=40 * work * depth, transcendentals=work, bytes_accessed=2 * work
         ),
         name="attend_back",
-    )(is_short, *heads, *grads, mixed, log_sums)
+    )(is_short, *heads, *grads, *saved)
 
 
 def normalize(hidden):
@@ -257,27 +294,47 @@
     return jnp.sum(values.astype(F32), 0, keepdims=True)
 
 
-def project_kernel(place_ref, tokens, rows, gain, shift, weight, bias, normed, *refs, sources, rounds, block):
-    outs, turned = refs[:-1], refs[-1]
+def row_of(vector):
+    return vector[...].astype(F32)[None, :]
+
+
+def project_kernel(
+    scalars, tokens, first_rows, second_rows, gain, shift, weight, query_bias, value_bias, normed, rows, *refs,
+    sources, rounds, block
+):
+    outs, turned, column = refs[:-2], refs[-2], refs[-1]
     step = pl.program_id(0)
+    pairs = sources // 2
     count = tokens.shape[0] // block
+    size = column.shape[1]
 
     @pl.when(step == 0)
     def _():
+        for index, group in enumerate((first_rows, second_rows)):
+            all_rows = group[...].astype(F32)
+            chosen = lax.broadcasted_iota(jnp.int32, all_rows.shape, 0) == scalars[4 + index]
+            rows[index : index + 1, :] = jnp.sum(jnp.where(chosen, all_rows, 0.0), 0, keepdims=True)
+        biases = row_of(query_bias), jnp.zeros((1, pairs * size), F32), row_of(value_bias)
+        for part, bias in enumerate(biases):
+            for pair in range(pairs):
+                here = jnp.broadcast_to(bias[:, pair * size : (pair + 1) * size], (128, size))
+                column[part * pairs + pair] = here.T
+
         def body(index, _):
             here = token_block(index, block)
-            row = rows[pl.ds(index // (count // 2), 1), :]
+            row = rows[pl.ds(lax.div(index, count // 2), 1), :]
             scaled, _ = normalize(tokens[here, :].astype(F32) + row)
-            low = (scaled * gain[...] + shift[...]).astype(BF16)
+            low = (scaled * row_of(gain) + row_of(shift)).astype(BF16)
             normed[here, :] = low
             turned[:, here] = low.T
             return 0
 
         lax.fori_loop(0, count, body, 0)
 
-    result = (dot(weight[...], turned[...], TN) + bias[...]).astype(BF16)
-    pair, low_bit = step % (sources // 2), place_ref[0] % 2
-    for high in range(sources // 2):
+    pair, high_bit, low_bit = lax.rem(step, pairs), lax.div(scalars[0], 2), lax.rem(scalars[0], 2)
+    bias = column[step - pair + (pair ^ high_bit)][:, 0:1]
+    result = (dot(weight[...], turned[...], TN) + bias).astype(BF16)
+    for high in range(pairs):
         for bit in range(2):
 
             @pl.when((pair == high) & (low_bit == bit))
@@ -288,11 +345,11 @@
                         outs[r * sources + 2 * high + (low ^ bit)][0] = result[at : at + HEAD_DIM]
 
 
-def project(place, tokens, rows, gain, shift, weight, bias, sources, rounds):
+def project(scalars, tokens, time_table, gain, shift, weight, query_bias, value_bias, sources, rounds):
     tok_here, width = tokens.shape
     pair = 2 * rounds * HEAD_DIM
     pairs = sources // 2
-    block_of = lambda i, p: i // pairs * pairs + (i % pairs ^ p[0] // 2)
+    group = lambda index: pl.BlockSpec((8, width), lambda i, p: (p[2 + index], 0))
     out = pl.pallas_call(
         partial(project_kernel, sources=sources, rounds=rounds, block=tok_here // 4),
         grid_spec=pltpu.PrefetchScalarGridSpec(
@@ -300,25 +357,39 @@
             grid=(3 * pairs,),
             in_specs=[
                 whole(tok_here, width),
-                whole(2, width),
-                whole(1, width),
-                whole(1, width),
-                pl.BlockSpec((width, pair), lambda i, p: (0, block_of(i, p))),
-                pl.BlockSpec((pair, 1), lambda i, p: (block_of(i, p), 0)),
+                group(0),
+                group(1),
+                whole(width),
+                whole(width),
+                pl.BlockSpec((width, pair), lambda i, p: (0, pair_block(i, p, pairs))),
+                whole(width),
+                whole(width),
             ],
-            out_specs=[whole(tok_here, width)]
-            + [pl.BlockSpec((1, HEAD_DIM, tok_here), lambda i, p: (i // pairs, 0, 0))] * (rounds * sources),
-            scratch_shapes=[pltpu.VMEM((width, tok_here), BF16)],
-        ),
-        out_shape=[jax.ShapeDtypeStruct((tok_here, width), BF16)]
+            out_specs=[whole(tok_here, width), whole(2, width)]
+            + [pl.BlockSpec((1, HEAD_DIM, tok_here), lambda i, p: (lax.div(i, pairs), 0, 0))]
+            * (rounds * sources),
+            scratch_shapes=[
+                pltpu.VMEM((width, tok_here), BF16),
+                pltpu.VMEM((3 * pairs, pair, 128), F32),
+            ],
+        ),
+        out_shape=[
+            jax.ShapeDtypeStruct((tok_here, width), BF16),
+            jax.ShapeDtypeStruct((2, width), F32),
+        ]
         + [jax.ShapeDtypeStruct((3, HEAD_DIM, tok_here), BF16)] * (rounds * sources),
-        compiler_params=pltpu.CompilerParams(vmem_limit_bytes=SMALL_VMEM),
+        compiler_params=pltpu.CompilerParams(vmem_limit_bytes=VMEM),
         cost_estimate=pl.CostEstimate(
             flops=2 * tok_here * weight.size, transcendentals=0, bytes_accessed=4 * weight.size
         ),
         name="project",
-    )(place, tokens, rows, gain, shift, weight, bias)
-    return out[0], [out[1 + r * sources : 1 + (r + 1) * sources] for r in range(rounds)]
+    )(scalars, tokens, time_table, time_table, gain, shift, weight, query_bias, value_bias)
+    return out[0], out[1], [out[2 + r * sources : 2 + (r + 1) * sources] for r in range(rounds)]
+
+
+def pair_block(step, scalars, pairs):
+    at = lax.rem(step, pairs)
+    return step - at + (at ^ lax.div(scalars[0], 2))
 
 
 def mlp_kernel(place_ref, *refs, groups, sources, block):
@@ -329,12 +400,12 @@
     result, g_resid = refs[11:13]
     sent_grads = refs[13 : 13 + pieces]
     send, keep, vectors, g_up_b = refs[13 + pieces : 17 + pieces]
-    attended, normed, resid, gelu_act, g_up, down_sum, g_normed, g_branch, g_attended = refs[17 + pieces :]
+    attended, normed, resid, gelu_act, g_up, down_sum, g_normed, g_branch, g_attended, bias = refs[17 + pieces :]
     step, last = pl.program_id(0), pl.num_programs(0) - 1
     tok_here, width = tokens.shape
     count = tok_here // block
     place = place_ref[0]
-    low_bit = place % 2 == 0
+    low_bit = lax.rem(place, 2) == 0
 
     def head_rows(groups):
         for index in range(len(groups) * sources):
@@ -358,17 +429,20 @@
 
     @pl.when(step == 0)
     def _():
+        bias_row = row_of(up_b)
+        for index in range(bias.shape[0]):
+            bias[index : index + 1, :] = bias_row[:, index * width : (index + 1) * width]
         for index, at, here in head_rows(in_groups):
             attended[here, :] = gathered[index][at]
 
         def body(index, _):
             here = token_block(index, block)
-            row = rows[pl.ds(index // (count // 2), 1), :]
+            row = rows[pl.ds(lax.div(index, count // 2), 1), :]
             hidden = tokens[here, :].astype(F32) + row
-            total = hidden + (dot(attended[:, here], out_w[...], TN) + out_b[...])
+            total = hidden + (dot(attended[:, here], out_w[...], TN) + row_of(out_b))
             resid[here, :] = total
             scaled, _ = normalize(total)
-            normed[here, :] = (scaled * gain[...] + shift[...]).astype(BF16)
+            normed[here, :] = (scaled * row_of(gain) + row_of(shift)).astype(BF16)
             return 0
 
         lax.fori_loop(0, count, body, 0)
@@ -379,7 +453,7 @@
     def _():
         def body(index, total):
             here = token_block(index, block)
-            act = dot(normed[here, :], up_w[...]) + up_b[...]
+            act = dot(normed[here, :], up_w[...]) + bias[pl.ds(step, 1), :]
             g_gelu = dot(cotangent[here, :], down_w[...], NT)
             below = 0.5 * (1.0 + lax.erf(act * 0.7071067811865476))
             density = 0.3989422804014327 * jnp.exp(-0.5 * act * act)
@@ -391,7 +465,7 @@
             g_normed[here, :] += dot(grad, up_w[...], NT)
             return total + column_sum(grad)
 
-        g_up_b[...] = lax.fori_loop(0, count, body, jnp.zeros(up_b.shape, F32))
+        g_up_b[...] = lax.fori_loop(0, count, body, jnp.zeros(g_up_b.shape, F32))
         put(0, dot(g_up[...], normed[...], TN))
         put(1, dot(cotangent[...], gelu_act[...], TN))
 
@@ -400,10 +474,10 @@
         def body(index, sums):
             here = token_block(index, block)
             total = resid[here, :]
-            result[here, :] = (total + (down_sum[here, :] + down_b[...])).astype(BF16)
+            result[here, :] = (total + (down_sum[here, :] + row_of(down_b))).astype(BF16)
             scaled, inverse = normalize(total)
             grad = g_normed[here, :]
-            inner = grad * gain[...]
+            inner = grad * row_of(gain)
             g_out = cotangent[here, :].astype(F32)
             g_total = g_out + inverse * (
                 inner
@@ -449,13 +523,13 @@
                 whole(2, width),
                 whole(tok_here, width),
                 whole(width, width),
-                whole(1, width),
-                whole(1, width),
-                whole(1, width),
+                whole(width),
+                whole(width),
+                whole(width),
                 pl.BlockSpec((width, width), lambda j, b: (0, at(j))),
-                pl.BlockSpec((1, width), lambda j, b: (0, at(j))),
+                whole(hidden_units),
                 pl.BlockSpec((width, width), lambda j, b: (at(j), 0)),
-                whole(1, width),
+                whole(width),
             ],
             out_specs=[whole(tok_here, width)] * 2
             + [whole(*shape) for shape in shapes]
@@ -470,6 +544,7 @@
                 pltpu.VMEM((tok_here, width), F32),
                 pltpu.VMEM((tok_here, width), BF16),
                 pltpu.VMEM((width, tok_here), BF16),
+                pltpu.VMEM((steps, width), F32),
             ],
         ),
         out_shape=[
@@ -494,36 +569,65 @@
     return out[0], out[1], grads, out[-4:]
 
 
-def finish_kernel(place_ref, *refs, rounds, sources, block):
-    pieces = rounds * sources
-    back, refs = refs[:pieces], refs[pieces:]
-    weight, tokens, rows, gain, g_resid, vectors, g_up_b, g_tokens, sums, g_normed, packed = refs
-    step, last = pl.program_id(0), pl.num_programs(0) - 1
-    pair, low_bit = step % (sources // 2), place_ref[0] % 2
-    for high in range(sources // 2):
+def unproject(scalars, back, weight, packed, bias, chosen, rounds, sources):
+    step, pairs = pl.program_id(0), sources // 2
+    pair, high_bit, low_bit = lax.rem(step, pairs), lax.div(scalars[0], 2), lax.rem(scalars[0], 2)
+    size = len(chosen) * HEAD_DIM
+
+    @pl.when(step == 0)
+    def _():
+        bias[...] = jnp.zeros_like(bias)
+
+    for high in range(pairs):
 
         @pl.when(pair == high)
         def _():
             for j in range(2 * high, 2 * high + 2):
-                for r in range(rounds):
-                    at = ((j % 2 ^ low_bit) * rounds + r) * HEAD_DIM
-                    packed[pl.ds(pl.multiple_of(at, HEAD_DIM), HEAD_DIM), :] = back[r * sources + j][0]
-
-    pairs, size = sources // 2, packed.shape[0]
+                for index in range(len(chosen)):
+                    at = ((j % 2 ^ low_bit) * len(chosen) + index) * HEAD_DIM
+                    here = pl.ds(pl.multiple_of(at, HEAD_DIM), HEAD_DIM)
+                    packed[here, :] = back[index * sources + j][0]
+
+    columns = [(low * rounds + chosen[0]) * HEAD_DIM for low in range(2)]
     ones = jnp.ones((8, packed.shape[1]), BF16)
-    bias = dot(ones, packed[...], NT)[0:1]
+    found = dot(ones, packed[...], NT)[0:1]
     for part in range(3):
         for at in range(pairs):
 
-            @pl.when((step // pairs == part) & ((pair ^ place_ref[0] // 2) == at))
+            @pl.when((lax.div(step, pairs) == part) & ((pair ^ high_bit) == at))
             def _():
-                sums[10 + part : 11 + part, at * size : (at + 1) * size] = bias
-
-    added = dot(packed[...], weight[...], (((0,), (1,)), ((), ())))
+                for low, column in enumerate(columns):
+                    start = 2 * at * rounds * HEAD_DIM + column
+                    bias[part : part + 1, start : start + size] = found[:, low * size : (low + 1) * size]
+
+    picked = jnp.concatenate([weight[:, column : column + size] for column in columns], 1)
+    return dot(packed[...], picked, (((0,), (1,)), ((), ())))
+
+
+def begin_kernel(scalars, *refs, chosen, rounds, sources):
+    back, (weight, g_normed, bias, packed) = refs[:-4], refs[-4:]
+    added = unproject(scalars, back, weight, packed, bias, chosen, rounds, sources)
+
+    @pl.when(pl.program_id(0) == 0)
+    def _():
+        g_normed[...] = added
+
+    @pl.when(pl.program_id(0) > 0)
+    def _():
+        g_normed[...] += added
+
+
+def finish_kernel(scalars, *refs, chosen, rounds, sources, block):
+    pieces = len(chosen) * sources
+    back, refs = refs[:pieces], refs[pieces:]
+    weight, tokens, rows, gain, g_resid, vectors, g_up_b, g_before, bias_before = refs[:9]
+    g_tokens, sums, g_normed, packed, bias = refs[9:]
+    step, last = pl.program_id(0), pl.num_programs(0) - 1
+    added = unproject(scalars, back, weight, packed, bias, chosen, rounds, sources)
 
     @pl.when(step == 0)
     def _():
-        g_normed[...] = added
+        g_normed[...] = g_before[...] + added
 
     @pl.when(step > 0)
     def _():
@@ -540,7 +644,7 @@
                 here = token_block(index + first * (count // 2), block)
                 scaled, inverse = normalize(tokens[here, :].astype(F32) + rows[first : first + 1, :])
                 grad = g_normed[here, :]
-                inner = grad * gain[...]
+                inner = grad * row_of(gain)
                 g_hidden = g_resid[here, :] + inverse * (
                     inner
                     - jnp.mean(inner, -1, keepdims=True)
@@ -557,37 +661,75 @@
         sums[2:6, :] = vectors[...]
         for index in range(4):
             sums[6 + index : 7 + index, :] = g_up_b[:, index * width : (index + 1) * width]
-        sums[13:14, :] = empty
-        is_short = place_ref[1] != 0
+        lane = lax.broadcasted_iota(jnp.int32, (1, width), 1)
+        is_short = scalars[1] != 0
+        sums[10:13, :] = bias_before[...] + bias[...]
+        pick = lambda at, other: jnp.where(lane == at, scalars[2 + at].astype(F32), other)
+        sums[13:14, :] = jnp.where(scalars[0] == 0, pick(0, pick(1, 0.0)), 0.0)
         sums[14:15, :] = jnp.where(is_short, one[2], one[2] + two[2])
         sums[15:16, :] = jnp.where(is_short, two[2], 0.0)
 
 
-def finish(place, back, weight, tokens, rows, gain, g_resid, vectors, g_up_b):
-    tok_here, width = tokens.shape
-    rounds, sources = len(back), len(back[0])
+def back_specs(back, width, sources, rounds):
+    pairs = sources // 2
+    block = pl.BlockSpec((1,) + back[0].shape[1:], lambda i, p: (lax.div(i, pairs), 0, 0))
+    pair = 2 * rounds * HEAD_DIM
+    return [block] * len(back) + [
+        pl.BlockSpec((width, pair), lambda i, p: (0, pair_block(i, p, pairs)))
+    ]
+
+
+def begin_finish(scalars, back, chosen, weight, rounds):
+    sources = len(back[0])
     pieces = [part for group in back for part in group]
-    pair = 2 * rounds * HEAD_DIM
-    pairs = sources // 2
+    width, tok_here = weight.shape[0], pieces[0].shape[2]
     return pl.pallas_call(
-        partial(finish_kernel, rounds=rounds, sources=sources, block=tok_here // 4),
+        partial(begin_kernel, chosen=chosen, rounds=rounds, sources=sources),
         grid_spec=pltpu.PrefetchScalarGridSpec(
             num_scalar_prefetch=1,
-            grid=(3 * pairs,),
-            in_specs=[pl.BlockSpec((1, HEAD_DIM, tok_here), lambda i, p: (i // pairs, 0, 0))] * len(pieces)
+            grid=(3 * sources // 2,),
+            in_specs=back_specs(pieces, width, sources, rounds),
+            out_specs=[whole(tok_here, width), whole(3, width)],
+            scratch_shapes=[pltpu.VMEM((2 * len(chosen) * HEAD_DIM, tok_here), BF16)],
+        ),
+        out_shape=[
+            jax.ShapeDtypeStruct((tok_here, width), F32),
+            jax.ShapeDtypeStruct((3, width), F32),
+        ],
+        compiler_params=pltpu.CompilerParams(vmem_limit_bytes=SMALL_VMEM),
+        cost_estimate=pl.CostEstimate(
+            flops=2 * tok_here * weight.size, transcendentals=0, bytes_accessed=4 * weight.size
+        ),
+        name="begin_finish",
+    )(scalars, *pieces, weight)
+
+
+def finish(scalars, back, chosen, weight, tokens, rows, gain, g_resid, vectors, g_up_b, before, rounds):
+    tok_here, width = tokens.shape
+    sources = len(back[0])
+    pieces = [part for group in back for part in group]
+    return pl.pallas_call(
+        partial(finish_kernel, chosen=chosen, rounds=rounds, sources=sources, block=tok_here // 4),
+        grid_spec=pltpu.PrefetchScalarGridSpec(
+            num_scalar_prefetch=1,
+            grid=(3 * sources // 2,),
+            in_specs=back_specs(pieces, width, sources, rounds)
             + [
-                pl.BlockSpec(
-                    (width, pair), lambda i, p: (0, i // pairs * pairs + (i % pairs ^ p[0] // 2))
-                ),
                 whole(tok_here, width),
                 whole(2, width),
-                whole(1, width),
+                whole(width),
                 whole(tok_here, width),
                 whole(*vectors.shape),
                 whole(*g_up_b.shape),
+                whole(tok_here, width),
+                whole(3, width),
             ],
             out_specs=[whole(tok_here, width), whole(16, width)],
-            scratch_shapes=[pltpu.VMEM((tok_here, width), F32), pltpu.VMEM((pair, tok_here), BF16)],
+            scratch_shapes=[
+                pltpu.VMEM((tok_here, width), F32),
+                pltpu.VMEM((2 * len(chosen) * HEAD_DIM, tok_here), BF16),
+                pltpu.VMEM((3, width), F32),
+            ],
         ),
         out_shape=[
             jax.ShapeDtypeStruct((tok_here, width), BF16),
@@ -598,7 +740,7 @@
             flops=2 * tok_here * weight.size, transcendentals=0, bytes_accessed=8 * weight.size
         ),
         name="finish",
-    )(place, *pieces, weight, tokens, rows, gain, g_resid, vectors, g_up_b)
+    )(scalars, *pieces, weight, tokens, rows, gain, g_resid, vectors, g_up_b, *before)
 
 
 def qkv_grad_kernel(block_ref, *refs, rounds, sources, order):
@@ -722,16 +864,19 @@
     for low in range(2):
         both = lambda at, size: jnp.concatenate([store[low, at : at + size], store[2 + low, at : at + size]], 0).T
         up[low * lanes : (low + 1) * lanes, :] = both(0, wide)
-        for k in range(steps):
-            at = (2 * k + low) * lanes
-            down[at : at + lanes, :] = both(wide + k * each, each)
-        out[low * lanes : (low + 1) * lanes, :] = both(2 * wide, each)
+        for half in range(2):
+            here = slice(half * each, (half + 1) * each)
+            share = store.at[2 * half + low]
+            for k in range(steps):
+                at, row = (2 * k + low) * lanes, wide + k * each
+                down[here, at : at + lanes] = share[row : row + each]
+            out[here, low * lanes : (low + 1) * lanes] = share[2 * wide : 2 * wide + each]
 
 
 def undeal(place, shares, steps, width, dp):
     rows, lanes = shares[0].shape
-    shapes = [(width, width * steps // dp), (width * steps, width // dp), (width, width // dp)]
-    return pl.pallas_call(
+    shapes = [(width, width * steps // dp), (width // dp, width * steps), (width // dp, width)]
+    up, down, out = pl.pallas_call(
         partial(undeal_kernel, sources=len(shares), steps=steps, each=width // dp // 2),
         grid_spec=pltpu.PrefetchScalarGridSpec(
             num_scalar_prefetch=1,
@@ -744,23 +889,19 @@
         cost_estimate=pl.CostEstimate(flops=0, transcendentals=0, bytes_accessed=24 * rows * lanes),
         name="undeal",
     )(place, *shares)
+    return up, down.T, out.T
 
 
 def turn_kernel(*refs):
     *parts, out = refs
-    half = len(parts) // 2
-    at = 0
-    for kept, got in zip(parts[:half], parts[half:]):
-        total = (kept[0].astype(F32) + got[...].astype(F32)).T.astype(BF16)
-        out[at : at + total.shape[0], :] = total
-        at += total.shape[0]
-
-
-def turn(kept, got):
-    columns, rows = sum(part.shape[1] for part in got), got[0].shape[0]
+    out[...] = total_of([part[0] for part in parts]).T.astype(BF16)
+
+
+def turn(parts):
+    _, rows, columns = parts[0].shape
     return pl.pallas_call(
         turn_kernel, out_shape=jax.ShapeDtypeStruct((columns, rows), BF16), name="turn"
-    )(*kept, *got)
+    )(*parts)
 
 
 def regroup_kernel(place_ref, *refs, rounds):
@@ -791,16 +932,15 @@
 
 
 def stack_kernel(parts, out):
-    rows = parts.shape[2]
-    for index in range(parts.shape[0]):
-        out[index * rows : (index + 1) * rows, :] = parts[index].astype(F32).T
+    both = [parts[index].astype(F32) for index in range(parts.shape[0])]
+    out[...] = jnp.concatenate(both, 1)
 
 
 def stack_rows(parts):
     count, columns, rows = parts.shape
     return pl.pallas_call(
-        stack_kernel, out_shape=jax.ShapeDtypeStruct((rows * count, columns), F32), name="stack_rows"
-    )(parts)
+        stack_kernel, out_shape=jax.ShapeDtypeStruct((columns, rows * count), F32), name="stack_rows"
+    )(parts).T
 
 
 def exchange(values, axis):
@@ -866,56 +1006,57 @@
     rounds = HEADS // sources
     is_short = data_group[0] == 0
     short_flag = is_short.astype(jnp.int32)[None]
-    rows = time_table[jnp.where(is_short, time_steps[0], time_steps[0, 0])].astype(F32)
-    flat = lambda vector: vector.astype(F32)[None]
-    qkv_bias = jnp.concatenate([query_bias, jnp.zeros_like(query_bias), value_bias]).astype(F32)
-
     place_arg = place.astype(jnp.int32)[None]
     block_arg = block.astype(jnp.int32)[None]
     few = dp <= 8
-
-    normed, sending = project(
-        place_arg,
+    row_steps = jnp.where(is_short, time_steps[0], time_steps[0, 0])
+    scalars = jnp.concatenate([place_arg, short_flag, lax.div(row_steps, 8), lax.rem(row_steps, 8)])
+
+    normed, rows, sending = project(
+        scalars,
         tokens,
-        rows,
-        flat(attn_norm_gain),
-        flat(attn_norm_bias),
+        time_table,
+        attn_norm_gain,
+        attn_norm_bias,
         qkv_weight,
-        qkv_bias[:, None],
+        query_bias,
+        value_bias,
         sources,
         rounds,
     )
-    heads, mixed, logs, sent = [trade(sending[0], "seq")], [], [], []
+    heads, saved, sent = [trade(sending[0], "seq")], [], []
     returned = []
     for r in range(rounds):
         if r + 1 < rounds:
-            ahead = sending[r + 1] if r < 1 else after(sending[r + 1], logs[r - 1])
+            ahead = sending[r + 1] if r < 1 else after(sending[r + 1], saved[r - 1][1])
             heads.append(trade(ahead, "seq"))
-        out, full, log = attend(short_flag, heads[r], sent[0] if r == 1 else ())
-        mixed.append(full)
-        logs.append(log)
+        ready = after(heads[r], saved[r - 1][1]) if r else heads[r]
+        out, kept = attend(short_flag, ready, sent[0] if r == 1 else ())
+        saved.append(kept)
         sent.append(out)
         if r >= 1:
-            returned.append(trade(out, "seq"))
-
-    across = swap(after(normed, log), "seq", 2)
+            returned.append(trade(after(out, *returned[-1]) if returned else out, "seq"))
+
+    beside = swap(after(normed, saved[1][1]), "seq", 1)
+    across = swap(after(normed, *returned[-1]), "seq", 2)
     groups = (((0, 1), (2,)), ((0,), (1, 2)))
     result, g_resid, sent_grads, (send, keep, vectors, g_up_b) = mlp(
         place_arg,
         groups,
         returned,
-        tokens,
+        after(tokens, beside),
         rows,
         cotangent,
         out_weight,
-        flat(out_bias),
-        flat(mlp_norm_gain),
-        flat(mlp_norm_bias),
+        out_bias,
+        mlp_norm_gain,
+        mlp_norm_bias,
         up_weight,
-        flat(up_bias),
+        up_bias,
         down_weight,
-        flat(down_bias),
+        down_bias,
     )
+    send, *sent_grads = after((send, *sent_grads), across)
     got = swap(send, "seq", 1)
     first_grads = trade(sent_grads[0], "seq")
     if few:
@@ -924,12 +1065,12 @@
         ready = outgoing
     else:
         ready = summed = total_of([keep, got]).astype(BF16)
-    rest_grads = trade(sent_grads[1], "seq")
-    beside = [normed, swap(normed, "seq", 1), across, swap(across, "seq", 1)]
-    held = after(heads[0], ready)
-    grads = [attend_back(short_flag, held, mixed[0], first_grads, logs[0], 0)]
+    rest_grads = trade(after(sent_grads[1], *first_grads), "seq")
+    beside = [normed, beside, across, swap(across, "seq", 1)]
+    grads = [attend_back(short_flag, after(heads[0], ready, beside[3]), saved[0], first_grads, 0)]
     back = [trade(grads[0], "seq")]
-    grads.append(attend_back(short_flag, heads[1], mixed[1], rest_grads, logs[1], 0))
+    held = after(heads[1], *grads[0])
+    grads.append(attend_back(short_flag, held, saved[1], rest_grads, 0))
     back.append(trade(grads[1], "seq"))
     order = (0, 4, 2, 6, 1, 5, 3, 7) if few else (0, 1)
     stay_a, away_a = qkv_grad(block_arg, grads, beside, order)
@@ -939,37 +1080,59 @@
         dealt = exchange(half_sum, "dp")
         ready = half_sum
     held = after(heads[2], stay_a, ready, *back[0])
-    grads.append(attend_back(short_flag, held, mixed[2], rest_grads, logs[2], 1))
+    grads.append(attend_back(short_flag, held, saved[2], rest_grads, 1))
     back.append(trade(grads[2], "seq"))
     grads[2] = after(grads[2], *back[1])
     stay_b, away_b = qkv_grad(block_arg, grads[2:], beside, order)
+    earlier = [after(parts, stay_b) for parts in back[:2]]
+    before = begin_finish(scalars, earlier, (0, 1), qkv_weight, rounds)
+    ready = before[1]
     if few:
-        parts = [stay_a, stay_b], [after(got_a, grads[2]), swap(away_b, "dp", 1)]
-        for bit in (2, 4):
-            kept = [total_of(pair).astype(BF16) for pair in zip(*parts)]
-            size = kept[0].shape[0] // 2
-            parts = [part[:size] for part in kept], [swap(part[size:], "dp", bit) for part in kept]
-        summed = turn(parts[0], [part[0] for part in parts[1]])
+        kept, got = [stay_a, stay_b], [after(got_a, grads[2]), swap(away_b, "dp", 1)]
+        part = jnp.concatenate([total_of(pair).astype(BF16) for pair in zip(kept, got)], 2)
+        share = total_of([after(dealt, before[1])[i] for i in range(dp)]).astype(BF16)
+        ready = part, share
+        sums = [part[:1]] + [swap(part[at : at + 1], "dp", bit) for at, bit in ((1, 4), (2, 2), (3, 6))]
+        share_across = swap(share, "seq", 2)
+
+    steps_arg = time_steps[0].astype(jnp.int32)
+    flags = jnp.concatenate([place_arg, short_flag, steps_arg])
+    g_tokens, small = finish(
+        flags,
+        after(back[2:], ready),
+        (2,),
+        qkv_weight,
+        tokens,
+        rows,
+        attn_norm_gain,
+        g_resid,
+        vectors,
+        g_up_b,
+        before,
+        rounds,
+    )
+    if few:
+        shares = [share, swap(share, "seq", 1), share_across, swap(share_across, "seq", 1)]
+        summed = turn(after(sums, small))
         columns = regroup(place_arg, spread(summed, "seq", sources), rounds)
-
-    flags = jnp.concatenate([place_arg, short_flag])
-    g_tokens, small = finish(
-        flags, back, qkv_weight, tokens, rows, flat(attn_norm_gain), g_resid, vectors, g_up_b
-    )
-    for bit in (1, 2):
-        small = small + swap(small, "seq", bit)
-    by_block = (jnp.arange(dp) == block)[:, None]
-    row_slot = jnp.where(by_block[:, :, None], small[None, 14:], 0.0).reshape(-1, width)
-    small = jnp.concatenate([small[:14], row_slot])
-    steps = jnp.where(by_block, time_steps.astype(F32), 0.0)
-    bit = 1
-    while bit < dp:
-        small = small + swap(small, "dp", bit)
-        steps = steps + swap(steps, "dp", bit)
-        bit *= 2
+    small = total_of(spread(small, "seq", sources))
     if few:
-        share = total_of([dealt[i] for i in range(dp)]).astype(BF16)
-        shares = spread(share, "seq", sources)
+        own, other = small, swap(small, "dp", 1)
+        small = jnp.concatenate([own[:13] + other[:13], own[13:], other[13:]])
+        all_small = jnp.stack([small] + [swap(small, "dp", bit) for bit in (2, 4, 6)])
+        small = jnp.sum(all_small[:, :13], 0)
+        by_block = all_small[:, 13:].reshape(dp, 3, width)
+    else:
+        slots = jnp.where((jnp.arange(dp) == block)[:, None, None], small[None, 13:], 0.0)
+        small = jnp.concatenate([small[:13], slots.reshape(-1, width)])
+        bit = 1
+        while bit < dp:
+            small = small + swap(small, "dp", bit)
+            bit *= 2
+        by_block = small[13:].reshape(dp, 3, width)
+    steps = by_block[:, 0, :2].reshape(1, -1).astype(jnp.int32)
+    all_rows = by_block[:, 1:].reshape(-1, width)
+    if few:
         sum_up, sum_down, sum_out = undeal(place_arg, shares, hidden_units // width, width, dp)
         sum_qkv = stack_rows(exchange(columns.reshape(dp, 3 * width // dp, width // dp), "dp"))
     else:
@@ -981,9 +1144,9 @@
             rounds,
         )
     share_cols = width // dp
-    rows_mine = lax.dynamic_slice_in_dim(small[14:], block * share_cols, share_cols, 1)
+    rows_mine = lax.dynamic_slice_in_dim(all_rows, block * share_cols, share_cols, 1)
     table_rows = time_table.shape[0]
-    hits = jnp.arange(table_rows, dtype=jnp.int32)[:, None] == steps.reshape(1, -1).astype(jnp.int32)
+    hits = jnp.arange(table_rows, dtype=jnp.int32)[:, None] == steps
     sum_table = jnp.dot(hits.astype(F32), rows_mine, precision=lax.Precision.HIGHEST)
     return (
         result[None],

time: 487 us -> 448 us (0.920)
  Pallas kernels: 313 us -> 238 us
  starting transfers between devices: 52.3 us -> 112 us
  waiting for transfers between devices: 64.8 us -> 44.2 us
    pallas_call x3, Pallas kernels: 132 us -> 73.7 us  [attend_back(): pl.pallas_call(partial(attend_back_kernel, sources=sources, segment=segme...]
    all_to_all x2, starting transfers between devices: 11.6 us -> 55 us  [exchange(): return lax.all_to_all(values, axis, split_axis=0, concat_axis=0, tiled=True)]
    pallas_call x3, Pallas kernels: 73.1 us -> 45.9 us  [attend(): pl.pallas_call(partial(attend_kernel, sources=sources, segment=segment, h...]
    ppermute x55 -> x53, waiting for transfers between devices: 58.2 us -> 35.5 us  [swap(): return lax.ppermute(values, axis, [(j, j ^ bit) for j in range(size)])]
    ppermute x55 -> x53, starting transfers between devices: 40.7 us -> 57 us  [swap(): return lax.ppermute(values, axis, [(j, j ^ bit) for j in range(size)])]
    pallas_call x2 -> x3, Pallas kernels: 19.3 us -> 27.4 us  [the longest x1 13.4 us: finish(): pl.pallas_call(partial(finish_kernel, chosen=chosen, rounds=rounds, sourc...]
    pallas_call x1, Pallas kernels: 7.66 us -> 12.7 us  [project(): pl.pallas_call(partial(project_kernel, sources=sources, rounds=rounds, bl...]
    unnamed x167 -> x150, local copies, waits for them, and re-layouts: 25.9 us -> 30.3 us
  transfers between devices with their start and end apart: 57 -> 55, of which waited for: 19 -> 11; matrix products, arithmetic and copies ran while one was open for 4% -> 2% of each run, Pallas kernels for 52% -> 48%
where the time goes in v3:
time: 448 us; the launch traced here: 440 us
  Pallas kernels  238 us (53%)
  starting transfers between devices  112 us (25%)
  waiting for transfers between devices  44.2 us (10%)
  local copies, waits for them, and re-layouts  31.8 us (7%)
  other arithmetic  10 us (2%)
    pallas_call x3, Pallas kernels, attend_back(): pl.pallas_call(partial(attend_back_kernel, sources=sources, segment=segme...  73.7 us
    ppermute x53, starting transfers between devices, swap(): return lax.ppermute(values, axis, [(j, j ^ bit) for j in range(size)])  57 us
    all_to_all x2, starting transfers between devices, exchange(): return lax.all_to_all(values, axis, split_axis=0, concat_axis=0, tiled=True)  55 us
    pallas_call x1, Pallas kernels, mlp(): pl.pallas_call(partial(mlp_kernel, groups=groups, sources=sources, block=...  53.5 us
    pallas_call x3, Pallas kernels, attend(): pl.pallas_call(partial(attend_kernel, sources=sources, segment=segment, h...  45.9 us
    ppermute x53, waiting for transfers between devices, swap(): return lax.ppermute(values, axis, [(j, j ^ bit) for j in range(size)])  35.5 us
    unnamed x150, local copies, waits for them, and re-layouts  30.3 us
    pallas_call x1, Pallas kernels, finish(): pl.pallas_call(partial(finish_kernel, chosen=chosen, rounds=rounds, sourc...  13.4 us
  transfers between devices with their start and end apart: 55, of which 11 were waited for; matrix products, arithmetic and copies ran while one was open for 2% of the time, Pallas kernels for 48%

profile of v3, /device:TPU:0, one launch (start us, length us, event | category | flops | bytes accessed | tf_op | source)
XLA Modules:
  0.0 439.9 jit_solution(13147447265574734850)
XLA Ops:
  3.2 12.7 %project.1 = (bf16[1024,768]{1,0:T(8,128)(2,1)}, f32[2,768]{1,0:T(2,128)}, bf16[3,64,1024]{2,1,0:T(8,128)(2,1)}, bf16[3,64,1024]{2,1,0:T(8,128)(2,1)}, bf16[3,64...) custom-call(s32[6]{0:T(128)} %pad_add_fusion.scalars, ...), custom_call_target="tpu_custom_call" | custom-call | flops 3623878656 | bytes 7077888 | tf_op jit(solution)/shard_map/project/pallas_call | solution.py:353
  21.2 8.0 %collective-permute-done.4.refs_2_ = bf16[3,64,1024]{2,1,0:T(8,128)(2,1)S(1)} collective-permute-done((bf16[3,64,1024]{2,1,0:T(8,128)(2,1)}, bf16[3,64,1024]{2,1,0:T(8,128)(2,1)S(1)}, u32[]{:S(2)}, u32[]{:S(2)}) %collective-permute-start.4) | collective-permute-done | bytes 393248 | tf_op jit(solution)/shard_map/ppermute | solution.py:791
  29.2 8.0 %collective-permute-done.5.refs_3_ = bf16[3,64,1024]{2,1,0:T(8,128)(2,1)S(1)} collective-permute-done((bf16[3,64,1024]{2,1,0:T(8,128)(2,1)}, bf16[3,64,1024]{2,1,0:T(8,128)(2,1)S(1)}, u32[]{:S(2)}, u32[]{:S(2)}) %collective-permute-start.5) | collective-permute-done | bytes 393248 | tf_op jit(solution)/shard_map/ppermute | solution.py:791
  38.3 15.3 %attend.3 = (bf16[1,64,1024]{2,1,0:T(8,128)(2,1)S(1)}, bf16[1,64,1024]{2,1,0:T(8,128)(2,1)S(1)}, bf16[1,64,1024]{2,1,0:T(8,128)(2,1)S(1)}, bf16[1,64,1024]{2,1,0...) custom-call(s32[1]{0:T(128)S(6)} %broadcast_in_dim.21.short_ref, ...), custom_call_target="tpu_custom_call" | custom-call | flops 17179869184 | bytes 33554432 | tf_op jit(solution)/shard_map/attend/pallas_call | solution.py:139
  56.9 15.2 %attend.4 = (bf16[2,64,1024]{2,1,0:T(8,128)(2,1)S(1)}, bf16[2,64,1024]{2,1,0:T(8,128)(2,1)S(1)}, bf16[2,64,1024]{2,1,0:T(8,128)(2,1)S(1)}, bf16[2,64,1024]{2,1,0...) custom-call(s32[1]{0:T(128)S(6)} %broadcast_in_dim.21.short_ref, ...), custom_call_target="tpu_custom_call" | custom-call | flops 17179869184 | bytes 33554432 | tf_op jit(solution)/shard_map/attend/pallas_call | solution.py:139
  75.6 15.4 %attend.5 = (bf16[1,64,1024]{2,1,0:T(8,128)(2,1)S(1)}, bf16[1,64,1024]{2,1,0:T(8,128)(2,1)S(1)}, bf16[1,64,1024]{2,1,0:T(8,128)(2,1)S(1)}, bf16[1,64,1024]{2,1,0...) custom-call(s32[1]{0:T(128)S(6)} %broadcast_in_dim.21.short_ref, ...), custom_call_target="tpu_custom_call" | custom-call | flops 17179869184 | bytes 33554432 | tf_op jit(solution)/shard_map/attend/pallas_call | solution.py:139
  95.3 4.5 %collective-permute-done.13.refs_6_ = bf16[1,64,1024]{2,1,0:T(8,128)(2,1)S(1)} collective-permute-done((bf16[1,64,1024]{2,1,0:T(8,128)(2,1)S(1)}, bf16[1,64,1024]{2,1,0:T(8,128)(2,1)S(1)}, u32[]{:S(2)}, u32[]{:S(2)}) %collective-permute-start.13) | collective-permute-done | bytes 131104 | tf_op jit(solution)/shard_map/ppermute | solution.py:791
  104.5 53.5 %mlp.1 = (bf16[1024,768]{1,0:T(8,128)(2,1)}, f32[1024,768]{1,0:T(8,128)}, bf16[1,64,1024]{2,1,0:T(8,128)(2,1)}, bf16[1,64,1024]{2,1,0:T(8,128)(2,1)}, bf16[1,64,...) custom-call(s32[1]{0:T(128)} %bitcast.place_ref, ...), custom_call_target="tpu_custom_call" | custom-call | flops 28991029248 | bytes 18874368 | tf_op jit(solution)/shard_map/mlp/pallas_call | solution.py:515
  160.6 4.6 %collective-permute-done.19.refs_5_ = bf16[1,64,1024]{2,1,0:T(8,128)(2,1)S(1)} collective-permute-done((bf16[1,64,1024]{2,1,0:T(8,128)(2,1)}, bf16[1,64,1024]{2,1,0:T(8,128)(2,1)S(1)}, u32[]{:S(2)}, u32[]{:S(2)}) %collective-permute-start.19) | collective-permute-done | bytes 131104 | tf_op jit(solution)/shard_map/ppermute | solution.py:791
  169.0 8.4 %deal.1 = (bf16[8,432,384]{2,1,0:T(8,128)(2,1)}, bf16[8,432,384]{2,1,0:T(8,128)(2,1)}) custom-call(s32[1]{0:T(128)S(6)} %select_n.21.bits_ref, bf16[10,2,384,384]{3,2,1,0:T(8,128)(2,1)} %bitcast.33, bf16[10,8,96,384]{3,2,1,0:T(8,128)(2,1)} %bitcast.34, bf16[10,8,96,384]{3,2,1,0:T(8,128)(2,1)} %bitcast.35, bf16[10,8,96,384]{3,2,1,0:T(8,128)(2,1)} %bitcast.36, ...), custom_call_target="tpu_custom_call" | custom-call | flops 2949120 | bytes 17694720 | tf_op jit(solution)/shard_map/deal/pallas_call | solution.py:844
  177.9 30.0 %attend_back.3 = (bf16[3,64,1024]{2,1,0:T(8,128)(2,1)}, bf16[3,64,1024]{2,1,0:T(8,128)(2,1)}, bf16[3,64,1024]{2,1,0:T(8,128)(2,1)}, bf16[3,64,1024]{2,1,0:T(8,128)(2,1)}) custom-call(s32[1]{0:T(128)S(6)} %broadcast_in_dim.21.short_ref, bf16[3,64,1024]{2,1,0:T(8,128)(2,1)} %get-tuple-element.217.refs_0_, bf16[3,64,1024]{2,1,0:T(8,128)(2,1)} %copy-done.28, ...), custom_call_target="tpu_custom_call" | custom-call | flops 42949672960 | bytes 33554432 | tf_op jit(solution)/shard_map/attend_back/pallas_call | solution.py:252
  209.8 22.0 %attend_back.4 = (bf16[3,64,1024]{2,1,0:T(8,128)(2,1)}, bf16[3,64,1024]{2,1,0:T(8,128)(2,1)}, bf16[3,64,1024]{2,1,0:T(8,128)(2,1)}, bf16[3,64,1024]{2,1,0:T(8,128)(2,1)}) custom-call(s32[1]{0:T(128)S(6)} %broadcast_in_dim.21.short_ref, bf16[3,64,1024]{2,1,0:T(8,128)(2,1)} %get-tuple-element.231.refs_0_, bf16[3,64,1024]{2,1,0:T(8,128)(2,1)} %copy-done.25, ...), custom_call_target="tpu_custom_call" | custom-call | flops 42949672960 | bytes 33554432 | tf_op jit(solution)/shard_map/attend_back/pallas_call | solution.py:252
  238.7 5.8 %qkv_grad.2 = (bf16[4,96,384]{2,1,0:T(8,128)(2,1)S(1)}, bf16[4,96,384]{2,1,0:T(8,128)(2,1)}) custom-call(s32[1]{0:T(128)} %bitcast.7.block_ref, bf16[3,64,1024]{2,1,0:T(8,128)(2,1)S(1)} %copy-done.4, bf16[3,64,1024]{2,1,0:T(8,128)(2,1)S(1)} %copy-done.15, bf16[3,64,1024]{2,1,0:T(8,128)(2,1)S(1)} %copy-done.13, bf16[3,64,1024]{2,1,0:T(8,128)(2,1)S(1)} %copy-done.9, ...), custom_call_target="tpu_custom_call" | custom-call | flops 2415919104 | bytes 9437184 | tf_op jit(solution)/shard_map/qkv_grad/pallas_call | solution.py:771
  246.9 4.0 add_convert_fusion
  250.9 48.3 %all-to-all-start = ((bf16[8,432,384]{2,1,0:T(8,128)(2,1)}), bf16[8,432,384]{2,1,0:T(8,128)(2,1)}, u32[]{:S(2)}, u32[]{:S(2)}) async-start(bf16[8,432,384]{2,1,0:T(8,128)(2,1)} %add_convert_fusion), calls=%async_computation | async-start | bytes 5308416 | tf_op jit(solution)/shard_map/all_to_all | solution.py:947
  301.3 21.7 %attend_back.5 = (bf16[3,64,1024]{2,1,0:T(8,128)(2,1)}, bf16[3,64,1024]{2,1,0:T(8,128)(2,1)}, bf16[3,64,1024]{2,1,0:T(8,128)(2,1)}, bf16[3,64,1024]{2,1,0:T(8,128)(2,1)}) custom-call(s32[1]{0:T(128)S(6)} %broadcast_in_dim.21.short_ref, bf16[3,64,1024]{2,1,0:T(8,128)(2,1)} %get-tuple-element.252.refs_0_, bf16[3,64,1024]{2,1,0:T(8,128)(2,1)} %copy-done.24, ...), custom_call_target="tpu_custom_call" | custom-call | flops 42949672960 | bytes 33554432 | tf_op jit(solution)/shard_map/attend_back/pallas_call | solution.py:252
  330.3 3.5 qkv_grad.3
  333.9 13.1 %collective-permute-start.36 = (bf16[4,96,192]{2,1,0:T(8,128)(2,1)S(1)}, bf16[4,96,192]{2,1,0:T(8,128)(2,1)S(1)}, u32[]{:S(2)}, u32[]{:S(2)}) collective-permute-start(bf16[4,96,192]{2,1,0:T(8,128)(2,1)S(1)} %get-tuple-element.270), channel_id=1, source_target_pairs={{0,4},{4,0},{8,12},{12,8},{16,20},{20,16},{24,28},{28,24},{1,5},{5... | collective-permute-start | bytes 442376 | tf_op jit(solution)/shard_map/ppermute | solution.py:791
  347.0 11.9 %begin_finish.1 = (f32[1024,768]{1,0:T(8,128)S(1)}, f32[3,768]{1,0:T(4,128)S(1)}) custom-call(s32[6]{0:T(128)S(1)} %copy-done.18, bf16[3,64,1024]{2,1,0:T(8,128)(2,1)S(1)} %copy-done.4, bf16[3,64,1024]{2,1,0:T(8,128)(2,1)} %collective-permute-done.26.refs_1_, bf16[3,64,1024]{2,1,0:T(8,128)(2,1)} %collective-permute-done.27.refs_2_, ...), custom_call_target="tpu_custom_call" | custom-call | flops 3623878656 | bytes 7077888 | tf_op jit(solution)/shard_map/begin_finish/pallas_call | solution.py:686
  369.8 13.4 %finish.1 = (bf16[1024,768]{1,0:T(8,128)(2,1)}, f32[16,768]{1,0:T(8,128)S(1)}) custom-call(s32[4]{0:T(128)S(1)} %pad_add_fusion.1.scalars, bf16[3,64,1024]{2,1,0:T(8,128)(2,1)S(1)} %copy-done.8, bf16[3,64,1024]{2,1,0:T(8,128)(2,1)} %collective-permute-done.29.refs_1_, bf16[3,64,1024]{2,1,0:T(8,128)(2,1)} %collective-permute-done.30.refs_2_, ...), custom_call_target="tpu_custom_call" | custom-call | flops 3623878656 | bytes 14155776 | tf_op jit(solution)/shard_map/finish/pallas_call | solution.py:711
  391.5 4.1 collective-permute-done.44.refs_1_
  413.0 6.7 %all-to-all-start.1 = ((bf16[8,288,96]{2,1,0:T(8,128)(2,1)}), bf16[8,288,96]{2,1,0:T(8,128)(2,1)S(1)}, u32[]{:S(2)}, u32[]{:S(2)}) async-start(bf16[8,288,96]{2,1,0:T(8,128)(2,1)} %bitcast.39), calls=%async_computation.1 | async-start | bytes 1179648 | tf_op jit(solution)/shard_map/all_to_all | solution.py:947
  424.5 3.3 undeal.1
  427.8 8.7 %all-to-all-done.1.parts = bf16[8,288,96]{2,1,0:T(8,128)(2,1)S(1)} async-done(((bf16[8,288,96]{2,1,0:T(8,128)(2,1)}), bf16[8,288,96]{2,1,0:T(8,128)(2,1)S(1)}, u32[]{:S(2)}, u32[]{:S(2)}) %all-to-all-start.1) | async-done | bytes 442400 | tf_op jit(solution)/shard_map/all_to_all | solution.py:947
  (278 shorter events, 95.4 us)
Async XLA Ops:
  19.1 35.6 %collective-permute-start = (bf16[3,64,1024]{2,1,0:T(8,128)(2,1)}, bf16[3,64,1024]{2,1,0:T(8,128)(2,1)S(1)}, u32[]{:S(2)}, u32[]{:S(2)}) collective-permute-start(bf16[3,64,1024]{2,1,0:T(8,128)(2,1)} %get-tuple-element.158), channel_id=1, source_target_pairs={{0,1},{1,0},{2,3},{3,2},{4,5},{5,4},{6,7},{7,6},{8,9},{9,8},{10,11... | collective-permute-start | bytes 1179656 | tf_op jit(solution)/shard_map/ppermute | solution.py:791
  19.2 35.5 %collective-permute-start.1 = (bf16[3,64,1024]{2,1,0:T(8,128)(2,1)}, bf16[3,64,1024]{2,1,0:T(8,128)(2,1)S(1)}, u32[]{:S(2)}, u32[]{:S(2)}) collective-permute-start(bf16[3,64,1024]{2,1,0:T(8,128)(2,1)} %get-tuple-element.159), channel_id=1, source_target_pairs={{0,2},{1,3},{2,0},{3,1},{4,6},{5,7},{6,4},{7,5},{8,10},{9,11},{10,... | collective-permute-start | bytes 1179656 | tf_op jit(solution)/shard_map/ppermute | solution.py:791
  21.2 33.5 %collective-permute-start.2 = (bf16[3,64,1024]{2,1,0:T(8,128)(2,1)}, bf16[3,64,1024]{2,1,0:T(8,128)(2,1)S(1)}, u32[]{:S(2)}, u32[]{:S(2)}) collective-permute-start(bf16[3,64,1024]{2,1,0:T(8,128)(2,1)} %get-tuple-element.160), channel_id=1, source_target_pairs={{0,3},{1,2},{2,1},{3,0},{4,7},{5,6},{6,5},{7,4},{8,11},{9,10},{10,... | collective-permute-start | bytes 1179656 | tf_op jit(solution)/shard_map/ppermute | solution.py:791
  54.7 20.4 %collective-permute-start.10 = (bf16[3,64,1024]{2,1,0:T(8,128)(2,1)S(1)}, bf16[3,64,1024]{2,1,0:T(8,128)(2,1)S(1)}, u32[]{:S(2)}, u32[]{:S(2)}) collective-permute-start(bf16[3,64,1024]{2,1,0:T(8,128)(2,1)S(1)} %copy-done.64), channel_id=1, source_target_pairs={{0,2},{1,3},{2,0},{3,1},{4,6},{5,7},{6,4},{7,5},{8,10},{9,11},{10,... | collective-permute-start | bytes 1179656 | tf_op jit(solution)/shard_map/ppermute | solution.py:791
  73.2 20.1 %collective-permute-start.6 = (bf16[2,64,1024]{2,1,0:T(8,128)(2,1)S(1)}, bf16[2,64,1024]{2,1,0:T(8,128)(2,1)S(1)}, u32[]{:S(2)}, u32[]{:S(2)}) collective-permute-start(bf16[2,64,1024]{2,1,0:T(8,128)(2,1)S(1)} %get-tuple-element.175), channel_id=1, source_target_pairs={{0,1},{1,0},{2,3},{3,2},{4,5},{5,4},{6,7},{7,6},{8,9},{9,8},{10,11... | collective-permute-start | bytes 786440 | tf_op jit(solution)/shard_map/ppermute | solution.py:791
  75.1 28.2 %collective-permute-start.15 = (bf16[1024,768]{1,0:T(8,128)(2,1)S(1)}, bf16[1024,768]{1,0:T(8,128)(2,1)S(1)}, u32[]{:S(2)}, u32[]{:S(2)}) collective-permute-start(bf16[1024,768]{1,0:T(8,128)(2,1)S(1)} %copy-done), channel_id=1, source_target_pairs={{0,1},{1,0},{2,3},{3,2},{4,5},{5,4},{6,7},{7,6},{8,9},{9,8},{10,11... | collective-permute-start | bytes 4718600 | tf_op jit(solution)/shard_map/ppermute | solution.py:791
  101.7 56.3 %collective-permute-start.16 = (bf16[1024,768]{1,0:T(8,128)(2,1)S(1)}, bf16[1024,768]{1,0:T(8,128)(2,1)}, u32[]{:S(2)}, u32[]{:S(2)}) collective-permute-start(bf16[1024,768]{1,0:T(8,128)(2,1)S(1)} %copy-done), channel_id=1, source_target_pairs={{0,2},{1,3},{2,0},{3,1},{4,6},{5,7},{6,4},{7,5},{8,10},{9,11},{10,... | collective-permute-start | bytes 4718600 | tf_op jit(solution)/shard_map/ppermute | solution.py:791
  167.1 41.0 %collective-permute-start.22 = (bf16[2,64,1024]{2,1,0:T(8,128)(2,1)}, bf16[2,64,1024]{2,1,0:T(8,128)(2,1)S(1)}, u32[]{:S(2)}, u32[]{:S(2)}) collective-permute-start(bf16[2,64,1024]{2,1,0:T(8,128)(2,1)} %get-tuple-element.240), channel_id=1, source_target_pairs={{0,1},{1,0},{2,3},{3,2},{4,5},{5,4},{6,7},{7,6},{8,9},{9,8},{10,11... | collective-permute-start | bytes 786440 | tf_op jit(solution)/shard_map/ppermute | solution.py:791
  167.4 42.4 %collective-permute-start.23 = (bf16[2,64,1024]{2,1,0:T(8,128)(2,1)}, bf16[2,64,1024]{2,1,0:T(8,128)(2,1)}, u32[]{:S(2)}, u32[]{:S(2)}) collective-permute-start(bf16[2,64,1024]{2,1,0:T(8,128)(2,1)} %get-tuple-element.241), channel_id=1, source_target_pairs={{0,2},{1,3},{2,0},{3,1},{4,6},{5,7},{6,4},{7,5},{8,10},{9,11},{10,... | collective-permute-start | bytes 786440 | tf_op jit(solution)/shard_map/ppermute | solution.py:791
  167.8 42.0 %collective-permute-start.24 = (bf16[2,64,1024]{2,1,0:T(8,128)(2,1)}, bf16[2,64,1024]{2,1,0:T(8,128)(2,1)}, u32[]{:S(2)}, u32[]{:S(2)}) collective-permute-start(bf16[2,64,1024]{2,1,0:T(8,128)(2,1)} %get-tuple-element.242), channel_id=1, source_target_pairs={{0,3},{1,2},{2,1},{3,0},{4,7},{5,6},{6,5},{7,4},{8,11},{9,10},{10,... | collective-permute-start | bytes 786440 | tf_op jit(solution)/shard_map/ppermute | solution.py:791
  177.4 67.9 %collective-permute-start.25 = (bf16[8,432,384]{2,1,0:T(8,128)(2,1)}, bf16[8,432,384]{2,1,0:T(8,128)(2,1)}, u32[]{:S(2)}, u32[]{:S(2)}) collective-permute-start(bf16[8,432,384]{2,1,0:T(8,128)(2,1)} %get-tuple-element.216), channel_id=1, source_target_pairs={{0,2},{1,3},{2,0},{3,1},{4,6},{5,7},{6,4},{7,5},{8,10},{9,11},{10,... | collective-permute-start | bytes 7962632 | tf_op jit(solution)/shard_map/ppermute | solution.py:791
  207.9 91.3 %collective-permute-start.26 = (bf16[3,64,1024]{2,1,0:T(8,128)(2,1)}, bf16[3,64,1024]{2,1,0:T(8,128)(2,1)}, u32[]{:S(2)}, u32[]{:S(2)}) collective-permute-start(bf16[3,64,1024]{2,1,0:T(8,128)(2,1)} %get-tuple-element.228.refs_1_), channel_id=1, source_target_pairs={{0,1},{1,0},{2,3},{3,2},{4,5},{5,4},{6,7},{7,6},{8,9},{9,8},{10,11... | collective-permute-start | bytes 1179656 | tf_op jit(solution)/shard_map/ppermute | solution.py:791
  208.1 91.2 %collective-permute-start.27 = (bf16[3,64,1024]{2,1,0:T(8,128)(2,1)}, bf16[3,64,1024]{2,1,0:T(8,128)(2,1)}, u32[]{:S(2)}, u32[]{:S(2)}) collective-permute-start(bf16[3,64,1024]{2,1,0:T(8,128)(2,1)} %get-tuple-element.229.refs_2_), channel_id=1, source_target_pairs={{0,2},{1,3},{2,0},{3,1},{4,6},{5,7},{6,4},{7,5},{8,10},{9,11},{10,... | collective-permute-start | bytes 1179656 | tf_op jit(solution)/shard_map/ppermute | solution.py:791
  209.8 91.5 %collective-permute-start.28 = (bf16[3,64,1024]{2,1,0:T(8,128)(2,1)}, bf16[3,64,1024]{2,1,0:T(8,128)(2,1)}, u32[]{:S(2)}, u32[]{:S(2)}) collective-permute-start(bf16[3,64,1024]{2,1,0:T(8,128)(2,1)} %get-tuple-element.230.refs_3_), channel_id=1, source_target_pairs={{0,3},{1,2},{2,1},{3,0},{4,7},{5,6},{6,5},{7,4},{8,11},{9,10},{10,... | collective-permute-start | bytes 1179656 | tf_op jit(solution)/shard_map/ppermute | solution.py:791
  231.8 91.5 %collective-permute-start.33 = (bf16[3,64,1024]{2,1,0:T(8,128)(2,1)}, bf16[3,64,1024]{2,1,0:T(8,128)(2,1)}, u32[]{:S(2)}, u32[]{:S(2)}) collective-permute-start(bf16[3,64,1024]{2,1,0:T(8,128)(2,1)} %get-tuple-element.246.refs_5_), channel_id=1, source_target_pairs={{0,1},{1,0},{2,3},{3,2},{4,5},{5,4},{6,7},{7,6},{8,9},{9,8},{10,11... | collective-permute-start | bytes 1179656 | tf_op jit(solution)/shard_map/ppermute | solution.py:791
  245.2 79.6 %collective-permute-start.34 = (bf16[3,64,1024]{2,1,0:T(8,128)(2,1)}, bf16[3,64,1024]{2,1,0:T(8,128)(2,1)}, u32[]{:S(2)}, u32[]{:S(2)}) collective-permute-start(bf16[3,64,1024]{2,1,0:T(8,128)(2,1)} %get-tuple-element.247.refs_6_), channel_id=1, source_target_pairs={{0,2},{1,3},{2,0},{3,1},{4,6},{5,7},{6,4},{7,5},{8,10},{9,11},{10,... | collective-permute-start | bytes 1179656 | tf_op jit(solution)/shard_map/ppermute | solution.py:791
  250.9 110.9 %all-to-all-start = ((bf16[8,432,384]{2,1,0:T(8,128)(2,1)}), bf16[8,432,384]{2,1,0:T(8,128)(2,1)}, u32[]{:S(2)}, u32[]{:S(2)}) async-start(bf16[8,432,384]{2,1,0:T(8,128)(2,1)} %add_convert_fusion), calls=%async_computation | async-start | bytes 5308416 | tf_op jit(solution)/shard_map/all_to_all | solution.py:947
  299.2 25.7 %collective-permute-start.35 = (bf16[3,64,1024]{2,1,0:T(8,128)(2,1)}, bf16[3,64,1024]{2,1,0:T(8,128)(2,1)}, u32[]{:S(2)}, u32[]{:S(2)}) collective-permute-start(bf16[3,64,1024]{2,1,0:T(8,128)(2,1)} %get-tuple-element.248.refs_7_), channel_id=1, source_target_pairs={{0,3},{1,2},{2,1},{3,0},{4,7},{5,6},{6,5},{7,4},{8,11},{9,10},{10,... | collective-permute-start | bytes 1179656 | tf_op jit(solution)/shard_map/ppermute | solution.py:791
  299.3 47.7 %collective-permute-start.32 = (bf16[4,96,384]{2,1,0:T(8,128)(2,1)}, bf16[4,96,384]{2,1,0:T(8,128)(2,1)}, u32[]{:S(2)}, u32[]{:S(2)}) collective-permute-start(bf16[4,96,384]{2,1,0:T(8,128)(2,1)} %get-tuple-element.263), channel_id=1, source_target_pairs={{0,4},{4,0},{8,12},{12,8},{16,20},{20,16},{24,28},{28,24},{1,5},{5... | collective-permute-start | bytes 884744 | tf_op jit(solution)/shard_map/ppermute | solution.py:791
  323.0 40.8 %collective-permute-start.29 = (bf16[3,64,1024]{2,1,0:T(8,128)(2,1)}, bf16[3,64,1024]{2,1,0:T(8,128)(2,1)}, u32[]{:S(2)}, u32[]{:S(2)}) collective-permute-start(bf16[3,64,1024]{2,1,0:T(8,128)(2,1)} %get-tuple-element.265.refs_1_), channel_id=1, source_target_pairs={{0,1},{1,0},{2,3},{3,2},{4,5},{5,4},{6,7},{7,6},{8,9},{9,8},{10,11... | collective-permute-start | bytes 1179656 | tf_op jit(solution)/shard_map/ppermute | solution.py:791
  323.3 40.5 %collective-permute-start.30 = (bf16[3,64,1024]{2,1,0:T(8,128)(2,1)}, bf16[3,64,1024]{2,1,0:T(8,128)(2,1)}, u32[]{:S(2)}, u32[]{:S(2)}) collective-permute-start(bf16[3,64,1024]{2,1,0:T(8,128)(2,1)} %get-tuple-element.266.refs_2_), channel_id=1, source_target_pairs={{0,2},{1,3},{2,0},{3,1},{4,6},{5,7},{6,4},{7,5},{8,10},{9,11},{10,... | collective-permute-start | bytes 1179656 | tf_op jit(solution)/shard_map/ppermute | solution.py:791
  324.8 39.0 %collective-permute-start.31 = (bf16[3,64,1024]{2,1,0:T(8,128)(2,1)}, bf16[3,64,1024]{2,1,0:T(8,128)(2,1)}, u32[]{:S(2)}, u32[]{:S(2)}) collective-permute-start(bf16[3,64,1024]{2,1,0:T(8,128)(2,1)} %get-tuple-element.267.refs_3_), channel_id=1, source_target_pairs={{0,3},{1,2},{2,1},{3,0},{4,7},{5,6},{6,5},{7,4},{8,11},{9,10},{10,... | collective-permute-start | bytes 1179656 | tf_op jit(solution)/shard_map/ppermute | solution.py:791
  333.9 27.9 %collective-permute-start.36 = (bf16[4,96,192]{2,1,0:T(8,128)(2,1)S(1)}, bf16[4,96,192]{2,1,0:T(8,128)(2,1)S(1)}, u32[]{:S(2)}, u32[]{:S(2)}) collective-permute-start(bf16[4,96,192]{2,1,0:T(8,128)(2,1)S(1)} %get-tuple-element.270), channel_id=1, source_target_pairs={{0,4},{4,0},{8,12},{12,8},{16,20},{20,16},{24,28},{28,24},{1,5},{5... | collective-permute-start | bytes 442376 | tf_op jit(solution)/shard_map/ppermute | solution.py:791
  413.0 23.4 %all-to-all-start.1 = ((bf16[8,288,96]{2,1,0:T(8,128)(2,1)}), bf16[8,288,96]{2,1,0:T(8,128)(2,1)S(1)}, u32[]{:S(2)}, u32[]{:S(2)}) async-start(bf16[8,288,96]{2,1,0:T(8,128)(2,1)} %bitcast.39), calls=%async_computation.1 | async-start | bytes 1179648 | tf_op jit(solution)/shard_map/all_to_all | solution.py:947
  (106 other events, 995.9 us)
